TPU v7x, 32 devices: a whole 2x2x4 slice. The times are simulated.
32 devices in a mesh: dp: 8 (over z, y), expert: 4 (over x, core).
Axes of the slice: x: 2, y: 2, z: 4, core: 2. Of those that a mesh axis runs over, the one named last changes fastest.
Arguments:
- tokens_in: bfloat16 [25216, 512], P(('dp', 'expert')), may hold values from -6 to 6
- grad_out: bfloat16 [25216, 512], P(('dp', 'expert')), may hold values from -6 to 6
- routes: int32 [25216, 2], P(('dp', 'expert')), may hold values from 0 to 15, all different within a row; in each aligned block of 197 rows (0 to 196, 197 to 393, ...) at most 41 rows name the same one
- norm_gains: bfloat16 [512, 2], P(('dp', 'expert')), may hold values from 0.5 to 1.5
- biases: bfloat16 [512, 5], P(('dp', 'expert')), may hold values from -1 to 1
- w_qkv: bfloat16 [512, 1536], P(('dp', 'expert')), may hold values from -0.25 to 0.25
- w_proj: bfloat16 [512, 512], P(('dp', 'expert')), may hold values from -2 to 2
- w_router: bfloat16 [512, 16], P(('dp', 'expert')), may hold values from -0.25 to 0.25
- w_up: bfloat16 [16, 512, 2048], P('expert'), may hold values from -0.25 to 0.25
- b_up: bfloat16 [16, 2048], P('expert'), may hold values from -1 to 1
- w_down: bfloat16 [16, 2048, 512], P('expert'), may hold values from -1.5 to 1.5
- b_down: bfloat16 [16, 512], P('expert'), may hold values from -9.5625 to 9.5625
Outputs:
- block_out: bfloat16 [25216, 512], P(('dp', 'expert'))
- grad_tokens: float32 [25216, 512], P(('dp', 'expert'))
- grad_gains: float32 [512, 2], P(('dp', 'expert'))
- grad_biases: float32 [512, 5], P(('dp', 'expert'))
- grad_qkv: float32 [512, 1536], P(('dp', 'expert'))
- grad_proj: float32 [512, 512], P(('dp', 'expert'))
- grad_router: float32 [512, 16], P(('dp', 'expert'))
- grad_up: float32 [16, 512, 2048], P('expert', None, 'dp')
- grad_b_up: float32 [16, 2048], P('expert', 'dp')
- grad_down: float32 [16, 2048, 512], P('expert', 'dp')
- grad_b_down: float32 [16, 512], P('expert', 'dp')
Inputs may be any that keep to these rules, and one draw needn't show every extreme that they name: `routes`: each row names two different experts. In each aligned block of 197 rows (one micro-batch of one device) no expert is named by more than 41 rows, and in every draw some expert is named by exactly 41 rows of some block.
All inputs are finite; a program needn't handle non-finite values.
Results may differ from a plain program's by a relative error of at most 0.017.
Values may be sent and summed in bfloat16 or wider, within the bound.
No kernel may reach another device: no remote copies, remote signals or barrier semaphores. Data moves between devices by JAX's collectives and lax.ppermute only.
A program may use at most 256 MiB of HBM per device.

v0:
```python
import jax
import jax.numpy as jnp
from jax import lax
from jax.sharding import PartitionSpec as P

HEAD = 64
SEQ = 197
MICRO = 4


EPSILON = 1e-06


def norm_rows(row_block):
    row_mean = jnp.mean(row_block, axis=-1, keepdims=True)
    centred = row_block - row_mean
    inv_std = lax.rsqrt(jnp.mean(centred * centred, axis=-1, keepdims=True) + EPSILON)
    return (centred * inv_std, inv_std)


def norm_back(grad_h, normed, inv_std, gain_vec):
    scaled = grad_h * gain_vec
    inner = (
        scaled
        - jnp.mean(scaled, axis=-1, keepdims=True)
        - normed * jnp.mean(scaled * normed, axis=-1, keepdims=True)
    )
    return (inv_std * inner, jnp.sum(grad_h * normed, axis=0), jnp.sum(grad_h, axis=0))


def dot_rows(left_mat, right_mat):
    return lax.dot_general(
        left_mat, right_mat, (((0,), (0,)), ((), ())), preferred_element_type=jnp.float32
    )


def dot_trans(left_mat, right_mat):
    return lax.dot_general(
        left_mat, right_mat, (((1,), (1,)), ((), ())), preferred_element_type=jnp.float32
    )


def gelu_parts(pre_act):
    normal_cdf = 0.5 * (1.0 + lax.erf(pre_act * 0.7071067811865476))
    normal_pdf = jnp.exp(-0.5 * pre_act * pre_act) * 0.3989422804014327
    return (normal_cdf, normal_pdf)


def on_device(
    tokens_in,
    grad_out,
    routes,
    norm_gains,
    biases,
    w_qkv,
    w_proj,
    w_router,
    w_up,
    b_up,
    w_down,
    b_down,
):
    model_width = tokens_in.shape[1]
    head_count = model_width // HEAD
    tok_block = tokens_in.shape[0] // MICRO
    image_count = tok_block // SEQ
    local_experts = w_up.shape[0]
    groups = lax.axis_size("expert")
    experts = local_experts * groups
    capacity = max(2, (2 * tok_block * 13 + 8 * experts - 1) // (8 * experts))
    slots_all = experts * capacity
    recv_rows = groups * capacity
    score_scale = HEAD ** (-0.5)
    b_up_f = b_up.astype(jnp.float32)
    b_down_f = b_down.astype(jnp.float32)
    expert_ids_all = jnp.arange(experts, dtype=jnp.int32)
    saved_list = []
    out_list = []
    for micro_idx in range(MICRO):
        dense_full = (
            lax.all_gather(w_qkv, ("dp", "expert"), axis=0, tiled=True),
            lax.all_gather(w_proj, ("dp", "expert"), axis=0, tiled=True),
            lax.all_gather(w_router, ("dp", "expert"), axis=0, tiled=True),
            lax.all_gather(norm_gains, ("dp", "expert"), axis=0, tiled=True),
            lax.all_gather(biases, ("dp", "expert"), axis=0, tiled=True),
        )
        full_qkv, full_proj, full_router, full_gains, full_biases = dense_full
        gains_f = full_gains.astype(jnp.float32)
        biases_f = full_biases.astype(jnp.float32)
        rows_in = lax.slice_in_dim(
            tokens_in, micro_idx * tok_block, (micro_idx + 1) * tok_block, axis=0
        ).astype(jnp.float32)
        normed_one, inv_one = norm_rows(rows_in)
        act_one = (normed_one * gains_f[:, 0] + biases_f[:, 3]).astype(jnp.bfloat16)
        qkv_bias = jnp.concatenate(
            [biases_f[:, 0], jnp.zeros((model_width,), jnp.float32), biases_f[:, 1]]
        )
        qkv_rows = (
            jnp.dot(act_one, full_qkv, preferred_element_type=jnp.float32) + qkv_bias
        ).astype(jnp.bfloat16)
        head_parts = qkv_rows.reshape(image_count, SEQ, 3, head_count, HEAD)
        queries = head_parts[:, :, 0]
        key_rows = head_parts[:, :, 1]
        values = head_parts[:, :, 2]
        scores = (
            jnp.einsum("ishd,ithd->ihst", queries, key_rows, preferred_element_type=jnp.float32)
            * score_scale
        )
        top_score = jnp.max(scores, axis=-1, keepdims=True)
        log_total = top_score + jnp.log(
            jnp.sum(jnp.exp(scores - top_score), axis=-1, keepdims=True)
        )
        weights = jnp.exp(scores - log_total).astype(jnp.bfloat16)
        mixed_rows = jnp.einsum(
            "ihst,ithd->ishd", weights, values, preferred_element_type=jnp.float32
        )
        mixed_rows = mixed_rows.astype(jnp.bfloat16).reshape(tok_block, model_width)
        attn_out = (
            jnp.dot(mixed_rows, full_proj, preferred_element_type=jnp.float32) + biases_f[:, 2]
        )
        resid_one = rows_in + attn_out
        normed_two, inv_two = norm_rows(resid_one)
        act_two = (normed_two * gains_f[:, 1] + biases_f[:, 4]).astype(jnp.bfloat16)
        logits = jnp.dot(act_two, full_router, preferred_element_type=jnp.float32)
        router_probs = jax.nn.softmax(logits, axis=-1)
        route_rows = lax.slice_in_dim(
            routes, micro_idx * tok_block, (micro_idx + 1) * tok_block, axis=0
        )
        expert_ids = jnp.concatenate([route_rows[:, 0], route_rows[:, 1]])
        chosen = (expert_ids[:, None] == expert_ids_all[None, :]).astype(jnp.int32)
        position = jnp.sum(chosen * (jnp.cumsum(chosen, axis=0) - 1), axis=1)
        slot_of = expert_ids * capacity + position
        slot_table = (
            jnp.full((slots_all,), 2 * tok_block, jnp.int32)
            .at[slot_of]
            .set(jnp.arange(2 * tok_block, dtype=jnp.int32))
        )
        onehot_f = chosen.astype(jnp.float32).reshape(2, tok_block, experts)
        gate_vals = jnp.sum(onehot_f * router_probs[None], axis=2)
        padded = jnp.concatenate([act_two, act_two, jnp.zeros((1, model_width), jnp.bfloat16)])
        send_rows = jnp.take(padded, slot_table, axis=0).reshape(
            groups, local_experts, capacity, model_width
        )
        received = lax.all_to_all(send_rows, "expert", split_axis=0, concat_axis=2, tiled=True)
        expert_in = received.reshape(local_experts, recv_rows, model_width)
        pre_act = (
            jnp.einsum("erd,edh->erh", expert_in, w_up, preferred_element_type=jnp.float32)
            + b_up_f[:, None, :]
        )
        normal_cdf, normal_pdf = gelu_parts(pre_act)
        hidden_act = (pre_act * normal_cdf).astype(jnp.bfloat16)
        expert_res = (
            jnp.einsum("erh,ehd->erd", hidden_act, w_down, preferred_element_type=jnp.float32)
            + b_down_f[:, None, :]
        )
        expert_res = expert_res.astype(jnp.bfloat16).reshape(
            1, local_experts, recv_rows, model_width
        )
        returned = lax.all_to_all(expert_res, "expert", split_axis=2, concat_axis=0, tiled=True)
        back_rows = returned.reshape(slots_all, model_width)
        picked = (
            jnp.take(back_rows, slot_of, axis=0)
            .astype(jnp.float32)
            .reshape(2, tok_block, model_width)
        )
        moe_out = gate_vals[0][:, None] * picked[0] + gate_vals[1][:, None] * picked[1]
        out_list.append((resid_one + moe_out).astype(jnp.bfloat16))
        stored = {
            "normed_one": normed_one,
            "inv_one": inv_one,
            "act_one": act_one,
            "qkv_rows": qkv_rows,
            "log_total": log_total,
            "mixed_rows": mixed_rows,
            "normed_two": normed_two,
            "inv_two": inv_two,
            "act_two": act_two,
            "router_probs": router_probs,
            "onehot_f": onehot_f,
            "gate_vals": gate_vals,
            "slot_of": slot_of,
            "slot_table": slot_table,
            "expert_in": expert_in,
            "picked": picked,
        }
        saved_list.append(stored)
    acc_qkv = jnp.zeros((model_width, 3 * model_width), jnp.float32)
    acc_proj = jnp.zeros((model_width, model_width), jnp.float32)
    acc_router = jnp.zeros((model_width, experts), jnp.float32)
    acc_gains = jnp.zeros((model_width, 2), jnp.float32)
    acc_biases = jnp.zeros((model_width, 5), jnp.float32)
    expert_totals = None
    grad_list = []
    for micro_idx in range(MICRO):
        stored = saved_list[micro_idx]
        dense_full = (
            lax.all_gather(w_qkv, ("dp", "expert"), axis=0, tiled=True),
            lax.all_gather(w_proj, ("dp", "expert"), axis=0, tiled=True),
            lax.all_gather(w_router, ("dp", "expert"), axis=0, tiled=True),
            lax.all_gather(norm_gains, ("dp", "expert"), axis=0, tiled=True),
            lax.all_gather(biases, ("dp", "expert"), axis=0, tiled=True),
        )
        full_qkv, full_proj, full_router, full_gains, full_biases = dense_full
        gains_f = full_gains.astype(jnp.float32)
        grad_rows = lax.slice_in_dim(
            grad_out, micro_idx * tok_block, (micro_idx + 1) * tok_block, axis=0
        ).astype(jnp.float32)
        gate_vals = stored["gate_vals"]
        grad_gate = jnp.sum(stored["picked"] * grad_rows[None], axis=2)
        grad_pick = (
            (gate_vals[:, :, None] * grad_rows[None])
            .astype(jnp.bfloat16)
            .reshape(2 * tok_block, model_width)
        )
        padded_grad = jnp.concatenate([grad_pick, jnp.zeros((1, model_width), jnp.bfloat16)])
        send_grad = jnp.take(padded_grad, stored["slot_table"], axis=0).reshape(
            groups, local_experts, capacity, model_width
        )
        grad_res = lax.all_to_all(
            send_grad, "expert", split_axis=0, concat_axis=2, tiled=True
        ).reshape(local_experts, recv_rows, model_width)
        expert_in = stored["expert_in"]
        pre_act = (
            jnp.einsum("erd,edh->erh", expert_in, w_up, preferred_element_type=jnp.float32)
            + b_up_f[:, None, :]
        )
        normal_cdf, normal_pdf = gelu_parts(pre_act)
        hidden_act = (pre_act * normal_cdf).astype(jnp.bfloat16)
        gelu_grad = normal_cdf + pre_act * normal_pdf
        part_down = jnp.einsum(
            "erh,erd->ehd", hidden_act, grad_res, preferred_element_type=jnp.float32
        )
        part_b_down = jnp.sum(grad_res.astype(jnp.float32), axis=1)
        grad_hidden = jnp.einsum(
            "erd,ehd->erh", grad_res, w_down, preferred_element_type=jnp.float32
        )
        grad_pre = (grad_hidden * gelu_grad).astype(jnp.bfloat16)
        part_up = jnp.einsum(
            "erd,erh->edh", expert_in, grad_pre, preferred_element_type=jnp.float32
        )
        part_b_up = jnp.sum(grad_pre.astype(jnp.float32), axis=1)
        grad_in = jnp.einsum(
            "erh,edh->erd", grad_pre, w_up, preferred_element_type=jnp.float32
        ).astype(jnp.bfloat16)
        grad_back = lax.all_to_all(
            grad_in.reshape(1, local_experts, recv_rows, model_width),
            "expert",
            split_axis=2,
            concat_axis=0,
            tiled=True,
        )
        grad_back = grad_back.reshape(slots_all, model_width)
        grad_choice = (
            jnp.take(grad_back, stored["slot_of"], axis=0)
            .astype(jnp.float32)
            .reshape(2, tok_block, model_width)
        )
        expert_parts_now = (part_up, part_b_up, part_down, part_b_down)
        expert_totals = (
            expert_parts_now
            if expert_totals is None
            else jax.tree.map(jnp.add, expert_totals, expert_parts_now)
        )
        router_probs = stored["router_probs"]
        grad_probs = jnp.sum(stored["onehot_f"] * grad_gate[:, :, None], axis=0)
        grad_logit = router_probs * (
            grad_probs - jnp.sum(grad_probs * router_probs, axis=-1, keepdims=True)
        )
        grad_logit = grad_logit.astype(jnp.bfloat16)
        acc_router = acc_router + dot_rows(stored["act_two"], grad_logit)
        grad_act_two = grad_choice[0] + grad_choice[1] + dot_trans(grad_logit, full_router)
        grad_resid, gain_two, shift_two = norm_back(
            grad_act_two, stored["normed_two"], stored["inv_two"], gains_f[:, 1]
        )
        grad_resid = grad_rows + grad_resid
        grad_attn = grad_resid.astype(jnp.bfloat16)
        acc_proj = acc_proj + dot_rows(stored["mixed_rows"], grad_attn)
        bias_proj = jnp.sum(grad_attn.astype(jnp.float32), axis=0)
        grad_mixed = (
            dot_trans(grad_attn, full_proj)
            .astype(jnp.bfloat16)
            .reshape(image_count, SEQ, head_count, HEAD)
        )
        head_parts = stored["qkv_rows"].reshape(image_count, SEQ, 3, head_count, HEAD)
        queries = head_parts[:, :, 0]
        key_rows = head_parts[:, :, 1]
        values = head_parts[:, :, 2]
        scores = (
            jnp.einsum("ishd,ithd->ihst", queries, key_rows, preferred_element_type=jnp.float32)
            * score_scale
        )
        weights_f = jnp.exp(scores - stored["log_total"])
        weights_b = weights_f.astype(jnp.bfloat16)
        grad_values = jnp.einsum(
            "ihst,ishd->ithd", weights_b, grad_mixed, preferred_element_type=jnp.float32
        )
        grad_weights = jnp.einsum(
            "ishd,ithd->ihst", grad_mixed, values, preferred_element_type=jnp.float32
        )
        grad_scores = weights_f * (
            grad_weights - jnp.sum(grad_weights * weights_f, axis=-1, keepdims=True)
        )
        grad_scores = grad_scores.astype(jnp.bfloat16)
        grad_queries = (
            jnp.einsum("ihst,ithd->ishd", grad_scores, key_rows, preferred_element_type=jnp.float32)
            * score_scale
        )
        grad_keys = (
            jnp.einsum("ihst,ishd->ithd", grad_scores, queries, preferred_element_type=jnp.float32)
            * score_scale
        )
        grad_qkv_rows = jnp.stack([grad_queries, grad_keys, grad_values], axis=2).reshape(
            tok_block, 3 * model_width
        )
        grad_qkv_rows = grad_qkv_rows.astype(jnp.bfloat16)
        acc_qkv = acc_qkv + dot_rows(stored["act_one"], grad_qkv_rows)
        qkv_sums = jnp.sum(grad_qkv_rows.astype(jnp.float32), axis=0)
        grad_act_one = dot_trans(grad_qkv_rows, full_qkv)
        grad_norm_one, gain_one, shift_one = norm_back(
            grad_act_one, stored["normed_one"], stored["inv_one"], gains_f[:, 0]
        )
        grad_list.append(grad_resid + grad_norm_one)
        acc_gains = acc_gains + jnp.stack([gain_one, gain_two], axis=1)
        acc_biases = acc_biases + jnp.stack(
            [qkv_sums[:model_width], qkv_sums[2 * model_width :], bias_proj, shift_one, shift_two],
            axis=1,
        )
    expert_grads = (
        lax.psum_scatter(
            expert_totals[0].astype(jnp.bfloat16), "dp", scatter_dimension=2, tiled=True
        ).astype(jnp.float32),
        lax.psum_scatter(
            expert_totals[1].astype(jnp.bfloat16), "dp", scatter_dimension=1, tiled=True
        ).astype(jnp.float32),
        lax.psum_scatter(
            expert_totals[2].astype(jnp.bfloat16), "dp", scatter_dimension=1, tiled=True
        ).astype(jnp.float32),
        lax.psum_scatter(
            expert_totals[3].astype(jnp.bfloat16), "dp", scatter_dimension=1, tiled=True
        ).astype(jnp.float32),
    )
    dense_sums = (
        lax.psum_scatter(acc_qkv, ("dp", "expert"), scatter_dimension=0, tiled=True),
        lax.psum_scatter(acc_proj, ("dp", "expert"), scatter_dimension=0, tiled=True),
        lax.psum_scatter(acc_router, ("dp", "expert"), scatter_dimension=0, tiled=True),
        lax.psum_scatter(acc_gains, ("dp", "expert"), scatter_dimension=0, tiled=True),
        lax.psum_scatter(acc_biases, ("dp", "expert"), scatter_dimension=0, tiled=True),
    )
    block_out = jnp.concatenate(out_list, axis=0)
    grad_tokens = jnp.concatenate(grad_list, axis=0)
    return (
        block_out,
        grad_tokens,
        dense_sums[3],
        dense_sums[4],
        dense_sums[0],
        dense_sums[1],
        dense_sums[2],
        expert_grads[0],
        expert_grads[1],
        expert_grads[2],
        expert_grads[3],
    )


def solution(mesh):
    in_specs = (
        P(("dp", "expert"), None),
        P(("dp", "expert"), None),
        P(("dp", "expert"), None),
        P(("dp", "expert"), None),
        P(("dp", "expert"), None),
        P(("dp", "expert"), None),
        P(("dp", "expert"), None),
        P(("dp", "expert"), None),
        P("expert", None, None),
        P("expert", None),
        P("expert", None, None),
        P("expert", None),
    )
    out_specs = (
        P(("dp", "expert"), None),
        P(("dp", "expert"), None),
        P(("dp", "expert"), None),
        P(("dp", "expert"), None),
        P(("dp", "expert"), None),
        P(("dp", "expert"), None),
        P(("dp", "expert"), None),
        P("expert", None, "dp"),
        P("expert", "dp"),
        P("expert", "dp", None),
        P("expert", "dp"),
    )
    return jax.shard_map(
        on_device, mesh=mesh, in_specs=in_specs, out_specs=out_specs, check_vma=False
    )
```

profile of v0, /device:TPU:0, one launch (start us, length us, event | category | flops | bytes accessed | tf_op | source)
XLA Modules:
  0.0 1637.7 jit_solution(1213482217216369953)
XLA Ops:
  9.2 43.2 %all-gather = bf16[32,16,2]{1,2,0:T(2,128)(2,1)S(1)} all-gather(bf16[1,16,2]{1,2,0:T(2,128)(2,1)} %bitcast.642), channel_id=1, replica_groups=mesh['dp'=8,'expert'=4] {'dp','expert'}, dimensions={0}, use_global_device_ids=true | all-gather | bytes 2112 | tf_op jit(solution)/shard_map/all_gather | solution.py:84
  72.7 37.0 %all-gather.1 = bf16[32,16,5]{1,2,0:T(8,128)(2,1)S(1)} all-gather(bf16[1,16,5]{1,2,0:T(8,128)(2,1)} %bitcast.619), channel_id=1, replica_groups=mesh['dp'=8,'expert'=4] {'dp','expert'}, dimensions={0}, use_global_device_ids=true | all-gather | bytes 5280 | tf_op jit(solution)/shard_map/all_gather | solution.py:85
  118.8 39.7 %all_gather.13 = bf16[512,512]{1,0:T(8,128)(2,1)S(1)} all-gather(bf16[16,512]{1,0:T(8,128)(2,1)S(1)} %copy-done.181), channel_id=1, replica_groups=mesh['dp'=8,'expert'=4] {'dp','expert'}, dimensions={0}, use_global_device_ids=true | all-gather | bytes 540672 | tf_op jit(solution)/shard_map/all_gather | solution.py:82
  196.5 38.6 %all_gather.14 = bf16[512,16]{1,0:T(8,128)(2,1)S(1)} all-gather(bf16[16,16]{1,0:T(8,128)(2,1)S(1)} %copy-done.258), channel_id=1, replica_groups=mesh['dp'=8,'expert'=4] {'dp','expert'}, dimensions={0}, use_global_device_ids=true | all-gather | bytes 16896 | tf_op jit(solution)/shard_map/all_gather | solution.py:83
  236.3 6.6 multiply_convert_fusion.2
  243.0 6.1 fusion.29
  254.5 10.1 all-to-all-done.3
  283.5 9.2 all-to-all-done.10
  292.6 7.7 convert_reduce_fusion.2
  300.4 7.3 fusion.33
  314.0 10.2 fusion.70
  404.9 6.5 fusion.31
  416.8 7.5 fusion.68
  431.2 8.7 multiply_convert_fusion.3
  526.5 8.3 convert_reduce_fusion
  541.1 8.1 convert_reduce_fusion.1
  549.2 6.3 fusion.35
  565.4 7.3 fusion.34
  573.9 7.3 convert_reduce_fusion.3
  585.5 9.4 fusion.74
  599.0 10.0 fusion.66
  679.8 21.0 %add_convert_fusion.1 = bf16[4,512,2048]{2,1,0:T(8,128)(2,1)} fusion(f32[4,512,2048]{2,1,0:T(8,128)} %fusion.66, f32[4,512,2048]{2,1,0:T(8,128)} %fusion.74, f32[4,512,2048]{2,1,0:T(8,128)} %fusion.70, bf16[4,164,2048]{2,1,0:T(8,128)(2,1)S(1)} %copy-done.10, bf16[4,164,512]{2,0,1:T(4,128)(2,1)} %bitcast.84), kind=kOutput, calls=%fused_computation.21 | convolution fusion | flops 1392508928 | bytes 62078976 | tf_op jit(solution)/shard_map/erd,erh->edh/dot_general | solution.py:238
  706.3 8.2 fusion.54
  714.5 9.3 fusion.60
  723.8 17.5 %add_convert_fusion = bf16[4,2048,512]{2,1,0:T(8,128)(2,1)} fusion(f32[4,2048,512]{2,1,0:T(8,128)} %fusion.54, f32[4,2048,512]{2,1,0:T(8,128)} %fusion.60, f32[4,2048,512]{2,1,0:T(8,128)S(1)} %fusion.57, bf16[4,164,512]{2,0,1:T(4,128)(2,1)} %bitcast.142, f32[4,164,2048]{2,1,0:T(8,128)} %copy-done.8, f32[4,2048]{1,0:T(4,128)S(1)} %convert_element_type.498), kind=kOutput, calls=%fused_computation.20 | convolution fusion | flops 1400569856 | bytes 64798720 | tf_op jit(solution)/shard_map/erh,erd->ehd/dot_general | solution.py:230
  762.9 61.6 %reduce-scatter.28.cloned.1.call-done = f32[16,2]{1,0:T(8,128)} async-done(((f32[512,2]{1,0:T(8,128)}), f32[16,2]{1,0:T(8,128)}) %reduce-scatter.28.cloned.1.call-update) | async-done | bytes 144
  825.8 130.1 %reduce-scatter.30.cloned.1.call-done = f32[16,5]{1,0:T(8,128)} async-done(((f32[512,5]{1,0:T(8,128)}), f32[16,5]{1,0:T(8,128)}) %reduce-scatter.30.cloned.1.call-update) | async-done | bytes 336
  957.3 147.9 %reduce-scatter.24.cloned.1.call-done = bf16[4,512,256]{2,1,0:T(8,128)(2,1)} async-done(((bf16[4,512,2048]{2,1,0:T(8,128)(2,1)}), bf16[4,512,256]{2,1,0:T(8,128)(2,1)}) %reduce-scatter.24.cloned.1.call-update) | async-done | bytes 1048592 | tf_op jit(solution)/shard_map/reduce_scatter | solution.py:329
  1107.9 149.3 %reduce-scatter.26.cloned.1.call-done = bf16[4,256,512]{2,1,0:T(8,128)(2,1)} async-done(((bf16[4,2048,512]{2,1,0:T(8,128)(2,1)}), bf16[4,256,512]{2,1,0:T(8,128)(2,1)}) %reduce-scatter.26.cloned.1.call-update) | async-done | bytes 1048592 | tf_op jit(solution)/shard_map/reduce_scatter | solution.py:335
  1260.1 132.5 %reduce-scatter.22.cloned.1.call-done = f32[16,16]{1,0:T(8,128)} async-done(((f32[512,16]{1,0:T(8,128)}), f32[16,16]{1,0:T(8,128)}) %reduce-scatter.22.cloned.1.call-update) | async-done | bytes 1040 | tf_op jit(solution)/shard_map/reduce_scatter | solution.py:345
  1392.6 133.6 %reduce-scatter.20.cloned.1.call-done = f32[16,512]{1,0:T(8,128)} async-done(((f32[512,512]{1,0:T(8,128)}), f32[16,512]{1,0:T(8,128)}) %reduce-scatter.20.cloned.1.call-update) | async-done | bytes 32784 | tf_op jit(solution)/shard_map/reduce_scatter | solution.py:344
  1526.2 104.2 %reduce-scatter.18.cloned.1.call-done = f32[16,1536]{1,0:T(8,128)} async-done(((f32[512,1536]{1,0:T(8,128)}), f32[16,1536]{1,0:T(8,128)}) %reduce-scatter.18.cloned.1.call-update) | async-done | bytes 98320 | tf_op jit(solution)/shard_map/reduce_scatter | solution.py:343
  (1007 shorter events, 408.3 us)
Async XLA Ops:
  7.2 111.6 %copy-start.181 = (bf16[16,512]{1,0:T(8,128)(2,1)S(1)}, bf16[16,512]{1,0:T(8,128)(2,1)}, u32[]{:S(2)}) copy-start(bf16[16,512]{1,0:T(8,128)(2,1)} %param.22) | copy-start | bytes 49156
  7.2 151.3 %copy-start.62 = (bf16[788,512]{1,0:T(8,128)(2,1)S(1)}, bf16[788,512]{1,0:T(8,128)(2,1)}, u32[]{:S(2)}) copy-start(bf16[788,512]{1,0:T(8,128)(2,1)} %param.17) | copy-start | bytes 2420740
  7.2 152.5 %all-gather.4.cloned.1.call-start = ((), (), s32[]{:S(2)}) async-start(), calls=%async_computation.25 | async-start | bytes 1622016 | tf_op jit(solution)/shard_map/all_gather | solution.py:81
  54.2 105.5 %copy-start.12 = (bf16[788,512]{1,0:T(8,128)(2,1)S(1)}, bf16[788,512]{1,0:T(8,128)(2,1)}, u32[]{:S(2)}) copy-start(bf16[788,512]{1,0:T(8,128)(2,1)} %param.16) | copy-start | bytes 2420740
  67.0 100.6 %copy-start.142 = (s32[1024]{0:T(1024)}, s32[1024]{0:T(1024)S(1)}, u32[]{:S(2)}) copy-start(s32[1024]{0:T(1024)S(1)} %pad_clamp_fusion.5) | copy-start | bytes 12292
  175.8 60.6 %all-to-all-start.2 = ((bf16[4,4,41,512]{3,1,2,0:T(4,128)(2,1)}), bf16[4,4,41,512]{3,1,2,0:T(4,128)(2,1)S(1)}, u32[]{:S(2)}, u32[]{:S(2)}) async-start(bf16[4,4,41,512]{3,1,2,0:T(4,128)(2,1)} %copy.325), calls=%async_computation.2 | async-start | bytes 1343488 | tf_op jit(solution)/shard_map/all_to_all | solution.py:144
  181.9 61.0 %copy-start.88 = (f32[4,512]{1,0:T(4,128)}, f32[4,512]{1,0:T(4,128)S(1)}, u32[]{:S(2)}) copy-start(f32[4,512]{1,0:T(4,128)S(1)} %convert_element_type.500) | copy-start | bytes 24580
  250.3 14.3 all-to-all-start.3
  278.7 13.9 all-to-all-start.10
  308.9 15.3 all-to-all-start.11
  376.3 19.8 %all-to-all-start.6 = ((bf16[4,4,41,512]{3,1,2,0:T(4,128)(2,1)}), bf16[4,4,41,512]{3,1,2,0:T(4,128)(2,1)}, u32[]{:S(2)}, u32[]{:S(2)}) async-start(bf16[4,4,41,512]{3,1,2,0:T(4,128)(2,1)} %copy.341), calls=%async_computation.6 | async-start | bytes 1343488 | tf_op jit(solution)/shard_map/all_to_all | solution.py:144
  396.1 16.5 %all-to-all-start.4 = ((bf16[4,4,41,512]{3,1,2,0:T(4,128)(2,1)}), bf16[4,4,41,512]{3,1,2,0:T(4,128)(2,1)S(1)}, u32[]{:S(2)}, u32[]{:S(2)}) async-start(bf16[4,4,41,512]{3,1,2,0:T(4,128)(2,1)} %copy.333), calls=%async_computation.4 | async-start | bytes 1343488 | tf_op jit(solution)/shard_map/all_to_all | solution.py:144
  412.6 14.7 all-to-all-start
  427.3 19.8 %all-to-all-start.7 = ((bf16[1,4,164,512]{3,1,0,2:T(4,128)(2,1)}), bf16[1,4,164,512]{3,1,0,2:T(4,128)(2,1)S(1)}, u32[]{:S(2)}, u32[]{:S(2)}) async-start(bf16[1,4,164,512]{3,1,0,2:T(4,128)(2,1)} %copy.343), calls=%async_computation.7 | async-start | bytes 1343488 | tf_op jit(solution)/shard_map/all_to_all | solution.py:159
  447.1 17.4 %all-to-all-start.1 = ((bf16[1,4,164,512]{3,1,0,2:T(4,128)(2,1)}), bf16[1,4,164,512]{3,1,0,2:T(4,128)(2,1)}, u32[]{:S(2)}, u32[]{:S(2)}) async-start(bf16[1,4,164,512]{3,1,0,2:T(4,128)(2,1)} %copy.319), calls=%async_computation.1 | async-start | bytes 1343488 | tf_op jit(solution)/shard_map/all_to_all | solution.py:159
  464.5 14.7 all-to-all-start.5
  500.5 22.5 %all-to-all-start.14 = ((bf16[4,4,41,512]{3,1,2,0:T(4,128)(2,1)}), bf16[4,4,41,512]{3,1,2,0:T(4,128)(2,1)}, u32[]{:S(2)}, u32[]{:S(2)}) async-start(bf16[4,4,41,512]{3,1,2,0:T(4,128)(2,1)} %copy.369), calls=%async_computation.14 | async-start | bytes 1343488 | tf_op jit(solution)/shard_map/all_to_all | solution.py:219
  522.4 116.7 %copy-start.128 = (bf16[197,16]{0,1:T(8,128)(2,1)}, bf16[197,16]{0,1:T(8,128)(2,1)S(1)}, u32[]{:S(2)}) copy-start(bf16[197,16]{0,1:T(8,128)(2,1)S(1)} %multiply_convert_fusion.15) | copy-start | bytes 18916
  523.0 13.9 all-to-all-start.12
  536.9 21.6 %all-to-all-start.8 = ((bf16[4,4,41,512]{3,1,2,0:T(4,128)(2,1)}), bf16[4,4,41,512]{3,1,2,0:T(4,128)(2,1)}, u32[]{:S(2)}, u32[]{:S(2)}) async-start(bf16[4,4,41,512]{3,1,2,0:T(4,128)(2,1)} %copy.345), calls=%async_computation.8 | async-start | bytes 1343488 | tf_op jit(solution)/shard_map/all_to_all | solution.py:219
  558.5 36.3 %all-to-all-start.15 = ((bf16[1,4,164,512]{3,1,0,2:T(4,128)(2,1)}), bf16[1,4,164,512]{3,1,0,2:T(4,128)(2,1)}, u32[]{:S(2)}, u32[]{:S(2)}) async-start(bf16[1,4,164,512]{3,1,0,2:T(4,128)(2,1)} %copy.371), calls=%async_computation.15 | async-start | bytes 1343488 | tf_op jit(solution)/shard_map/all_to_all | solution.py:245
  562.7 191.8 %reduce-scatter.34.cloned.1.call-start = ((), (), s32[]{:S(2)}) async-start(), calls=%async_computation.34 | async-start | bytes 147456
  594.8 14.7 all-to-all-start.13
  609.5 20.3 %all-to-all-start.9 = ((bf16[1,4,164,512]{3,1,0,2:T(4,128)(2,1)}), bf16[1,4,164,512]{3,1,0,2:T(4,128)(2,1)}, u32[]{:S(2)}, u32[]{:S(2)}) async-start(bf16[1,4,164,512]{3,1,0,2:T(4,128)(2,1)} %copy.347), calls=%async_computation.9 | async-start | bytes 1343488 | tf_op jit(solution)/shard_map/all_to_all | solution.py:245
  613.9 142.0 %reduce-scatter.32.cloned.1.call-start = ((), (), s32[]{:S(2)}) async-start(), calls=%async_computation.33 | async-start | bytes 589824
  615.1 209.4 %reduce-scatter.28.cloned.1.call-start = ((), (), s32[]{:S(2)}) async-start(), calls=%async_computation.31 | async-start | bytes 270336
  678.6 277.3 %reduce-scatter.30.cloned.1.call-start = ((), (), s32[]{:S(2)}) async-start(), calls=%async_computation.32 | async-start | bytes 270336
  679.7 425.5 %reduce-scatter.24.cloned.1.call-start = ((), (), s32[]{:S(2)}) async-start(), calls=%async_computation.29 | async-start | bytes 9437184 | tf_op jit(solution)/shard_map/reduce_scatter | solution.py:329
  700.8 556.5 %reduce-scatter.26.cloned.1.call-start = ((), (), s32[]{:S(2)}) async-start(), calls=%async_computation.30 | async-start | bytes 9437184 | tf_op jit(solution)/shard_map/reduce_scatter | solution.py:335
  741.5 651.1 %reduce-scatter.22.cloned.1.call-start = ((), (), s32[]{:S(2)}) async-start(), calls=%async_computation.28 | async-start | bytes 270336 | tf_op jit(solution)/shard_map/reduce_scatter | solution.py:345
  744.2 782.0 %reduce-scatter.20.cloned.1.call-start = ((), (), s32[]{:S(2)}) async-start(), calls=%async_computation.27 | async-start | bytes 1081344 | tf_op jit(solution)/shard_map/reduce_scatter | solution.py:344
  746.9 883.5 %reduce-scatter.18.cloned.1.call-start = ((), (), s32[]{:S(2)}) async-start(), calls=%async_computation.26 | async-start | bytes 3244032 | tf_op jit(solution)/shard_map/reduce_scatter | solution.py:343
  (282 other events, 1881.2 us)
Sparse Core Ops, SparseCore 0:
  10.9 57.7 all-gather.3
  566.8 58.5 reduce-scatter.33
  628.8 60.9 reduce-scatter.31
  692.0 132.4 reduce-scatter.27
  826.6 129.3 reduce-scatter.29
  959.9 145.2 reduce-scatter.23
  1108.9 148.3 reduce-scatter.25
  1260.2 132.3 reduce-scatter.21
  1395.4 130.7 reduce-scatter.19
  1532.9 97.4 reduce-scatter.17
where the time goes:
time: 1650 us; the launch traced here: 1640 us
  waiting for transfers between devices  886 us (54%)
  matrix products  258 us (16%)
  local copies, waits for them, and re-layouts  170 us (10%)
  blocking collectives  158 us (10%)
  other arithmetic  81.7 us (5%)
  starting transfers between devices  64.9 us (4%)
  between operations  19.1 us (1%)
    unnamed x14, waiting for transfers between devices  193 us
    reduce_scatter x1, waiting for transfers between devices, on_device(): lax.psum_scatter(expert_totals[2].astype(jnp.bfloat16), 'dp', scatter_dim...  149 us
    reduce_scatter x1, waiting for transfers between devices, on_device(): lax.psum_scatter(expert_totals[0].astype(jnp.bfloat16), 'dp', scatter_dim...  148 us
    reduce_scatter x1, waiting for transfers between devices, on_device(): lax.psum_scatter(acc_proj, ('dp', 'expert'), scatter_dimension=0, tiled=T...  134 us
    reduce_scatter x1, waiting for transfers between devices, on_device(): lax.psum_scatter(acc_router, ('dp', 'expert'), scatter_dimension=0, tiled...  133 us
    reduce_scatter x1, waiting for transfers between devices, on_device(): lax.psum_scatter(acc_qkv, ('dp', 'expert'), scatter_dimension=0, tiled=True)  104 us
    dot_general x4, matrix products, on_device(): jnp.einsum('erd,erh->edh', expert_in, grad_pre, preferred_element_type=jn...  50.5 us
    all_gather x1, blocking collectives, on_device(): lax.all_gather(norm_gains, ('dp', 'expert'), axis=0, tiled=True)  43.2 us
  transfers between devices with their start and end apart: 26, of which 13 were waited for; matrix products, arithmetic and copies ran while one was open for 23% of the time, Pallas kernels for 0%

commit v1 on v0

v1 whole, which is shorter than its diff:
```python
import jax
import jax.numpy as jnp
from jax import lax
from jax.sharding import PartitionSpec as P

HEAD = 64
SEQ = 197
ROWS = 208
MICRO = 4
CORES = 2
EPSILON = 1e-06
BF = jnp.bfloat16
F32 = jnp.float32


def norm_rows(row_block):
    row_mean = jnp.mean(row_block, axis=-1, keepdims=True)
    centred = row_block - row_mean
    inv_std = lax.rsqrt(jnp.mean(centred * centred, axis=-1, keepdims=True) + EPSILON)
    return (centred * inv_std, inv_std)


def norm_back(grad_h, normed, inv_std, gain_vec):
    scaled = grad_h * gain_vec
    return inv_std * (
        scaled
        - jnp.mean(scaled, axis=-1, keepdims=True)
        - normed * jnp.mean(scaled * normed, axis=-1, keepdims=True)
    )


def gelu_parts(pre_act):
    normal_cdf = 0.5 * (1.0 + lax.erf(pre_act * 0.7071067811865476))
    normal_pdf = jnp.exp(-0.5 * pre_act * pre_act) * 0.3989422804014327
    return (normal_cdf, normal_pdf)


def ein(spec, left, right):
    return jnp.einsum(spec, left, right, preferred_element_type=F32)


class Place:
    def __init__(self, mesh):
        self.ne = mesh.shape["expert"]
        self.nd = mesh.shape["dp"]
        self.nx = self.ne // CORES
        bits = self.nd.bit_length() - 1
        self.ny = 1 << (bits // 2)
        self.nz = self.nd // self.ny
        self.nh = self.nz // 2

    def here(self):
        ei = lax.axis_index("expert")
        di = lax.axis_index("dp")
        self.ei, self.di = ei, di
        self.x, self.c = ei // CORES, ei % CORES
        self.z, self.y = di // self.ny, di % self.ny
        self.zh, self.zl = self.z // 2, self.z % 2

    def core(self, val):
        return lax.ppermute(val, "expert", [(i, i ^ 1) for i in range(self.ne)])

    def xs(self, val, k):
        n, c = self.nx, CORES
        return lax.ppermute(val, "expert", [(i, (i // c + k) % n * c + i % c) for i in range(self.ne)])

    def ys(self, val, k):
        n = self.ny
        return lax.ppermute(val, "dp", [(i, i // n * n + (i + k) % n) for i in range(self.nd)])

    def zs(self, val, k):
        n, m = self.nz, self.ny
        return lax.ppermute(val, "dp", [(i, (i // m + k) % n * m + i % m) for i in range(self.nd)])

    def zp(self, val):
        n, m = self.nz, self.ny
        return lax.ppermute(val, "dp", [(i, (i // m ^ 1) * m + i % m) for i in range(self.nd)])

    def zhs(self, val, k):
        n, m = self.nh, self.ny
        return lax.ppermute(
            val,
            "dp",
            [(i, ((i // m // 2 + k) % n * 2 + i // m % 2) * m + i % m) for i in range(self.nd)],
        )

    def group(self, val):
        mine = [val] + [self.xs(val, k) for k in range(1, self.nx)]
        other = [self.core(v) for v in mine]
        return [v for pair in zip(mine, other) for v in pair]


def ordered(parts, own):
    n = len(parts)
    if n == 1:
        return parts[0][None]
    line = jnp.stack(parts[::-1] + parts[::-1])
    return lax.dynamic_slice_in_dim(line, n - 1 - own, n, axis=0)


def gather_dense(pl, piece):
    rows, cols = piece.shape
    val = ordered([piece] + [pl.zs(piece, k) for k in range(1, pl.nz)], pl.z)
    ys = [val] + [pl.ys(val, k) for k in range(1, pl.ny)]
    val = ordered(ys, pl.y)
    xs = [val] + [pl.xs(val, k) for k in range(1, pl.nx)]
    val = ordered(xs, pl.x)
    val = ordered([val, pl.core(val)], pl.c)
    return val.transpose(3, 2, 1, 0, 4, 5).reshape(pl.nd * pl.ne * rows, cols)


def scatter_rows(pl, full):
    cols = full.shape[1]
    val = full.reshape(pl.nz, pl.ny, pl.nx, CORES, -1, cols)

    def pick(v, axis, idx):
        return lax.dynamic_index_in_dim(v, idx, axis, keepdims=False)

    val = pick(val, 3, pl.c) + pl.core(pick(val, 3, pl.c ^ 1).astype(BF)).astype(F32)
    val = pick(val, 2, pl.x) + sum(
        pl.xs(pick(val, 2, (pl.x + k) % pl.nx).astype(BF), k).astype(F32) for k in range(1, pl.nx)
    )
    val = pick(val, 1, pl.y) + sum(
        pl.ys(pick(val, 1, (pl.y + k) % pl.ny).astype(BF), k).astype(F32) for k in range(1, pl.ny)
    )
    val = pick(val, 0, pl.z) + sum(
        pl.zs(pick(val, 0, (pl.z + k) % pl.nz).astype(BF), k).astype(F32) for k in range(1, pl.nz)
    )
    return val


def on_device(
    pl,
    tokens_in,
    grad_out,
    routes,
    norm_gains,
    biases,
    w_qkv,
    w_proj,
    w_router,
    w_up,
    b_up,
    w_down,
    b_down,
):
    pl.here()
    width = tokens_in.shape[1]
    heads = width // HEAD
    local = w_up.shape[0]
    hidden = w_up.shape[2]
    experts = local * pl.ne
    blocks = MICRO
    cap = max(2, (2 * SEQ * 13 + 8 * experts - 1) // (8 * experts))
    slots = -(-cap // 16) * 16
    hb = hidden // pl.nd
    score_scale = HEAD ** (-0.5)
    wide = experts + 7

    tok = tokens_in.reshape(blocks, SEQ, width).astype(F32)
    dy = grad_out.reshape(blocks, SEQ, width)
    pad_rows = lambda v: jnp.pad(v, ((0, 0), (0, ROWS - SEQ), (0, 0)))

    piece = jnp.concatenate([w_qkv, w_proj, w_router, norm_gains, biases], axis=1)
    cols = piece.shape[1]
    piece = jnp.pad(piece, ((0, 0), (0, -cols % 128)))
    dense = gather_dense(pl, piece)
    full_qkv = dense[:, : 3 * width]
    full_proj = dense[:, 3 * width : 4 * width]
    full_router = dense[:, 4 * width : 4 * width + experts]
    vecs = dense[:, 4 * width + experts : 4 * width + wide].astype(F32)
    gain_one, gain_two = vecs[:, 0], vecs[:, 1]
    bias_q, bias_v, bias_p, shift_one, shift_two = [vecs[:, 2 + i] for i in range(5)]

    route_rows = routes.reshape(blocks, SEQ, 2)
    names = jnp.arange(experts, dtype=jnp.int32)
    onehot = [(route_rows[:, :, c, None] == names).astype(F32) for c in range(2)]
    sel = onehot[0] + onehot[1]
    tri = (jnp.arange(SEQ)[:, None] >= jnp.arange(SEQ)[None, :]).astype(BF)
    pos = ein("ts,bse->bet", tri, sel.astype(BF)).astype(jnp.int32) - 1
    pos = jnp.where(sel.transpose(0, 2, 1) > 0, pos, -1)
    pos = jnp.pad(pos, ((0, 0), (0, 0), (0, ROWS - SEQ)), constant_values=-1)

    normed_one, inv_one = norm_rows(tok)
    act_one = (normed_one * gain_one + shift_one).astype(BF)
    qkv_bias = jnp.concatenate([bias_q, jnp.zeros_like(bias_q), bias_v])
    qkv = (ein("btd,df->btf", act_one, full_qkv) + qkv_bias).astype(BF)
    parts = qkv.reshape(blocks, SEQ, 3, heads, HEAD)
    queries, keys, values = parts[:, :, 0], parts[:, :, 1], parts[:, :, 2]
    scores = ein("ishd,ithd->ihst", queries, keys) * score_scale
    top = jnp.max(scores, axis=-1, keepdims=True)
    lse = top + jnp.log(jnp.sum(jnp.exp(scores - top), axis=-1, keepdims=True))
    probs = jnp.exp(scores - lse)
    mixed = ein("ihst,ithd->ishd", probs.astype(BF), values).astype(BF).reshape(blocks, SEQ, width)
    resid = tok + ein("btd,df->btf", mixed, full_proj) + bias_p
    normed_two, inv_two = norm_rows(resid)
    act_two = (normed_two * gain_two + shift_two).astype(BF)
    router = jax.nn.softmax(ein("btd,de->bte", act_two, full_router), axis=-1)

    act_pad, dy_pad = pad_rows(act_two), pad_rows(dy)
    mine = [act_pad, dy_pad, pos]
    peer = [pl.zp(v) for v in mine]
    near = list(zip(*[pl.group(v) for v in mine]))
    far = list(zip(*[pl.group(v) for v in peer]))

    def gather(source):
        act, dys, where = source
        logits = ein("btd,de->bte", act, full_router)
        gates = jax.nn.softmax(logits, axis=-1)
        own = lax.dynamic_slice_in_dim(where, pl.ei * local, local, axis=1)
        gates = lax.dynamic_slice_in_dim(gates, pl.ei * local, local, axis=2)
        pick = jnp.arange(slots)[None, None, :, None] == own[:, :, None, :]
        pickb = pick.astype(BF)
        rows = ein("bejt,btd->ebjd", pickb, act).astype(BF)
        dyr = ein("bejt,btd->ebjd", pickb, dys).astype(BF)
        gate = jnp.sum(jnp.where(pick, gates.transpose(0, 2, 1)[:, :, None, :], 0.0), axis=3)
        gate = gate.transpose(1, 0, 2)
        flat = lambda v: v.reshape(local, blocks * slots, *v.shape[3:])
        return flat(rows), flat(dyr), flat(gate), pickb

    near_g = [gather(s) for s in near]
    far_g = [gather(s) for s in far]
    cat = lambda gs, i: jnp.concatenate([g[i] for g in gs], axis=1)
    b_up_f, b_down_f = b_up.astype(F32), b_down.astype(F32)

    rows, dyr, gate = [cat(near_g, i) for i in range(3)]
    dres = (gate[:, :, None] * dyr.astype(F32)).astype(BF)
    pre = ein("erd,edh->erh", rows, w_up) + b_up_f[:, None, :]
    cdf, pdf = gelu_parts(pre)
    hid = (pre * cdf).astype(BF)
    res = (ein("erh,ehd->erd", hid, w_down) + b_down_f[:, None, :]).astype(BF)
    dpre = (ein("erd,ehd->erh", dres, w_down) * (cdf + pre * pdf)).astype(BF)
    din = ein("erh,edh->erd", dpre, w_up).astype(BF)
    dgate = jnp.sum(res.astype(F32) * dyr.astype(F32), axis=2)
    resg = (gate[:, :, None] * res.astype(F32)).astype(BF)
    part_b_up = jnp.sum(dpre.astype(F32), axis=1)
    part_b_down = jnp.sum(dres.astype(F32), axis=1)

    sends = []
    for s, g in enumerate(near_g):
        pickb = g[3]
        cut = lambda v: v[:, s * blocks * slots : (s + 1) * blocks * slots].reshape(
            local, blocks, slots, *v.shape[2:]
        )
        out_p = ein("bejt,ebjd->btd", pickb, cut(resg)).astype(BF)
        din_p = ein("bejt,ebjd->btd", pickb, cut(din)).astype(BF)
        dg = jnp.sum(pickb.astype(F32) * cut(dgate).transpose(1, 0, 2)[..., None], axis=2)
        dg_all = jnp.zeros((blocks, experts, ROWS), F32)
        dg_all = lax.dynamic_update_slice_in_dim(dg_all, dg, pl.ei * local, axis=1)
        sends.append((out_p, din_p, dg_all.astype(BF)))
    add = lambda a, b: (a.astype(F32) + b.astype(F32)).astype(a.dtype)
    pair = []
    for k in range(pl.nx):
        got = [pl.core(v) for v in sends[2 * k + 1]]
        pair.append([add(a, b) for a, b in zip(sends[2 * k], got)])
    total = pair[0]
    for k in range(1, pl.nx):
        got = [pl.xs(v, pl.nx - k) for v in pair[k]]
        total = [add(a, b) for a, b in zip(total, got)]
    moe = total[0][:, :SEQ].astype(F32)
    dchoice = total[1][:, :SEQ].astype(F32)
    dprob_all = total[2][:, :, :SEQ].astype(F32).transpose(0, 2, 1)
    block_out = (resid + moe).astype(BF).reshape(-1, width)

    rows2 = jnp.concatenate([rows, cat(far_g, 0)], axis=1)
    dyr2 = jnp.concatenate([dyr, cat(far_g, 1)], axis=1)
    gate2 = jnp.concatenate([gate, cat(far_g, 2)], axis=1)
    dres2 = (gate2[:, :, None] * dyr2.astype(F32)).astype(BF)
    ups, downs = [], []
    for kz in range(pl.nh):
        for ky in range(pl.ny):
            dest = (((pl.zh + kz) % pl.nh) * 2 + pl.zl) * pl.ny + (pl.y + ky) % pl.ny
            wu = lax.dynamic_slice_in_dim(w_up, dest * hb, hb, axis=2)
            wd = lax.dynamic_slice_in_dim(w_down, dest * hb, hb, axis=1)
            bu = lax.dynamic_slice_in_dim(b_up_f, dest * hb, hb, axis=1)
            pre = ein("erd,edh->erh", rows2, wu) + bu[:, None, :]
            cdf, pdf = gelu_parts(pre)
            hid = (pre * cdf).astype(BF)
            dpre = (ein("erd,ehd->erh", dres2, wd) * (cdf + pre * pdf)).astype(BF)
            downs.append(ein("erh,erd->ehd", hid, dres2).astype(BF))
            ups.append(ein("erd,erh->edh", rows2, dpre).astype(BF))

    def reduce_expert(vals):
        level = []
        for kz in range(pl.nh):
            mine = vals[kz * pl.ny].astype(F32)
            for ky in range(1, pl.ny):
                mine = mine + pl.ys(vals[kz * pl.ny + ky], ky).astype(F32)
            level.append(mine)
        mine = level[0]
        for kz in range(1, pl.nh):
            mine = mine + pl.zhs(level[kz].astype(BF), kz).astype(F32)
        return mine

    grad_up = reduce_expert(ups)
    grad_down = reduce_expert(downs)
    small = jnp.concatenate(
        [part_b_up.reshape(local, pl.nd, -1), part_b_down.reshape(local, pl.nd, -1)], axis=2
    ).transpose(1, 0, 2)
    small = small.reshape(pl.nz, pl.ny, local, -1)
    pick = lambda v, idx: lax.dynamic_index_in_dim(v, idx, 0, keepdims=False)
    small = pick(small, pl.z) + sum(
        pl.zs(pick(small, (pl.z + k) % pl.nz), k) for k in range(1, pl.nz)
    )
    small = pick(small, pl.y) + sum(
        pl.ys(pick(small, (pl.y + k) % pl.ny), k) for k in range(1, pl.ny)
    )
    grad_b_up, grad_b_down = small[:, :hb], small[:, hb:]

    dy_f = dy.astype(F32)
    dgates = [jnp.sum(o * dprob_all, axis=2, keepdims=True) for o in onehot]
    dprob = onehot[0] * dgates[0] + onehot[1] * dgates[1]
    dlogit = router * (dprob - jnp.sum(dprob * router, axis=-1, keepdims=True))
    dlogit = dlogit.astype(BF)
    g_router = ein("btd,bte->de", act_two, dlogit)
    dact_two = dchoice + ein("bte,de->btd", dlogit, full_router)
    dresid = dy_f + norm_back(dact_two, normed_two, inv_two, gain_two)
    dattn = dresid.astype(BF)
    g_proj = ein("btd,btf->df", mixed, dattn)
    dmixed = ein("btf,df->btd", dattn, full_proj).astype(BF).reshape(blocks, SEQ, heads, HEAD)
    probs_low = probs.astype(BF)
    dvalues = ein("ihst,ishd->ithd", probs_low, dmixed)
    dprobs = ein("ishd,ithd->ihst", dmixed, values)
    dscores = (probs * (dprobs - jnp.sum(dprobs * probs, axis=-1, keepdims=True))).astype(BF)
    dqueries = ein("ihst,ithd->ishd", dscores, keys) * score_scale
    dkeys = ein("ihst,ishd->ithd", dscores, queries) * score_scale
    dqkv = jnp.stack([dqueries, dkeys, dvalues], axis=2).reshape(blocks, SEQ, 3 * width).astype(BF)
    g_qkv = ein("btd,btf->df", act_one, dqkv)
    qkv_sums = jnp.sum(dqkv.astype(F32), axis=(0, 1))
    dact_one = ein("btf,df->btd", dqkv, full_qkv)
    grad_tokens = dresid + norm_back(dact_one, normed_one, inv_one, gain_one)
    g_vecs = jnp.stack(
        [
            jnp.sum(dact_one * normed_one, axis=(0, 1)),
            jnp.sum(dact_two * normed_two, axis=(0, 1)),
            qkv_sums[:width],
            qkv_sums[2 * width :],
            jnp.sum(dattn.astype(F32), axis=(0, 1)),
            jnp.sum(dact_one, axis=(0, 1)),
            jnp.sum(dact_two, axis=(0, 1)),
        ],
        axis=1,
    )
    grads = jnp.concatenate([g_qkv, g_proj, g_router, g_vecs], axis=1)
    grads = jnp.pad(grads, ((0, 0), (0, -cols % 128)))
    grads = scatter_rows(pl, grads)
    at = 4 * width
    return (
        block_out,
        grad_tokens.reshape(-1, width),
        grads[:, at + experts : at + experts + 2],
        grads[:, at + experts + 2 : at + experts + 7],
        grads[:, : 3 * width],
        grads[:, 3 * width : at],
        grads[:, at : at + experts],
        grad_up,
        grad_b_up,
        grad_down,
        grad_b_down,
    )


def solution(mesh):
    pl = Place(mesh)
    tok = P(("dp", "expert"), None)
    in_specs = (tok,) * 8 + (
        P("expert", None, None),
        P("expert", None),
        P("expert", None, None),
        P("expert", None),
    )
    out_specs = (tok,) * 7 + (
        P("expert", None, "dp"),
        P("expert", "dp"),
        P("expert", "dp", None),
        P("expert", "dp"),
    )

    def run(*args):
        return on_device(pl, *args)

    return jax.shard_map(run, mesh=mesh, in_specs=in_specs, out_specs=out_specs, check_vma=False)
```

time: 1650 us -> 566 us (0.34)
  waiting for transfers between devices: 886 us -> 139 us
  blocking collectives: 158 us -> 0 us
  local copies, waits for them, and re-layouts: 170 us -> 85.4 us
  other arithmetic: 81.7 us -> 43.7 us
  starting transfers between devices: 64.9 us -> 42.7 us
  matrix products: 258 us -> 241 us
    reduce_scatter x5 -> x0, waiting for transfers between devices: 668 us -> none  [the longest x1 149 us: on_device(): lax.psum_scatter(expert_totals[2].astype(jnp.bfloat16), 'dp', scatter_dim...]
    unnamed x14 -> x0, waiting for transfers between devices: 193 us -> none
    all_gather x4 -> x0, blocking collectives: 158 us -> none  [the longest x1 43.2 us: on_device(): lax.all_gather(norm_gains, ('dp', 'expert'), axis=0, tiled=True)]
    ppermute x0 -> x52, waiting for transfers between devices: none -> 139 us  [the longest x2 70.8 us: zhs(): lax.ppermute(val, 'dp', [(i, ((i // m // 2 + k) % n * 2 + i // m % 2) * m...]
    all_to_all x16 -> x0, starting transfers between devices: 63.8 us -> none  [the longest x4 16.9 us: on_device(): lax.all_to_all(grad_in.reshape(1, local_experts, recv_rows, model_width),...]
    gather x16 -> x0, local copies, waits for them, and re-layouts: 44.9 us -> none  [the longest x4 13 us: on_device(): jnp.take(padded, slot_table, axis=0)]
    ppermute x0 -> x52, starting transfers between devices: none -> 42.7 us  [the longest x9 12.2 us: zs(): lax.ppermute(val, 'dp', [(i, (i // m + k) % n * m + i % m) for i in range...]
    reshape x32 -> x18, local copies, waits for them, and re-layouts: 46.2 us -> 8.24 us  [the longest x1 2.77 us: on_device(): grad_tokens.reshape(-1, width)]
  transfers between devices with their start and end apart: 26 -> 52, of which waited for: 13 -> 13; matrix products, arithmetic and copies ran while one was open for 23% -> 65% of each run, Pallas kernels for 0% -> 0%
where the time goes in v1:
time: 566 us; the launch traced here: 555 us
  matrix products  241 us (43%)
  waiting for transfers between devices  139 us (25%)
  local copies, waits for them, and re-layouts  85.4 us (15%)
  other arithmetic  43.7 us (8%)
  starting transfers between devices  42.7 us (8%)
    dot_general x63, matrix products, ein(): return jnp.einsum(spec, left, right, preferred_element_type=F32)  240 us
    ppermute x2, waiting for transfers between devices, zhs(): lax.ppermute(val, 'dp', [(i, ((i // m // 2 + k) % n * 2 + i // m % 2) * m...  70.8 us
    ppermute x11, waiting for transfers between devices, xs(): lax.ppermute(val, 'expert', [(i, (i // c + k) % n * c + i % c) for i in r...  58.5 us
    unnamed x175, local copies, waits for them, and re-layouts  28.3 us
    ppermute x9, starting transfers between devices, zs(): lax.ppermute(val, 'dp', [(i, (i // m + k) % n * m + i % m) for i in range...  12.2 us
  transfers between devices with their start and end apart: 52, of which 13 were waited for; matrix products, arithmetic and copies ran while one was open for 65% of the time, Pallas kernels for 0%

profile of v1, /device:TPU:0, one launch (start us, length us, event | category | flops | bytes accessed | tf_op | source)
XLA Modules:
  0.0 554.5 jit_solution(14702509172474689618)
XLA Ops:
  3.8 5.0 collective-permute-start
  32.8 15.5 %collective-permute-done.35 = s32[4,16,208]{2,1,0:T(8,128)S(1)} collective-permute-done((s32[4,16,208]{2,1,0:T(8,128)S(1)}, s32[4,16,208]{2,1,0:T(8,128)S(1)}, u32[]{:S(2)}, u32[]{:S(2)}) %collective-permute-start.35) | collective-permute-done | bytes 53280 | tf_op jit(solution)/shard_map/ppermute | solution.py:65
  51.2 5.1 collective-permute-done.3
  63.1 9.3 %collective-permute-done.4 = bf16[2,4,16,2176]{3,2,1,0:T(8,128)(2,1)S(1)} collective-permute-done((bf16[2,4,16,2176]{3,2,1,0:T(8,128)(2,1)S(1)}, bf16[2,4,16,2176]{3,2,1,0:T(8,128)(2,1)S(1)}, u32[]{:S(2)}, u32[]{:S(2)}) %collective-permute-start.4) | collective-permute-done | bytes 557088 | tf_op jit(solution)/shard_map/ppermute | solution.py:65
  75.1 13.1 %collective-permute-done.40 = bf16[4,208,512]{2,1,0:T(8,128)(2,1)} collective-permute-done((bf16[4,208,512]{2,1,0:T(8,128)(2,1)S(1)}, bf16[4,208,512]{2,1,0:T(8,128)(2,1)}, u32[]{:S(2)}, u32[]{:S(2)}) %collective-permute-start.40) | collective-permute-done | bytes 852000 | tf_op jit(solution)/shard_map/ppermute | solution.py:65
  96.9 3.2 add_convert_fusion.1
  126.8 6.7 %collective-permute-done.9 = bf16[4,208,512]{2,1,0:T(8,128)(2,1)} collective-permute-done((bf16[4,208,512]{2,1,0:T(8,128)(2,1)}, bf16[4,208,512]{2,1,0:T(8,128)(2,1)}, u32[]{:S(2)}, u32[]{:S(2)}) %collective-permute-start.9) | collective-permute-done | bytes 852000 | tf_op jit(solution)/shard_map/ppermute | solution.py:65
  158.1 15.2 %fusion.43 = f32[4,768,2048]{2,1,0:T(8,128)} fusion(bf16[4,512,2048]{2,1,0:T(8,128)(2,1)} %param.20, bf16[4,192,512]{2,1,0:T(8,128)(2,1)} %bitcast.444, bf16[4,192,512]{2,1,0:T(8,128)(2,1)} %bitcast.447, bf16[4,192,512]{2,1,0:T(8,128)(2,1)} %bitcast.449, bf16[4,192,512]{2,1,0:T(8,128)(2,1)} %bitcast.443), kind=kOutput, calls=%fused_computation.78 | convolution fusion | flops 6455033856 | bytes 36700160 | tf_op jit(solution)/shard_map/erd,edh->erh/dot_general | solution.py:39
  173.4 22.0 %convert_reduce_fusion = (f32[4,2048]{1,0:T(4,128)S(1)}, bf16[4,768,2048]{2,1,0:T(8,128)(2,1)}) fusion(f32[4,768,2048]{2,1,0:T(8,128)} %fusion.43, f32[4,2048]{1,0:T(4,128)S(1)} %convert_element_type.557, bf16[4,2048,512]{2,1,0:T(8,128)(2,1)} %param.22, f32[4,768]{1,0:T(4,128)S(1)} %pad_maximum_fusion.2, bf16[4,192,512]{2,1,0:T(8,128)(2,1)} %bitcast.462, ...), kind=kOutput, calls=%fused_computation.10 | convolution fusion | flops 6539960320 | bytes 49360896 | tf_op jit(solution)/shard_map/erd,ehd->erh/dot_general | solution.py:39
  195.5 15.4 %convert_reduce_fusion.1 = (f32[4,512]{1,0:T(4,128)}, f32[4,768]{1,0:T(4,128)S(1)}, bf16[4,768,512]{2,1,0:T(8,128)(2,1)}) fusion(f32[4,768]{1,0:T(4,128)S(1)} %pad_maximum_fusion.2, bf16[4,192,512]{2,1,0:T(8,128)(2,1)S(1)} %bitcast.463, bf16[4,192,512]{2,1,0:T(8,128)(2,1)S(1)} %bitcast.457, bf16[4,192,512]{2,1,0:T(8,128)(2,1)S(1)} %bitcast.460, ...), kind=kOutput, calls=%fused_computation.59 | convolution fusion | flops 6510078976 | bytes 39919616 | tf_op jit(solution)/shard_map/erh,ehd->erd/dot_general | solution.py:39
  215.8 12.3 %convolution_convert_fusion = bf16[4,768,512]{2,1,0:T(8,128)(2,1)S(1)} fusion(bf16[4,768,2048]{2,1,0:T(8,128)(2,1)} %get-tuple-element.160, bf16[4,512,2048]{2,1,0:T(8,128)(2,1)} %param.20), kind=kOutput, calls=%fused_computation.91 | convolution fusion | flops 6444023808 | bytes 24117248 | tf_op jit(solution)/shard_map/erh,edh->erd/dot_general | solution.py:39
  279.3 7.6 %fusion.92 = f32[4,1536,256]{2,1,0:T(8,128)} fusion(bf16[4,1536,512]{2,1,0:T(8,128)(2,1)} %get-tuple-element.169, bf16[4,512,2048]{2,1,0:T(8,128)(2,1)} %param.20, s32[]{:T(128)S(6)} %select_n.241), kind=kOutput, calls=%fused_computation.210 | convolution fusion | flops 1610612736 | bytes 13631492 | tf_op jit(solution)/shard_map/erd,edh->erh/dot_general | solution.py:39
  286.9 5.7 %fusion.100 = f32[4,1536,256]{2,1,0:T(8,128)} fusion(bf16[4,1536,512]{2,1,0:T(8,128)(2,1)S(1)} %copy-done.1, bf16[4,512,2048]{2,1,0:T(8,128)(2,1)} %param.20, s32[]{:T(128)S(6)} %select_n.238), kind=kOutput, calls=%fused_computation.216 | convolution fusion | flops 1610612736 | bytes 13631492 | tf_op jit(solution)/shard_map/erd,edh->erh/dot_general | solution.py:39
  292.5 5.7 %fusion.104 = f32[4,1536,256]{2,1,0:T(8,128)} fusion(bf16[4,1536,512]{2,1,0:T(8,128)(2,1)S(1)} %copy-done.1, bf16[4,512,2048]{2,1,0:T(8,128)(2,1)} %param.20, s32[]{:T(128)S(6)} %select_n.237), kind=kOutput, calls=%fused_computation.219 | convolution fusion | flops 1610612736 | bytes 13631492 | tf_op jit(solution)/shard_map/erd,edh->erh/dot_general | solution.py:39
  299.4 11.1 %convolution_convert_fusion.2 = bf16[4,512,256]{2,1,0:T(8,128)(2,1)} fusion(bf16[4,1536,512]{2,1,0:T(8,128)(2,1)} %get-tuple-element.169, f32[4,1536,256]{2,1,0:T(8,128)} %fusion.92, f32[4,256]{1,0:T(4,128)S(1)} %copy-done.69, bf16[4,2048,512]{2,1,0:T(8,128)(2,1)} %param.22, s32[]{:T(128)S(6)} %select_n.241, bf16[4,1536,512]{2,1,0:T(8,128)(2,1)} %get-tuple-element.170, ...), kind=kOutput, calls=%fused_computation.146 | convolution fusion | flops 3248488448 | bytes 21000196 | tf_op jit(solution)/shard_map/erd,erh->edh/dot_general | solution.py:39
  310.5 7.0 %fusion.60 = bf16[4,256,512]{2,1,0:T(8,128)(2,1)} fusion(f32[4,1536,256]{2,1,0:T(8,128)} %fusion.92, f32[4,256]{1,0:T(4,128)S(1)} %copy-done.69, bf16[4,1536,512]{2,1,0:T(8,128)(2,1)} %get-tuple-element.170, f32[4,1536]{1,0:T(4,128)S(1)} %concatenate.40), kind=kOutput, calls=%fused_computation.141 | convolution fusion | flops 1630011392 | bytes 13660160 | tf_op jit(solution)/shard_map/erh,erd->ehd/dot_general | solution.py:39
  317.5 11.5 %convolution_convert_fusion.4 = bf16[4,512,256]{2,1,0:T(8,128)(2,1)} fusion(bf16[4,1536,512]{2,1,0:T(8,128)(2,1)} %get-tuple-element.169, f32[4,1536,256]{2,1,0:T(8,128)} %fusion.100, f32[4,256]{1,0:T(4,128)S(1)} %copy-done.68, bf16[4,2048,512]{2,1,0:T(8,128)(2,1)} %param.22, s32[]{:T(128)S(6)} %select_n.238, ...), kind=kOutput, calls=%fused_computation.148 | convolution fusion | flops 3248488448 | bytes 21000196 | tf_op jit(solution)/shard_map/erd,erh->edh/dot_general | solution.py:39
  328.9 7.1 %fusion.62 = bf16[4,256,512]{2,1,0:T(8,128)(2,1)} fusion(f32[4,1536,256]{2,1,0:T(8,128)} %fusion.100, f32[4,256]{1,0:T(4,128)S(1)} %copy-done.68, bf16[4,1536,512]{2,1,0:T(8,128)(2,1)} %get-tuple-element.170, f32[4,1536]{1,0:T(4,128)S(1)} %concatenate.40), kind=kOutput, calls=%fused_computation.143 | convolution fusion | flops 1630011392 | bytes 13660160 | tf_op jit(solution)/shard_map/erh,erd->ehd/dot_general | solution.py:39
  339.8 11.0 %convolution_convert_fusion.5 = bf16[4,512,256]{2,1,0:T(8,128)(2,1)} fusion(bf16[4,1536,512]{2,1,0:T(8,128)(2,1)} %get-tuple-element.169, f32[4,1536,256]{2,1,0:T(8,128)} %fusion.104, f32[4,256]{1,0:T(4,128)S(1)} %copy-done.67, bf16[4,2048,512]{2,1,0:T(8,128)(2,1)} %param.22, s32[]{:T(128)S(6)} %select_n.237, ...), kind=kOutput, calls=%fused_computation.149 | convolution fusion | flops 3248488448 | bytes 21000196 | tf_op jit(solution)/shard_map/erd,erh->edh/dot_general | solution.py:39
  350.8 7.2 %fusion.63 = bf16[4,256,512]{2,1,0:T(8,128)(2,1)} fusion(f32[4,1536,256]{2,1,0:T(8,128)} %fusion.104, f32[4,256]{1,0:T(4,128)S(1)} %copy-done.67, bf16[4,1536,512]{2,1,0:T(8,128)(2,1)} %get-tuple-element.170, f32[4,1536]{1,0:T(4,128)S(1)} %concatenate.40), kind=kOutput, calls=%fused_computation.144 | convolution fusion | flops 1630011392 | bytes 13660160 | tf_op jit(solution)/shard_map/erh,erd->ehd/dot_general | solution.py:39
  360.1 7.6 %fusion.96 = f32[4,1536,256]{2,1,0:T(8,128)} fusion(bf16[4,1536,512]{2,1,0:T(8,128)(2,1)} %get-tuple-element.169, bf16[4,512,2048]{2,1,0:T(8,128)(2,1)} %param.20, s32[]{:T(128)S(6)} %select_n.240), kind=kOutput, calls=%fused_computation.213 | convolution fusion | flops 1610612736 | bytes 13631492 | tf_op jit(solution)/shard_map/erd,edh->erh/dot_general | solution.py:39
  374.6 6.1 %collective-permute-done.14 = bf16[4,208,512]{2,1,0:T(8,128)(2,1)S(1)} collective-permute-done((bf16[4,208,512]{2,1,0:T(8,128)(2,1)S(1)}, bf16[4,208,512]{2,1,0:T(8,128)(2,1)S(1)}, u32[]{:S(2)}, u32[]{:S(2)}) %collective-permute-start.14) | collective-permute-done | bytes 852000 | tf_op jit(solution)/shard_map/ppermute | solution.py:65
  388.8 5.3 convolution_bitcast_fusion.1
  394.1 4.5 multiply_reduce_fusion
  398.6 4.4 multiply_convert_fusion.3
  422.7 5.8 %convolution_bitcast_fusion = f32[512,1536]{1,0:T(8,128)} fusion(bf16[4,197,512]{2,1,0:T(8,128)(2,1)} %convert_element_type.633, bf16[4,197,1536]{1,2,0:T(8,128)(2,1)} %bitcast.451), kind=kOutput, calls=%fused_computation.73 | convolution fusion | flops 1239416832 | bytes 6373376 | tf_op jit(solution)/shard_map/btd,btf->df/dot_general | solution.py:39
  428.6 5.7 %concatenate.38 = f32[512,2071]{1,0:T(8,128)} concatenate(f32[512,1536]{1,0:T(8,128)} %convolution_bitcast_fusion, f32[512,512]{1,0:T(8,128)S(1)} %copy-done.25, f32[512,16]{1,0:T(8,128)S(1)} %copy-done.38, f32[512,1]{1,0:T(8,128)S(1)} %copy.357, f32[512,1]{1,0:T(8,128)S(1)} %copy.358, f32[512,1]{1,0:T(8,128)S(1)} %copy-done.39, f32[512,1]{1,0:T(8,128)S(1)} %copy-done.40, ...), dimensions={1} | concatenate | bytes 8482816 | tf_op jit(solution)/shard_map/concatenate | solution.py:344
  439.1 11.1 %add_convert_fusion.3 = bf16[4,512,256]{2,1,0:T(8,128)(2,1)} fusion(bf16[4,512,256]{2,1,0:T(8,128)(2,1)} %collective-permute-done.43, bf16[4,1536,512]{2,1,0:T(8,128)(2,1)} %get-tuple-element.169, f32[4,1536,256]{2,1,0:T(8,128)} %fusion.96, f32[4,256]{1,0:T(4,128)S(1)} %copy-done.66, bf16[4,2048,512]{2,1,0:T(8,128)(2,1)} %param.22, s32[]{:T(128)S(6)} %select_n.240, ...), kind=kOutput, calls=%fused_computation.105 | convolution fusion | flops 3250585600 | bytes 22048772 | tf_op jit(solution)/shard_map/erd,erh->edh/dot_general | solution.py:39
  454.8 6.7 %add_convert_fusion.2 = bf16[4,256,512]{2,1,0:T(8,128)(2,1)S(1)} fusion(bf16[4,256,512]{2,1,0:T(8,128)(2,1)} %collective-permute-done.50, f32[4,1536,256]{2,1,0:T(8,128)} %fusion.96, f32[4,256]{1,0:T(4,128)S(1)} %copy-done.66, bf16[4,1536,512]{2,1,0:T(8,128)(2,1)} %get-tuple-element.170, f32[4,1536]{1,0:T(4,128)S(1)} %concatenate.40), kind=kOutput, calls=%fused_computation.103 | convolution fusion | flops 1632108544 | bytes 14708736 | tf_op jit(solution)/shard_map/erh,erd->ehd/dot_general | solution.py:39
  462.4 6.6 %collective-permute-done.25 = bf16[4,2,16,2176]{3,2,0,1:T(8,128)(2,1)S(1)} collective-permute-done((bf16[4,2,16,2176]{3,2,0,1:T(8,128)(2,1)S(1)}, bf16[4,2,16,2176]{3,2,0,1:T(8,128)(2,1)S(1)}, u32[]{:S(2)}, u32[]{:S(2)}) %collective-permute-start.25) | collective-permute-done | bytes 557088 | tf_op jit(solution)/shard_map/ppermute | solution.py:65
  470.7 51.5 %collective-permute-done.44 = bf16[4,512,256]{2,1,0:T(8,128)(2,1)S(1)} collective-permute-done((bf16[4,512,256]{2,1,0:T(8,128)(2,1)}, bf16[4,512,256]{2,1,0:T(8,128)(2,1)S(1)}, u32[]{:S(2)}, u32[]{:S(2)}) %collective-permute-start.44) | collective-permute-done | bytes 1048608 | tf_op jit(solution)/shard_map/ppermute | solution.py:81
  528.4 19.4 %collective-permute-done.51 = bf16[4,256,512]{2,1,0:T(8,128)(2,1)S(1)} collective-permute-done((bf16[4,256,512]{2,1,0:T(8,128)(2,1)S(1)}, bf16[4,256,512]{2,1,0:T(8,128)(2,1)S(1)}, u32[]{:S(2)}, u32[]{:S(2)}) %collective-permute-start.51) | collective-permute-done | bytes 1048608 | tf_op jit(solution)/shard_map/ppermute | solution.py:81
  (491 shorter events, 220.5 us)
Async XLA Ops:
  3.8 24.0 %collective-permute-start = (bf16[16,2176]{1,0:T(8,128)(2,1)}, bf16[16,2176]{1,0:T(8,128)(2,1)S(1)}, u32[]{:S(2)}, u32[]{:S(2)}) collective-permute-start(bf16[16,2176]{1,0:T(8,128)(2,1)} %pad.19), channel_id=1, source_target_pairs={{0,24},{4,28},{8,0},{12,4},{16,8},{20,12},{24,16},{28,20},{1,25},{... | collective-permute-start | bytes 208904 | tf_op jit(solution)/shard_map/ppermute | solution.py:73
  8.9 20.7 %collective-permute-start.1 = (bf16[16,2176]{1,0:T(8,128)(2,1)}, bf16[16,2176]{1,0:T(8,128)(2,1)S(1)}, u32[]{:S(2)}, u32[]{:S(2)}) collective-permute-start(bf16[16,2176]{1,0:T(8,128)(2,1)} %pad.19), channel_id=1, source_target_pairs={{0,16},{4,20},{8,24},{12,28},{16,0},{20,4},{24,8},{28,12},{1,17},{... | collective-permute-start | bytes 208904 | tf_op jit(solution)/shard_map/ppermute | solution.py:73
  8.9 21.0 %collective-permute-start.2 = (bf16[16,2176]{1,0:T(8,128)(2,1)}, bf16[16,2176]{1,0:T(8,128)(2,1)}, u32[]{:S(2)}, u32[]{:S(2)}) collective-permute-start(bf16[16,2176]{1,0:T(8,128)(2,1)} %pad.19), channel_id=1, source_target_pairs={{0,8},{4,12},{8,16},{12,20},{16,24},{20,28},{24,0},{28,4},{1,9},{5... | collective-permute-start | bytes 208904 | tf_op jit(solution)/shard_map/ppermute | solution.py:73
  25.6 32.2 %collective-permute-start.16 = (bf16[4,208,512]{2,1,0:T(8,128)(2,1)}, bf16[4,208,512]{2,1,0:T(8,128)(2,1)S(1)}, u32[]{:S(2)}, u32[]{:S(2)}) collective-permute-start(bf16[4,208,512]{2,1,0:T(8,128)(2,1)} %pad.22), channel_id=1, source_target_pairs={{0,2},{1,3},{2,0},{3,1},{4,6},{5,7},{6,4},{7,5},{8,10},{9,11},{10,... | collective-permute-start | bytes 2555912 | tf_op jit(solution)/shard_map/ppermute | solution.py:65
  27.8 30.4 %collective-permute-start.15 = (bf16[4,208,512]{2,1,0:T(8,128)(2,1)}, bf16[4,208,512]{2,1,0:T(8,128)(2,1)S(1)}, u32[]{:S(2)}, u32[]{:S(2)}) collective-permute-start(bf16[4,208,512]{2,1,0:T(8,128)(2,1)} %pad.22), channel_id=1, source_target_pairs={{0,1},{1,0},{2,3},{3,2},{4,5},{5,4},{6,7},{7,6},{8,9},{9,8},{10,11... | collective-permute-start | bytes 2555912 | tf_op jit(solution)/shard_map/ppermute | solution.py:61
  27.8 30.9 %collective-permute-start.38 = (bf16[4,208,512]{2,1,0:T(8,128)(2,1)}, bf16[4,208,512]{2,1,0:T(8,128)(2,1)S(1)}, u32[]{:S(2)}, u32[]{:S(2)}) collective-permute-start(bf16[4,208,512]{2,1,0:T(8,128)(2,1)} %pad.22), channel_id=1, source_target_pairs={{0,8},{4,12},{8,0},{12,4},{16,24},{20,28},{24,16},{28,20},{1,9},{5... | collective-permute-start | bytes 2555912 | tf_op jit(solution)/shard_map/ppermute | solution.py:77
  29.9 19.9 %collective-permute-start.33 = (s32[4,16,208]{2,1,0:T(8,128)S(1)}, s32[4,16,208]{2,1,0:T(8,128)S(1)}, u32[]{:S(2)}, u32[]{:S(2)}) collective-permute-start(s32[4,16,208]{2,1,0:T(8,128)S(1)} %collective-permute-done.31), channel_id=1, source_target_pairs={{0,1},{1,0},{2,3},{3,2},{4,5},{5,4},{6,7},{7,6},{8,9},{9,8},{10,11... | collective-permute-start | bytes 159752 | tf_op jit(solution)/shard_map/ppermute | solution.py:61
  59.7 28.5 %collective-permute-start.40 = (bf16[4,208,512]{2,1,0:T(8,128)(2,1)S(1)}, bf16[4,208,512]{2,1,0:T(8,128)(2,1)}, u32[]{:S(2)}, u32[]{:S(2)}) collective-permute-start(bf16[4,208,512]{2,1,0:T(8,128)(2,1)S(1)} %collective-permute-done.38), channel_id=1, source_target_pairs={{0,2},{1,3},{2,0},{3,1},{4,6},{5,7},{6,4},{7,5},{8,10},{9,11},{10,... | collective-permute-start | bytes 2555912 | tf_op jit(solution)/shard_map/ppermute | solution.py:65
  73.2 20.5 %collective-permute-start.5 = (bf16[2,2,4,16,2176]{4,3,2,1,0:T(8,128)(2,1)S(1)}, bf16[2,2,4,16,2176]{4,3,2,1,0:T(8,128)(2,1)S(1)}, u32[]{:S(2)}, u32[]{:S(2)}) collective-permute-start(bf16[2,2,4,16,2176]{4,3,2,1,0:T(8,128)(2,1)S(1)} %fusion.91), channel_id=1, source_target_pairs={{0,1},{1,0},{2,3},{3,2},{4,5},{5,4},{6,7},{7,6},{8,9},{9,8},{10,11... | collective-permute-start | bytes 3342344 | tf_op jit(solution)/shard_map/ppermute | solution.py:61
  89.8 32.7 %collective-permute-start.41 = (bf16[4,208,512]{2,1,0:T(8,128)(2,1)}, bf16[4,208,512]{2,1,0:T(8,128)(2,1)}, u32[]{:S(2)}, u32[]{:S(2)}) collective-permute-start(bf16[4,208,512]{2,1,0:T(8,128)(2,1)} %collective-permute-done.40), channel_id=1, source_target_pairs={{0,1},{1,0},{2,3},{3,2},{4,5},{5,4},{6,7},{7,6},{8,9},{9,8},{10,11... | collective-permute-start | bytes 2555912 | tf_op jit(solution)/shard_map/ppermute | solution.py:61
  111.8 21.7 %collective-permute-start.9 = (bf16[4,208,512]{2,1,0:T(8,128)(2,1)}, bf16[4,208,512]{2,1,0:T(8,128)(2,1)}, u32[]{:S(2)}, u32[]{:S(2)}) collective-permute-start(bf16[4,208,512]{2,1,0:T(8,128)(2,1)} %pad.21), channel_id=1, source_target_pairs={{0,2},{1,3},{2,0},{3,1},{4,6},{5,7},{6,4},{7,5},{8,10},{9,11},{10,... | collective-permute-start | bytes 2555912 | tf_op jit(solution)/shard_map/ppermute | solution.py:65
  112.9 25.4 %collective-permute-start.30 = (bf16[4,208,512]{2,1,0:T(8,128)(2,1)}, bf16[4,208,512]{2,1,0:T(8,128)(2,1)}, u32[]{:S(2)}, u32[]{:S(2)}) collective-permute-start(bf16[4,208,512]{2,1,0:T(8,128)(2,1)} %pad.21), channel_id=1, source_target_pairs={{0,8},{4,12},{8,0},{12,4},{16,24},{20,28},{24,16},{28,20},{1,9},{5... | collective-permute-start | bytes 2555912 | tf_op jit(solution)/shard_map/ppermute | solution.py:77
  146.1 90.8 %collective-permute-start.32 = (bf16[4,208,512]{2,1,0:T(8,128)(2,1)}, bf16[4,208,512]{2,1,0:T(8,128)(2,1)}, u32[]{:S(2)}, u32[]{:S(2)}) collective-permute-start(bf16[4,208,512]{2,1,0:T(8,128)(2,1)} %collective-permute-done.30), channel_id=1, source_target_pairs={{0,1},{1,0},{2,3},{3,2},{4,5},{5,4},{6,7},{7,6},{8,9},{9,8},{10,11... | collective-permute-start | bytes 2555912 | tf_op jit(solution)/shard_map/ppermute | solution.py:61
  146.6 98.0 %collective-permute-start.34 = (bf16[4,208,512]{2,1,0:T(8,128)(2,1)}, bf16[4,208,512]{2,1,0:T(8,128)(2,1)}, u32[]{:S(2)}, u32[]{:S(2)}) collective-permute-start(bf16[4,208,512]{2,1,0:T(8,128)(2,1)} %collective-permute-done.30), channel_id=1, source_target_pairs={{0,2},{1,3},{2,0},{3,1},{4,6},{5,7},{6,4},{7,5},{8,10},{9,11},{10,... | collective-permute-start | bytes 2555912 | tf_op jit(solution)/shard_map/ppermute | solution.py:65
  212.6 49.7 %collective-permute-start.22 = (bf16[4,16,208]{2,1,0:T(8,128)(2,1)}, bf16[4,16,208]{2,1,0:T(8,128)(2,1)S(1)}, u32[]{:S(2)}, u32[]{:S(2)}) collective-permute-start(bf16[4,16,208]{2,1,0:T(8,128)(2,1)} %constant_dynamic-update-slice_fusion.16), channel_id=1, source_target_pairs={{0,1},{1,0},{2,3},{3,2},{4,5},{5,4},{6,7},{7,6},{8,9},{9,8},{10,11... | collective-permute-start | bytes 79880 | tf_op jit(solution)/shard_map/ppermute | solution.py:61
  215.2 53.5 %collective-permute-start.21 = (bf16[4,16,208]{2,1,0:T(8,128)(2,1)}, bf16[4,16,208]{2,1,0:T(8,128)(2,1)}, u32[]{:S(2)}, u32[]{:S(2)}) collective-permute-start(bf16[4,16,208]{2,1,0:T(8,128)(2,1)} %constant_dynamic-update-slice_fusion.18), channel_id=1, source_target_pairs={{0,1},{1,0},{2,3},{3,2},{4,5},{5,4},{6,7},{7,6},{8,9},{9,8},{10,11... | collective-permute-start | bytes 79880 | tf_op jit(solution)/shard_map/ppermute | solution.py:61
  261.6 74.4 %collective-permute-start.19 = (bf16[4,208,512]{2,1,0:T(8,128)(2,1)}, bf16[4,208,512]{2,1,0:T(8,128)(2,1)}, u32[]{:S(2)}, u32[]{:S(2)}) collective-permute-start(bf16[4,208,512]{2,1,0:T(8,128)(2,1)} %bitcast_convert_fusion), channel_id=1, source_target_pairs={{0,1},{1,0},{2,3},{3,2},{4,5},{5,4},{6,7},{7,6},{8,9},{9,8},{10,11... | collective-permute-start | bytes 2555912 | tf_op jit(solution)/shard_map/ppermute | solution.py:61
  261.7 107.6 %collective-permute-start.18 = (bf16[4,208,512]{2,1,0:T(8,128)(2,1)}, bf16[4,208,512]{2,1,0:T(8,128)(2,1)}, u32[]{:S(2)}, u32[]{:S(2)}) collective-permute-start(bf16[4,208,512]{2,1,0:T(8,128)(2,1)} %bitcast_convert_fusion.2), channel_id=1, source_target_pairs={{0,1},{1,0},{2,3},{3,2},{4,5},{5,4},{6,7},{7,6},{8,9},{9,8},{10,11... | collective-permute-start | bytes 2555912 | tf_op jit(solution)/shard_map/ppermute | solution.py:61
  262.2 95.9 %collective-permute-start.13 = (bf16[4,208,512]{2,1,0:T(8,128)(2,1)}, bf16[4,208,512]{2,1,0:T(8,128)(2,1)}, u32[]{:S(2)}, u32[]{:S(2)}) collective-permute-start(bf16[4,208,512]{2,1,0:T(8,128)(2,1)} %bitcast_convert_fusion.4), channel_id=1, source_target_pairs={{0,1},{1,0},{2,3},{3,2},{4,5},{5,4},{6,7},{7,6},{8,9},{9,8},{10,11... | collective-permute-start | bytes 2555912 | tf_op jit(solution)/shard_map/ppermute | solution.py:61
  268.7 105.3 %collective-permute-start.12 = (bf16[4,208,512]{2,1,0:T(8,128)(2,1)}, bf16[4,208,512]{2,1,0:T(8,128)(2,1)}, u32[]{:S(2)}, u32[]{:S(2)}) collective-permute-start(bf16[4,208,512]{2,1,0:T(8,128)(2,1)} %bitcast_convert_fusion.6), channel_id=1, source_target_pairs={{0,1},{1,0},{2,3},{3,2},{4,5},{5,4},{6,7},{7,6},{8,9},{9,8},{10,11... | collective-permute-start | bytes 2555912 | tf_op jit(solution)/shard_map/ppermute | solution.py:61
  338.3 31.5 %collective-permute-start.20 = (bf16[4,208,512]{2,1,0:T(8,128)(2,1)}, bf16[4,208,512]{2,1,0:T(8,128)(2,1)}, u32[]{:S(2)}, u32[]{:S(2)}) collective-permute-start(bf16[4,208,512]{2,1,0:T(8,128)(2,1)} %add_convert_fusion.4), channel_id=1, source_target_pairs={{0,2},{1,3},{2,0},{3,1},{4,6},{5,7},{6,4},{7,5},{8,10},{9,11},{10,... | collective-permute-start | bytes 2555912 | tf_op jit(solution)/shard_map/ppermute | solution.py:65
  359.5 21.1 %collective-permute-start.14 = (bf16[4,208,512]{2,1,0:T(8,128)(2,1)S(1)}, bf16[4,208,512]{2,1,0:T(8,128)(2,1)S(1)}, u32[]{:S(2)}, u32[]{:S(2)}) collective-permute-start(bf16[4,208,512]{2,1,0:T(8,128)(2,1)S(1)} %add_convert_fusion.5), channel_id=1, source_target_pairs={{0,2},{1,3},{2,0},{3,1},{4,6},{5,7},{6,4},{7,5},{8,10},{9,11},{10,... | collective-permute-start | bytes 2555912 | tf_op jit(solution)/shard_map/ppermute | solution.py:65
  367.7 71.4 %collective-permute-start.43 = (bf16[4,512,256]{2,1,0:T(8,128)(2,1)}, bf16[4,512,256]{2,1,0:T(8,128)(2,1)}, u32[]{:S(2)}, u32[]{:S(2)}) collective-permute-start(bf16[4,512,256]{2,1,0:T(8,128)(2,1)} %convolution_convert_fusion.2), channel_id=1, source_target_pairs={{0,4},{4,0},{8,12},{12,8},{16,20},{20,16},{24,28},{28,24},{1,5},{5... | collective-permute-start | bytes 3145736 | tf_op jit(solution)/shard_map/ppermute | solution.py:69
  369.3 101.5 %collective-permute-start.42 = (bf16[4,512,256]{2,1,0:T(8,128)(2,1)}, bf16[4,512,256]{2,1,0:T(8,128)(2,1)}, u32[]{:S(2)}, u32[]{:S(2)}) collective-permute-start(bf16[4,512,256]{2,1,0:T(8,128)(2,1)} %convolution_convert_fusion.4), channel_id=1, source_target_pairs={{0,4},{4,0},{8,12},{12,8},{16,20},{20,16},{24,28},{28,24},{1,5},{5... | collective-permute-start | bytes 3145736 | tf_op jit(solution)/shard_map/ppermute | solution.py:69
  369.8 85.1 %collective-permute-start.50 = (bf16[4,256,512]{2,1,0:T(8,128)(2,1)}, bf16[4,256,512]{2,1,0:T(8,128)(2,1)}, u32[]{:S(2)}, u32[]{:S(2)}) collective-permute-start(bf16[4,256,512]{2,1,0:T(8,128)(2,1)} %fusion.60), channel_id=1, source_target_pairs={{0,4},{4,0},{8,12},{12,8},{16,20},{20,16},{24,28},{28,24},{1,5},{5... | collective-permute-start | bytes 3145736 | tf_op jit(solution)/shard_map/ppermute | solution.py:69
  374.0 154.3 %collective-permute-start.49 = (bf16[4,256,512]{2,1,0:T(8,128)(2,1)}, bf16[4,256,512]{2,1,0:T(8,128)(2,1)}, u32[]{:S(2)}, u32[]{:S(2)}) collective-permute-start(bf16[4,256,512]{2,1,0:T(8,128)(2,1)} %fusion.62), channel_id=1, source_target_pairs={{0,4},{4,0},{8,12},{12,8},{16,20},{20,16},{24,28},{28,24},{1,5},{5... | collective-permute-start | bytes 3145736 | tf_op jit(solution)/shard_map/ppermute | solution.py:69
  450.2 72.0 %collective-permute-start.44 = (bf16[4,512,256]{2,1,0:T(8,128)(2,1)}, bf16[4,512,256]{2,1,0:T(8,128)(2,1)S(1)}, u32[]{:S(2)}, u32[]{:S(2)}) collective-permute-start(bf16[4,512,256]{2,1,0:T(8,128)(2,1)} %add_convert_fusion.3), channel_id=1, source_target_pairs={{0,16},{4,20},{8,24},{12,28},{16,0},{20,4},{24,8},{28,12},{1,17},{... | collective-permute-start | bytes 3145736 | tf_op jit(solution)/shard_map/ppermute | solution.py:81
  461.5 86.2 %collective-permute-start.51 = (bf16[4,256,512]{2,1,0:T(8,128)(2,1)S(1)}, bf16[4,256,512]{2,1,0:T(8,128)(2,1)S(1)}, u32[]{:S(2)}, u32[]{:S(2)}) collective-permute-start(bf16[4,256,512]{2,1,0:T(8,128)(2,1)S(1)} %add_convert_fusion.2), channel_id=1, source_target_pairs={{0,16},{4,20},{8,24},{12,28},{16,0},{20,4},{24,8},{28,12},{1,17},{... | collective-permute-start | bytes 3145736 | tf_op jit(solution)/shard_map/ppermute | solution.py:81
  469.2 56.0 %collective-permute-start.26 = (bf16[4,16,2176]{2,1,0:T(8,128)(2,1)S(1)}, bf16[4,16,2176]{2,1,0:T(8,128)(2,1)S(1)}, u32[]{:S(2)}, u32[]{:S(2)}) collective-permute-start(bf16[4,16,2176]{2,1,0:T(8,128)(2,1)S(1)} %fusion.172), channel_id=1, source_target_pairs={{0,4},{4,0},{8,12},{12,8},{16,20},{20,16},{24,28},{28,24},{1,5},{5... | collective-permute-start | bytes 835592 | tf_op jit(solution)/shard_map/ppermute | solution.py:69
  525.2 25.5 %collective-permute-start.29 = (bf16[16,2176]{1,0:T(8,128)(2,1)S(1)}, bf16[16,2176]{1,0:T(8,128)(2,1)S(1)}, u32[]{:S(2)}, u32[]{:S(2)}) collective-permute-start(bf16[16,2176]{1,0:T(8,128)(2,1)S(1)} %get-tuple-element.114), channel_id=1, source_target_pairs={{0,24},{4,28},{8,0},{12,4},{16,8},{20,12},{24,16},{28,20},{1,25},{... | collective-permute-start | bytes 208904 | tf_op jit(solution)/shard_map/ppermute | solution.py:73
  527.7 23.0 %collective-permute-start.28 = (bf16[16,2176]{1,0:T(8,128)(2,1)S(1)}, bf16[16,2176]{1,0:T(8,128)(2,1)S(1)}, u32[]{:S(2)}, u32[]{:S(2)}) collective-permute-start(bf16[16,2176]{1,0:T(8,128)(2,1)S(1)} %get-tuple-element.115), channel_id=1, source_target_pairs={{0,16},{4,20},{8,24},{12,28},{16,0},{20,4},{24,8},{28,12},{1,17},{... | collective-permute-start | bytes 208904 | tf_op jit(solution)/shard_map/ppermute | solution.py:73
  527.7 23.0 %collective-permute-start.27 = (bf16[16,2176]{1,0:T(8,128)(2,1)S(1)}, bf16[16,2176]{1,0:T(8,128)(2,1)S(1)}, u32[]{:S(2)}, u32[]{:S(2)}) collective-permute-start(bf16[16,2176]{1,0:T(8,128)(2,1)S(1)} %get-tuple-element.113), channel_id=1, source_target_pairs={{0,8},{4,12},{8,16},{12,20},{16,24},{20,28},{24,0},{28,4},{1,9},{5... | collective-permute-start | bytes 208904 | tf_op jit(solution)/shard_map/ppermute | solution.py:73
  (95 other events, 1220.0 us)

commit v2 on v1

v2 whole, which is shorter than its diff:
```python
import functools

import jax
import jax.numpy as jnp
from jax import lax
from jax.experimental import pallas as pl
from jax.experimental.pallas import tpu as pltpu
from jax.sharding import PartitionSpec as P

HEAD = 64
SEQ = 197
MICRO = 4
HALF = 2
CORES = 2
EPSILON = 1e-06
BF = jnp.bfloat16
F32 = jnp.float32


LOW = -1e30


def cost(us):
    return pl.CostEstimate(flops=int(us * 0.35e9), bytes_accessed=1 << 20, transcendentals=0)


def dot(left, right, over_left, over_right):
    return lax.dot_general(
        left, right, (((over_left,), (over_right,)), ((), ())), preferred_element_type=F32
    )


def iota(shape, axis):
    return lax.broadcasted_iota(jnp.int32, shape, axis)


def norm_rows(row_block):
    row_mean = jnp.mean(row_block, axis=-1, keepdims=True)
    centred = row_block - row_mean
    inv_std = lax.rsqrt(jnp.mean(centred * centred, axis=-1, keepdims=True) + EPSILON)
    return (centred * inv_std, inv_std)


def norm_back(grad_h, normed, inv_std, gain_vec):
    scaled = grad_h * gain_vec
    return inv_std * (
        scaled
        - jnp.mean(scaled, axis=-1, keepdims=True)
        - normed * jnp.mean(scaled * normed, axis=-1, keepdims=True)
    )


def gelu_parts(pre_act):
    normal_cdf = 0.5 * (1.0 + lax.erf(pre_act * 0.7071067811865476))
    normal_pdf = jnp.exp(-0.5 * pre_act * pre_act) * 0.3989422804014327
    return (normal_cdf, normal_pdf)


def half_lanes(pair, side):
    lane = iota(pair.shape, 1)
    keep = lane < HEAD if side == 0 else lane >= HEAD
    return jnp.where(keep, pair, jnp.zeros_like(pair))


def router_rows(tailt, act, experts):
    logits = dot(tailt, act, 1, 1)[:experts]
    top = jnp.max(logits, axis=0, keepdims=True)
    powers = jnp.exp(logits - top)
    return powers / jnp.sum(powers, axis=0, keepdims=True)


def forward_kernel(experts, tok, dense, tailt, qkv_o, mix_o, res_o, act_o, lse_o):
    width = tok.shape[2]
    rows = tok.shape[1]
    pairs = width // (2 * HEAD)
    vec = tailt[...].astype(F32)[experts : experts + 7]
    x = tok[0].astype(F32)
    normed, _ = norm_rows(x)
    act = (normed * vec[0:1] + vec[5:6]).astype(BF)
    bias = jnp.concatenate([vec[2:3], jnp.zeros_like(vec[2:3]), vec[3:4]], axis=1)
    qkv_o[0] = (dot(act, dense[:, : 3 * width], 1, 0) + bias).astype(BF)
    seen = iota((rows, rows), 1) < SEQ
    lse_all = jnp.zeros((rows, 128), F32)
    lane = iota((rows, 128), 1)
    for p in range(pairs):
        at = p * 2 * HEAD
        q = qkv_o[0, :, at : at + 2 * HEAD]
        k = qkv_o[0, :, width + at : width + at + 2 * HEAD]
        v = qkv_o[0, :, 2 * width + at : 2 * width + at + 2 * HEAD]
        both = None
        for side in range(2):
            scores = dot(half_lanes(q, side), k, 1, 1) * (HEAD ** (-0.5))
            scores = jnp.where(seen, scores, LOW)
            top = jnp.max(scores, axis=1, keepdims=True)
            lse = top + jnp.log(jnp.sum(jnp.exp(scores - top), axis=1, keepdims=True))
            low = jnp.exp(scores - lse).astype(BF)
            part = dot(low, half_lanes(v, side), 1, 0)
            both = part if both is None else both + part
            lse_all = jnp.where(lane == 2 * p + side, lse, lse_all)
        mix_o[0, :, at : at + 2 * HEAD] = both.astype(BF)
    lse_o[0] = lse_all
    resid = x + (dot(mix_o[0], dense[:, 3 * width : 4 * width], 1, 0) + vec[4:5])
    res_o[0] = resid
    normed, _ = norm_rows(resid)
    act = (normed * vec[1:2] + vec[6:7]).astype(BF)
    act_o[0] = act
    gates = router_rows(tailt[...], act, experts)
    half = experts // 2
    blank = jnp.zeros((half, width // 2 - rows), F32)
    packed = jnp.concatenate([gates[:half], blank, gates[half:], blank], axis=1)
    act_o[0, rows - half :, :] = packed.astype(BF)


def run_forward(tok, dense, tailt, part, experts):
    _, rows, width = tok.shape
    whole = lambda a: pl.BlockSpec(a.shape, lambda i: (0,) * a.ndim)
    row = lambda n: pl.BlockSpec((1, rows, n), lambda i: (i, 0, 0))
    out = lambda n, d: jax.ShapeDtypeStruct((HALF, rows, n), d)
    return pl.pallas_call(
        functools.partial(forward_kernel, experts),
        grid=(HALF,),
        in_specs=[
            pl.BlockSpec((1, rows, width), lambda i: (part * HALF + i, 0, 0)),
            whole(dense),
            whole(tailt),
        ],
        out_specs=[row(3 * width), row(width), row(width), row(width), row(128)],
        out_shape=[out(3 * width, BF), out(width, BF), out(width, F32), out(width, BF), out(128, F32)],
        name="dense_forward",
        cost_estimate=cost(5),
        compiler_params=pltpu.CompilerParams(vmem_limit_bytes=60 << 20),
    )(tok, dense, tailt)


def packed_row(block, experts, e):
    rows, width = block.shape
    half = experts // 2
    table = block[rows - half :].astype(F32)
    side = e // half
    line = jnp.sum(jnp.where(iota(table.shape, 0) == e - side * half, table, 0.0), axis=0, keepdims=True)
    mid = width // 2
    return jnp.where(side == 0, line[:, :rows], line[:, mid : mid + rows])


def pick_rows(experts, local, slots, ei, sources, x_ref, g_ref, raw_ref, gate_ref, p_ref):
    for s, (act, dys) in enumerate(sources):
        for i in range(HALF):
            block = s * HALF + i
            at = block * slots
            rows, dyr = act[i], dys[i]
            hot, gates = [], []
            for j in range(local):
                slot = packed_row(dyr, experts, ei * local + j)
                gate = packed_row(rows, experts, ei * local + j)
                hit = iota((slots, rows.shape[0]), 0).astype(F32) == slot
                gates.append(jnp.sum(jnp.where(hit, gate, 0.0), axis=1, keepdims=True))
                hot.append(jnp.where(hit, 1.0, 0.0).astype(BF))
            hot = jnp.concatenate(hot, axis=0)
            x = dot(hot, rows, 1, 0).astype(BF)
            raw = dot(hot, dyr, 1, 0)
            if p_ref is not None:
                p_ref[block] = hot
            for j in range(local):
                cut = slice(j * slots, (j + 1) * slots)
                x_ref[j, at : at + slots, :] = x[cut]
                g_ref[j, at : at + slots, :] = (gates[j] * raw[cut]).astype(BF)
                if raw_ref is not None:
                    raw_ref[j, at : at + slots, :] = raw[cut].astype(BF)
                    gate_ref[j, at : at + slots, :] = jnp.broadcast_to(gates[j], (slots, 128))


def expert_kernel(experts, n_src, slots, chunk, ei_ref, *refs):
    acts, refs = refs[:n_src], refs[n_src:]
    dys, refs = refs[:n_src], refs[n_src:]
    wu, bu, wd, bd = refs[:4]
    out_near, out_far, x_ref, g_ref, gbu, gbd = refs[4:10]
    raw_ref, gate_ref, p_ref, resg_ref, din_ref, dg_ref = refs[10:]
    local = x_ref.shape[0]
    rows = acts[0].shape[1]
    hidden = wu.shape[2]
    ei = ei_ref[0]
    e = pl.program_id(0)

    @pl.when(e == 0)
    def _():
        pick_rows(
            experts, local, slots, ei, list(zip(acts, dys)), x_ref, g_ref, raw_ref, gate_ref, p_ref
        )

    x, g = x_ref[e], g_ref[e]
    res = din = None
    for h in range(0, hidden, chunk):
        cut = slice(h, h + chunk)
        up, down = wu[0, :, cut], wd[0, cut]
        pre = dot(x, up, 1, 0) + bu[0, :, cut].astype(F32)
        cdf, pdf = gelu_parts(pre)
        hid = (pre * cdf).astype(BF)
        dpre = (dot(g, down, 1, 1) * (cdf + pre * pdf)).astype(BF)
        gbu[0, :, cut] = jnp.sum(dpre.astype(F32), axis=0, keepdims=True)
        res_part, din_part = dot(hid, down, 1, 0), dot(dpre, up, 1, 1)
        res = res_part if res is None else res + res_part
        din = din_part if din is None else din + din_part
    gbd[0] = jnp.sum(g.astype(F32), axis=0, keepdims=True)
    res = (res + bd[0].astype(F32)).astype(BF).astype(F32)
    dg = jnp.sum(res * raw_ref[e].astype(F32), axis=1, keepdims=True)
    dg_ref[e] = jnp.broadcast_to(dg, dg_ref.shape[1:])
    resg_ref[e] = (gate_ref[e][:, 0:1] * res).astype(BF)
    din_ref[e] = din.astype(BF)

    @pl.when(e == local - 1)
    def _():
        for s in range(n_src):
            out = (out_near, out_far)[s % CORES]

            for i in range(HALF):
                block = s * HALF + i
                at = block * slots
                hot = p_ref[block]
                for kind, ref in enumerate((resg_ref, din_ref)):
                    part = jnp.concatenate([ref[j, at : at + slots, :] for j in range(local)], axis=0)
                    to = (kind * HALF + i) * rows
                    out[s // CORES, to : to + rows, :] = dot(hot, part, 0, 0).astype(BF)
                eid = iota((experts, rows), 0)
                dprob = jnp.zeros((experts, rows), F32)
                for j in range(local):
                    dg = dg_ref[j, at : at + slots, :][:, 0:1]
                    mine = hot[j * slots : (j + 1) * slots].astype(F32)
                    row = jnp.sum(mine * dg, axis=0, keepdims=True)
                    dprob = jnp.where(eid == ei * local + j, row, dprob)
                to = 2 * HALF * rows + i * experts
                out[s // CORES, to : to + experts, 0:rows] = dprob.astype(BF)


def run_experts(place, sources, w_up, b_up, w_down, b_down, experts, slots):
    local, width, hidden = w_up.shape
    n_src = len(sources)
    span = sources[0][0].shape[1]
    blocks = n_src * HALF
    rows = blocks * slots
    back = HALF * (2 * span + experts)
    flat = [s[i] for i in range(2) for s in sources]
    keep = lambda *s: pl.BlockSpec(s, lambda e, p: (0,) * len(s))
    each = lambda *s: pl.BlockSpec((1,) + s, lambda e, p: (e, 0, 0))
    return pl.pallas_call(
        functools.partial(expert_kernel, experts, n_src, slots, min(hidden, 1024)),
        grid_spec=pltpu.PrefetchScalarGridSpec(
            num_scalar_prefetch=1,
            grid=(local,),
            in_specs=[keep(HALF, span, width)] * len(flat)
            + [
                each(width, hidden),
                each(1, hidden),
                each(hidden, width),
                each(1, width),
            ],
            out_specs=[
                keep(n_src // CORES, back, width),
                keep(n_src // CORES, back, width),
                keep(local, rows, width),
                keep(local, rows, width),
                each(1, hidden),
                each(1, width),
            ],
            scratch_shapes=[
                pltpu.VMEM((local, rows, width), BF),
                pltpu.VMEM((local, rows, 128), F32),
                pltpu.VMEM((blocks, local * slots, span), BF),
                pltpu.VMEM((local, rows, width), BF),
                pltpu.VMEM((local, rows, width), BF),
                pltpu.VMEM((local, rows, 128), F32),
            ],
        ),
        out_shape=[
            jax.ShapeDtypeStruct((n_src // CORES, back, width), BF),
            jax.ShapeDtypeStruct((n_src // CORES, back, width), BF),
            jax.ShapeDtypeStruct((local, rows, width), BF),
            jax.ShapeDtypeStruct((local, rows, width), BF),
            jax.ShapeDtypeStruct((local, 1, hidden), F32),
            jax.ShapeDtypeStruct((local, 1, width), F32),
        ],
        name="experts",
        cost_estimate=cost(24),
        compiler_params=pltpu.CompilerParams(vmem_limit_bytes=60 << 20),
    )(place.ei.reshape(1), *flat, w_up, b_up, w_down, b_down)


def pick_kernel(experts, n_src, slots, ei_ref, *refs):
    x_ref, g_ref = refs[2 * n_src :]
    sources = list(zip(refs[:n_src], refs[n_src : 2 * n_src]))
    pick_rows(experts, x_ref.shape[0], slots, ei_ref[0], sources, x_ref, g_ref, None, None, None)


def run_pick(place, part, sources, local, experts, slots):
    _, span, width = sources[0][0].shape
    n_src = len(sources)
    rows = n_src * HALF * slots
    flat = [s[i] for i in range(2) for s in sources]
    half = lambda h: pl.BlockSpec((HALF, span, width), lambda i, p: (h, 0, 0))
    keep = pl.BlockSpec((local, rows, width), lambda i, p: (0, 0, 0))
    return pl.pallas_call(
        functools.partial(pick_kernel, experts, n_src, slots),
        grid_spec=pltpu.PrefetchScalarGridSpec(
            num_scalar_prefetch=1,
            grid=(1,),
            in_specs=[half(0)] * n_src + [half(part)] * n_src,
            out_specs=[keep] * 2,
        ),
        out_shape=[jax.ShapeDtypeStruct((local, rows, width), BF)] * 2,
        name="pick_rows",
        cost_estimate=cost(5),
        compiler_params=pltpu.CompilerParams(vmem_limit_bytes=60 << 20),
    )(place.ei.reshape(1), *flat)


def weight_grad_kernel(n_rows, ny, hb, own_ref, *refs):
    xs, gs = refs[:n_rows], refs[n_rows : 2 * n_rows]
    wu, bu, wd = refs[2 * n_rows : 2 * n_rows + 3]
    outs, total = refs[2 * n_rows + 3 : -1], refs[-1]
    up = down = None
    for x_ref, g_ref in zip(xs, gs):
        x, g = x_ref[0], g_ref[0]
        pre = dot(x, wu[0], 1, 0) + bu[0].astype(F32)
        cdf, pdf = gelu_parts(pre)
        hid = (pre * cdf).astype(BF)
        dpre = (dot(g, wd[0], 1, 1) * (cdf + pre * pdf)).astype(BF)
        down_part, up_part = dot(hid, g, 0, 0), dot(dpre, x, 0, 0)
        down = down_part if down is None else down + down_part
        up = up_part if up is None else up + up_part
    total[0] = up.astype(BF)
    total[1] = down.astype(BF)
    for k in range(ny):
        at = pl.multiple_of(lax.rem(own_ref[0] + k, ny) * hb, 16)
        outs[k][0] = total[:, pl.ds(at, hb), :]


def run_weight_grad(place, e, xs, gs, w_up, b_up, w_down):
    _, width, hidden = w_up.shape
    cols = hidden // place.nz
    nh, ny = place.nh, place.ny
    hb = cols // ny
    own = [place.y] + [(place.zh + k) % nh * 2 + place.zl for k in range(nh)]
    row = [pl.BlockSpec((1,) + x.shape[1:], lambda k, p: (e, 0, 0)) for x in xs]
    return pl.pallas_call(
        functools.partial(weight_grad_kernel, len(xs), ny, hb),
        grid_spec=pltpu.PrefetchScalarGridSpec(
            num_scalar_prefetch=1,
            grid=(nh,),
            in_specs=row
            + row
            + [
                pl.BlockSpec((1, width, cols), lambda k, p: (e, 0, p[k + 1])),
                pl.BlockSpec((1, 1, cols), lambda k, p: (e, 0, p[k + 1])),
                pl.BlockSpec((1, cols, width), lambda k, p: (e, p[k + 1], 0)),
            ],
            out_specs=[pl.BlockSpec((1, 2, hb, width), lambda k, p: (k, 0, 0, 0))] * ny,
            scratch_shapes=[pltpu.VMEM((2, cols, width), BF)],
        ),
        out_shape=[jax.ShapeDtypeStruct((nh, 2, hb, width), BF)] * ny,
        name="weight_grad",
        cost_estimate=cost(1),
        compiler_params=pltpu.CompilerParams(vmem_limit_bytes=60 << 20),
    )(jnp.stack(own).astype(jnp.int32), *xs, *gs, w_up, b_up, w_down)


def backward_kernel(experts, n_back, first, share, core_ref, *refs):
    tok, dy, dense, tailt, qkv, mix, resid, act_two, lse = refs[:9]
    moes, dins, dgs = [refs[9 + k * n_back : 9 + (k + 1) * n_back] for k in range(3)]
    refs = refs[9 + 3 * n_back :]
    if not first:
        before, before_t = refs[:2]
        refs = refs[2:]
    if share:
        out, gtok, keep, send, dqkv, acc, acc_t = refs
    else:
        out, gtok, acc, acc_t, dqkv = refs
    width = tok.shape[2]
    rows = tok.shape[1]
    pairs = width // (2 * HEAD)
    scale = HEAD ** (-0.5)

    @pl.when(pl.program_id(0) == 0)
    def _():
        if first:
            acc[...] = jnp.zeros_like(acc)
            acc_t[...] = jnp.zeros_like(acc_t)
        else:
            acc[:, : 4 * width] = before[...]
            acc_t[...] = before_t[...]

    total = lambda parts: functools.reduce(jnp.add, [p[...].astype(F32) for p in parts])
    tail = tailt[...]
    vec = tail.astype(F32)[experts : experts + 7]
    res = resid[0]
    out[0] = (res + total(moes)).astype(BF)
    normed_two, inv_two = norm_rows(res)
    probs = router_rows(tail, act_two[0], experts)
    dprob = total(dgs)[:, 0:rows]
    dlogit = probs * (dprob - jnp.sum(dprob * probs, axis=0, keepdims=True))
    dlogit = jnp.concatenate([dlogit, jnp.zeros((128 - experts, rows), F32)], axis=0).astype(BF)
    dact_two = total(dins) + dot(dlogit, tail, 0, 0)
    dyf = jnp.where(iota((rows, width), 0) < SEQ, dy[0].astype(F32), 0.0)
    dresid = dyf + norm_back(dact_two, normed_two, inv_two, vec[1:2])
    dattn = dresid.astype(BF)
    acc[:, 3 * width : 4 * width] += dot(mix[0], dattn, 0, 0)
    dmixed = dot(dattn, dense[:, 3 * width : 4 * width], 1, 1).astype(BF)
    seen = iota((rows, rows), 1) < SEQ
    for p in range(pairs):
        at = p * 2 * HEAD
        q = qkv[0, :, at : at + 2 * HEAD]
        k = qkv[0, :, width + at : width + at + 2 * HEAD]
        v = qkv[0, :, 2 * width + at : 2 * width + at + 2 * HEAD]
        dm = dmixed[:, at : at + 2 * HEAD]
        dq = dk = dv = None
        for side in range(2):
            q_s, dm_s = half_lanes(q, side), half_lanes(dm, side)
            scores = dot(q_s, k, 1, 1) * scale
            which = 2 * p + side
            weights = jnp.exp(jnp.where(seen, scores, LOW) - lse[0][:, which : which + 1])
            low = weights.astype(BF)
            dv_s = dot(low, dm_s, 0, 0)
            dw = dot(dm_s, v, 1, 1)
            ds = (weights * (dw - jnp.sum(dw * weights, axis=1, keepdims=True))).astype(BF)
            dq_s = dot(ds, half_lanes(k, side), 1, 0)
            dk_s = dot(ds, q_s, 0, 0)
            dq = dq_s if dq is None else dq + dq_s
            dk = dk_s if dk is None else dk + dk_s
            dv = dv_s if dv is None else dv + dv_s
        dqkv[:, at : at + 2 * HEAD] = (dq * scale).astype(BF)
        dqkv[:, width + at : width + at + 2 * HEAD] = (dk * scale).astype(BF)
        dqkv[:, 2 * width + at : 2 * width + at + 2 * HEAD] = dv.astype(BF)
    normed_one, inv_one = norm_rows(tok[0].astype(F32))
    act_one = (normed_one * vec[0:1] + vec[5:6]).astype(BF)
    acc[:, : 3 * width] += dot(act_one, dqkv[...], 0, 0)
    dact_one = dot(dqkv[...], dense[:, : 3 * width], 1, 1)
    gtok[0] = dresid + norm_back(dact_one, normed_one, inv_one, vec[0:1])
    rowsum = lambda v: jnp.sum(v.astype(F32), axis=0, keepdims=True)
    sums = [
        rowsum(dact_one * normed_one),
        rowsum(dact_two * normed_two),
        rowsum(dqkv[:, :width]),
        rowsum(dqkv[:, 2 * width :]),
        rowsum(dattn),
        rowsum(dact_one),
        rowsum(dact_two),
    ]
    acc_t[...] += dot(dlogit, act_two[0], 1, 0)
    for i, row in enumerate(sums):
        acc_t[experts + i : experts + i + 1, :] += row
    if share:

        @pl.when(pl.program_id(0) == HALF - 1)
        def _():
            last = jnp.transpose(acc_t[...], (1, 0))
            acc[:, 4 * width : 4 * width + 128] = last
            core = core_ref[0]

            def body(i, carry):
                to = pl.multiple_of(i * share, 16)
                for ref, side in ((keep, core), (send, 1 - core)):
                    at = pl.multiple_of((i * CORES + side) * share, 16)
                    ref[pl.ds(to, share), :] = acc[pl.ds(at, share), :].astype(BF)
                return carry

            lax.fori_loop(0, width // share // CORES, body, 0)


def run_backward(place, part, tok, dy, dense, tailt, saved, backs, before, experts, share):
    _, rows, width = tok.shape
    whole = lambda a: pl.BlockSpec(a.shape, lambda i, c: (0,) * len(a.shape))
    at_half = pl.BlockSpec((1, rows, width), lambda i, c: (part * HALF + i, 0, 0))
    row = lambda n: pl.BlockSpec((1, rows, n), lambda i, c: (i, 0, 0))
    first = 2 * HALF * rows // experts
    back_specs = (
        [pl.BlockSpec((rows, width), lambda i, c: (i, 0))] * len(backs)
        + [pl.BlockSpec((rows, width), lambda i, c: (HALF + i, 0))] * len(backs)
        + [pl.BlockSpec((experts, width), lambda i, c: (first + i, 0))] * len(backs)
    )
    args = [tok, dy, dense, tailt, *saved, *backs, *backs, *backs]
    specs = [at_half, at_half, whole(dense), whole(tailt)]
    specs += [row(3 * width), row(width), row(width), row(width), row(128)] + back_specs
    cols = dense.shape[1]
    scratch = [pltpu.VMEM((rows, 3 * width), BF)]
    if share:
        sums = [jax.ShapeDtypeStruct((width // CORES, cols), BF)] * 2
        scratch += [pltpu.VMEM((width, cols), F32), pltpu.VMEM((128, width), F32)]
    else:
        sums = [
            jax.ShapeDtypeStruct((width, 4 * width), F32),
            jax.ShapeDtypeStruct((128, width), F32),
        ]
    if before is not None:
        args += list(before)
        specs += [whole(b) for b in before]
    return pl.pallas_call(
        functools.partial(backward_kernel, experts, len(backs), before is None, share),
        grid_spec=pltpu.PrefetchScalarGridSpec(
            num_scalar_prefetch=1,
            grid=(HALF,),
            in_specs=specs,
            out_specs=[row(width), row(width), whole(sums[0]), whole(sums[1])],
            scratch_shapes=scratch,
        ),
        out_shape=[
            jax.ShapeDtypeStruct((HALF, rows, width), BF),
            jax.ShapeDtypeStruct((HALF, rows, width), F32),
            *sums,
        ],
        name="dense_backward",
        cost_estimate=cost(1),
        compiler_params=pltpu.CompilerParams(vmem_limit_bytes=60 << 20),
    )(place.c.reshape(1), *args)


def arrange_kernel(n, share, at_ref, near, other, dense, tailt):
    def body(i, carry):
        at = pl.multiple_of(i * share, 16)
        for k, ref in enumerate((near, other)):
            to = pl.multiple_of(at_ref[k * n + i] * share, 16)
            dense[pl.ds(to, share), :] = ref[pl.ds(at, share), :]
        return carry

    lax.fori_loop(0, n, body, 0)
    wide = dense.shape[1]
    tailt[...] = jnp.transpose(dense[:, wide - 128 :].astype(F32), (1, 0)).astype(BF)


def arrange(near, other, order, share):
    n = order.shape[0] // 2
    width, wide = 2 * near.shape[0], near.shape[1]
    vmem = pl.BlockSpec(memory_space=pltpu.VMEM)
    return pl.pallas_call(
        functools.partial(arrange_kernel, n, share),
        in_specs=[pl.BlockSpec(memory_space=pltpu.SMEM), vmem, vmem],
        out_specs=[vmem, vmem],
        out_shape=[
            jax.ShapeDtypeStruct((width, wide), BF),
            jax.ShapeDtypeStruct((128, width), BF),
        ],
        name="arrange",
        compiler_params=pltpu.CompilerParams(vmem_limit_bytes=60 << 20),
        cost_estimate=cost(3),
    )(order, near, other)


class Place:
    def __init__(self, mesh):
        self.ne = mesh.shape["expert"]
        self.nd = mesh.shape["dp"]
        self.nx = self.ne // CORES
        bits = self.nd.bit_length() - 1
        self.ny = 1 << (bits // 2)
        self.nz = self.nd // self.ny
        self.nh = self.nz // 2

    def here(self):
        ei = lax.axis_index("expert")
        di = lax.axis_index("dp")
        self.ei, self.di = ei, di
        self.x, self.c = ei // CORES, ei % CORES
        self.z, self.y = di // self.ny, di % self.ny
        self.zh, self.zl = self.z // 2, self.z % 2

    def core(self, val):
        return lax.ppermute(val, "expert", [(i, i ^ 1) for i in range(self.ne)])

    def xs(self, val, k):
        n, c = self.nx, CORES
        return lax.ppermute(val, "expert", [(i, (i // c + k) % n * c + i % c) for i in range(self.ne)])

    def ys(self, val, k):
        n = self.ny
        return lax.ppermute(val, "dp", [(i, i // n * n + (i + k) % n) for i in range(self.nd)])

    def zs(self, val, k):
        n, m = self.nz, self.ny
        return lax.ppermute(val, "dp", [(i, (i // m + k) % n * m + i % m) for i in range(self.nd)])

    def zp(self, val):
        n, m = self.nz, self.ny
        return lax.ppermute(val, "dp", [(i, (i // m ^ 1) * m + i % m) for i in range(self.nd)])

    def zhs(self, val, k):
        n, m = self.nh, self.ny
        return lax.ppermute(
            val,
            "dp",
            [(i, ((i // m // 2 + k) % n * 2 + i // m % 2) * m + i % m) for i in range(self.nd)],
        )

    def xy(self, val, kx, ky):
        def move(i):
            d, e = i // self.ne, i % self.ne
            d = d // self.ny * self.ny + (d + ky) % self.ny
            e = (e // CORES + kx) % self.nx * CORES + e % CORES
            return d * self.ne + e

        return lax.ppermute(val, ("dp", "expert"), [(i, move(i)) for i in range(self.nd * self.ne)])

    def group(self, val):
        mine = [val] + [self.xs(val, k) for k in range(1, self.nx)]
        other = [self.core(v) for v in mine]
        return [v for pair in zip(mine, other) for v in pair]


def after(val, *deps):
    return lax.optimization_barrier((val, *deps))[0]


def gather_dense(place, piece):
    share, wide = piece.shape
    nz, ny, nx = place.nz, place.ny, place.nx
    line = jnp.concatenate([piece] + [place.zs(piece, k) for k in range(1, nz)], axis=0)
    moves = [(ky, kx) for ky in range(ny) for kx in range(nx)]
    near = jnp.concatenate([line] + [place.xy(line, kx, ky) for ky, kx in moves[1:]], axis=0)
    other = place.core(near)
    order = []
    for c in (place.c, 1 - place.c):
        for ky, kx in moves:
            for kz in range(nz):
                dp = (place.z - kz) % nz * ny + (place.y - ky) % ny
                order.append(dp * place.ne + (place.x - kx) % nx * CORES + c)
    order = jnp.stack(order).astype(jnp.int32)
    if share % 16 == 0:
        return line, near, *arrange(near, other, order, share)
    full = jnp.concatenate([near, other]).reshape(-1, share, wide)
    dense = jnp.zeros_like(full).at[order].set(full).reshape(-1, wide)
    return line, near, dense, dense[:, wide - 128 :].T


def scatter_rows(place, keep, send, small, used, first, second, third):
    wide = keep.shape[1]
    add = lambda a, b: (a.astype(F32) + b.astype(F32)).astype(BF)

    def stage(v, n, own, shift, last=False):
        pick = lambda i: lax.dynamic_index_in_dim(v, i % n, 0, keepdims=False)
        total = pick(own).astype(F32)
        for k in range(1, n):
            total = total + shift(pick(own + k), k).astype(F32)
        return total if last else total.astype(BF)

    val = after(add(keep, place.core(after(send, *first))), *second)
    val = val.reshape(place.nz, place.ny, place.nx, -1, wide)
    val = stage(jnp.moveaxis(val, 2, 0), place.nx, place.x, place.xs)
    val = after(val, *third)
    val = jnp.concatenate([val[..., :used], small, val[..., used + small.shape[-1] :]], axis=-1)
    val = stage(jnp.moveaxis(val, 1, 0), place.ny, place.y, place.ys)
    return stage(val, place.nz, place.z, place.zs, last=True)


def on_device(
    place,
    tokens_in,
    grad_out,
    routes,
    norm_gains,
    biases,
    w_qkv,
    w_proj,
    w_router,
    w_up,
    b_up,
    w_down,
    b_down,
):
    place.here()
    width = tokens_in.shape[1]
    local, _, hidden = w_up.shape
    experts = local * place.ne
    cap = max(2, (2 * SEQ * 13 + 8 * experts - 1) // (8 * experts))
    slots = -(-cap // 16) * 16
    rows = -(-(SEQ + experts // 2) // 16) * 16
    hb = hidden // place.nd
    nh, ny = place.nh, place.ny
    share = w_qkv.shape[0]
    halves = range(MICRO // HALF)

    n_small = -(-local * (hb + width // place.nd) // share)
    used = experts + 7
    assert used + n_small <= 128 or share % 16
    piece = jnp.concatenate([w_qkv, w_proj, w_router, norm_gains, biases], axis=1)
    piece = jnp.pad(piece, ((0, 0), (0, 4 * width + 128 - piece.shape[1])))
    line, near, dense, tailt = gather_dense(place, piece)

    route_rows = routes.reshape(MICRO, SEQ, 2)
    names = jnp.arange(experts, dtype=jnp.int32)
    sel = jnp.any(route_rows[:, :, :, None] == names, axis=2)
    tri = (jnp.arange(SEQ)[:, None] >= jnp.arange(SEQ)[None, :]).astype(BF)
    pos = jnp.einsum("ts,bse->bet", tri, sel.astype(BF), preferred_element_type=F32)
    pos = jnp.where(sel.transpose(0, 2, 1), pos - 1, -1).astype(BF)
    pos = jnp.pad(pos, ((0, 0), (0, 0), (0, width // 2 - SEQ)), constant_values=-1)
    pos = jnp.concatenate([pos[:, : experts // 2], pos[:, experts // 2 :]], axis=2)

    blocks = lambda v: v.reshape(MICRO, SEQ, width)
    tok = jnp.pad(blocks(tokens_in), ((0, 0), (0, rows - SEQ), (0, 0)))
    gap = jnp.zeros((MICRO, rows - SEQ - experts // 2, width), BF)
    dy = jnp.concatenate([blocks(grad_out), gap, pos], axis=1)
    bu3, bd3 = b_up[:, None, :], b_down[:, None, :]
    dys = [dy[h * HALF : (h + 1) * HALF] for h in halves]
    dy_near = [place.group(dys[0])] + [place.group(after(d, near)) for d in dys[1:]]
    dy_z = place.zp(after(dy, line))

    saved, acts = [], []
    for h in halves:
        *keep, act, lse = run_forward(tok, dense, tailt, h, experts)
        saved.append((*keep, act, lse))
        acts.append(act)
    crossed = [[place.xs(act, k) for k in range(1, place.nx)] for act in acts]
    near, far = [], []
    for h in halves:
        mine = [acts[h], *crossed[h]]
        other = [place.core(after(v, acts[-1])) for v in mine]
        near.append([v for pair in zip(mine, other) for v in pair])
    for h in halves:
        far.append(place.group(after(place.zp(acts[h]), *crossed[-1])))
    dy_far = place.group(after(dy_z, *crossed[-1]))
    results, x_far, g_far = [], [], []
    for h in halves:
        src = list(zip(near[h], dy_near[h]))
        for at in range(0, len(src), 4):
            results.append(
                run_experts(place, src[at : at + 4], w_up, bu3, w_down, bd3, experts, slots)
            )
    for h in halves:
        src = list(zip(far[h], dy_far))
        for at in range(0, len(src), 4):
            x, g = run_pick(place, h, src[at : at + 4], local, experts, slots)
            x_far.append(x)
            g_far.append(g)

    xs = [r[2] for r in results] + x_far
    gs = [r[3] for r in results] + g_far
    add = lambda a, b: (a.astype(F32) + b.astype(F32)).astype(BF)

    def to_y(vals, *deps):
        mine = after(vals[0], *deps) if deps else vals[0]
        for ky in range(1, ny):
            mine = add(mine, place.ys(vals[ky], ky))
        return mine

    def to_z(mine):
        out = mine[0].astype(F32)
        for kz in range(1, nh):
            out = out + place.zhs(mine[kz], kz).astype(F32)
        return out

    part_b_up = sum(r[4] for r in results).reshape(local, place.nd, -1)
    part_b_down = sum(r[5] for r in results).reshape(local, place.nd, -1)
    small = jnp.concatenate([part_b_up, part_b_down], axis=2).transpose(1, 0, 2)
    small = small.reshape(place.nd, -1)
    small = jnp.pad(small, ((0, 0), (0, share * n_small - small.shape[1])))
    small = small.reshape(place.nz, ny, share, n_small).astype(BF)

    backs = []
    per = len(results) // len(halves)
    for h in halves:
        pair = [add(r[0], place.core(r[1])) for r in results[h * per : (h + 1) * per]]
        pair = [p[k] for p in pair for k in range(p.shape[0])]
        backs.append([pair[0]] + [place.xs(pair[k], place.nx - k) for k in range(1, place.nx)])

    sums = None
    outs, gtoks, sent, summed = [], [], [], []

    def weights(e, *deps):
        if e >= local:
            return
        first = after(xs[0], *deps) if deps else xs[0]
        sent.append(run_weight_grad(place, e, [first, *xs[1:]], gs, w_up, bu3, w_down))

    def tokens_back(h, *deps):
        nonlocal sums
        last = share if h == len(halves) - 1 and share % 16 == 0 else 0
        grads = after(dy, *deps)
        out, gtok, *sums = run_backward(
            place, h, tok, grads, dense, tailt, saved[h], backs[h], sums, experts, last
        )
        outs.append(out)
        gtoks.append(gtok)

    weights(0)
    weights(1, sent[0][0])
    tokens_back(0, sent[1][0])
    summed.append(to_y(sent[0], gtoks[0]))
    weights(2, gtoks[0], summed[0])
    weights(3, sent[2][0])
    summed.append(to_y(sent[1], sent[3][0]))
    both = [to_z(summed[0])]
    tokens_back(1, sent[3][0], summed[1], both[0])
    summed.append(to_y(sent[2], gtoks[1]))
    summed.append(to_y(sent[3], summed[2]))
    both += [to_z(v) for v in summed[1:]]
    grad_up = jnp.stack([b[0].T for b in both])
    grad_down = jnp.stack([b[1] for b in both])
    tokens = lambda v: jnp.concatenate(v, axis=0)[:, :SEQ].reshape(-1, width)
    if share % 16:
        full = jnp.concatenate([sums[0], sums[1].T], axis=1).astype(BF)
        full = jnp.moveaxis(full.reshape(-1, CORES, share, full.shape[1]), 1, 0)
        side = lambda c: lax.dynamic_index_in_dim(full, c, 0, keepdims=False)
        sums = [side(c).reshape(-1, full.shape[3]) for c in (place.c, 1 - place.c)]
    if used + n_small > 128:
        sums = [jnp.pad(v, ((0, 0), (0, used + n_small - 128))) for v in sums]
    waits = [summed[2]], [summed[3], both[1]], [both[2]]
    grads = scatter_rows(place, *sums, small, 4 * width + used, *waits)
    tiny = grads[:, 4 * width + used : 4 * width + used + n_small].reshape(-1)
    tiny = tiny[: local * (hb + width // place.nd)].reshape(local, -1)
    grad_b_up, grad_b_down = tiny[:, :hb], tiny[:, hb:]
    at = 4 * width
    return (
        tokens(outs),
        tokens(gtoks),
        grads[:, at + experts : at + experts + 2],
        grads[:, at + experts + 2 : at + experts + 7],
        grads[:, : 3 * width],
        grads[:, 3 * width : at],
        grads[:, at : at + experts],
        grad_up,
        grad_b_up,
        grad_down,
        grad_b_down,
    )


def solution(mesh):
    place = Place(mesh)
    tok = P(("dp", "expert"), None)
    in_specs = (tok,) * 8 + (
        P("expert", None, None),
        P("expert", None),
        P("expert", None, None),
        P("expert", None),
    )
    out_specs = (tok,) * 7 + (
        P("expert", None, "dp"),
        P("expert", "dp"),
        P("expert", "dp", None),
        P("expert", "dp"),
    )

    def run(*args):
        return on_device(place, *args)

    return jax.shard_map(run, mesh=mesh, in_specs=in_specs, out_specs=out_specs, check_vma=False)
```

time: 566 us -> 343 us (0.61); the launches traced: 555 us -> 340 us
  matrix products: 241 us -> 0.18 us
  Pallas kernels: 0 us -> 157 us
  local copies, waits for them, and re-layouts: 85.4 us -> 32.4 us
  waiting for transfers between devices: 139 us -> 90.5 us
  other arithmetic: 43.7 us -> 17.6 us
    dot_general x63 -> x1, matrix products: 240 us -> 0.18 us  [on_device(): jnp.einsum('ts,bse->bet', tri, sel.astype(BF), preferred_element_type=F32)]
    pallas_call x0 -> x13, Pallas kernels: none -> 157 us  [the longest x4 51.1 us: run_weight_grad(): pl.pallas_call(functools.partial(weight_grad_kernel, len(xs), ny, hb), gr...]
    ppermute x2 -> x4, waiting for transfers between devices: 70.8 us -> 32 us  [zhs(): lax.ppermute(val, 'dp', [(i, ((i // m // 2 + k) % n * 2 + i // m % 2) * m...]
    ppermute x11 -> x10, waiting for transfers between devices: 58.5 us -> 23.1 us  [xs(): lax.ppermute(val, 'expert', [(i, (i // c + k) % n * c + i % c) for i in r...]
    convert_element_type x25 -> x3, local copies, waits for them, and re-layouts: 17.8 us -> 0.11 us  [on_device(): small = small.reshape(place.nz, ny, share, n_small).astype(BF)]
    unnamed x175 -> x93, local copies, waits for them, and re-layouts: 28.3 us -> 12 us
    reduce_sum x22 -> x0, other arithmetic: 13.3 us -> none  [the longest x1 2.75 us: on_device(): jnp.sum(dattn.astype(F32), axis=(0, 1))]
    ppermute x0 -> x3, waiting for transfers between devices: none -> 10.1 us  [xy(): lax.ppermute(val, ('dp', 'expert'), [(i, move(i)) for i in range(self.nd...]
  transfers between devices with their start and end apart: 52 -> 49, of which waited for: 13 -> 15; matrix products, arithmetic and copies ran while one was open for 65% -> 11% of each run, Pallas kernels for 0% -> 46%
where the time goes in v2:
time: 343 us; the launch traced here: 340 us
  Pallas kernels  157 us (46%)
  waiting for transfers between devices  90.5 us (26%)
  starting transfers between devices  40.1 us (12%)
  local copies, waits for them, and re-layouts  32.4 us (9%)
  other arithmetic  17.6 us (5%)
    pallas_call x4, Pallas kernels, run_weight_grad(): pl.pallas_call(functools.partial(weight_grad_kernel, len(xs), ny, hb), gr...  51.1 us
    pallas_call x2, Pallas kernels, run_experts(): pl.pallas_call(functools.partial(expert_kernel, experts, n_src, slots, mi...  47.9 us
    ppermute x4, waiting for transfers between devices, zhs(): lax.ppermute(val, 'dp', [(i, ((i // m // 2 + k) % n * 2 + i // m % 2) * m...  32 us
    pallas_call x2, Pallas kernels, run_backward(): pl.pallas_call(functools.partial(backward_kernel, experts, len(backs), be...  30.6 us
    ppermute x10, waiting for transfers between devices, xs(): lax.ppermute(val, 'expert', [(i, (i // c + k) % n * c + i % c) for i in r...  23.1 us
    ppermute x5, waiting for transfers between devices, ys(): lax.ppermute(val, 'dp', [(i, i // n * n + (i + k) % n) for i in range(sel...  16.4 us
    pallas_call x2, Pallas kernels, run_forward(): pl.pallas_call(functools.partial(forward_kernel, experts), grid=(HALF,),...  14.8 us
    unnamed x93, local copies, waits for them, and re-layouts  12 us
  transfers between devices with their start and end apart: 49, of which 15 were waited for; matrix products, arithmetic and copies ran while one was open for 11% of the time, Pallas kernels for 46%

profile of v2, /device:TPU:0, one launch (start us, length us, event | category | flops | bytes accessed | tf_op | source)
XLA Modules:
  0.0 339.5 jit_solution(13731150166016241303)
XLA Ops:
  3.8 5.0 %collective-permute-start.2 = (bf16[16,2176]{1,0:T(8,128)(2,1)S(1)}, bf16[16,2176]{1,0:T(8,128)(2,1)S(1)}, u32[]{:S(2)}, u32[]{:S(2)}) collective-permute-start(bf16[16,2176]{1,0:T(8,128)(2,1)S(1)} %get-tuple-element.193), channel_id=1, source_target_pairs={{0,24},{4,28},{8,0},{12,4},{16,8},{20,12},{24,16},{28,20},{1,25},{... | collective-permute-start | bytes 208904 | tf_op jit(solution)/shard_map/ppermute | solution.py:576
  11.4 4.2 %collective-permute-done.1 = bf16[16,2176]{1,0:T(8,128)(2,1)S(1)} collective-permute-done((bf16[16,2176]{1,0:T(8,128)(2,1)S(1)}, bf16[16,2176]{1,0:T(8,128)(2,1)S(1)}, u32[]{:S(2)}, u32[]{:S(2)}) %collective-permute-start.1) | collective-permute-done | bytes 69664 | tf_op jit(solution)/shard_map/ppermute | solution.py:576
  15.7 2.5 collective-permute-start.5
  21.1 10.1 %collective-permute-done.3 = bf16[64,2176]{1,0:T(8,128)(2,1)S(1)} collective-permute-done((bf16[64,2176]{1,0:T(8,128)(2,1)S(1)}, bf16[64,2176]{1,0:T(8,128)(2,1)S(1)}, u32[]{:S(2)}, u32[]{:S(2)}) %collective-permute-start.3) | collective-permute-done | bytes 278560 | tf_op jit(solution)/shard_map/ppermute | solution.py:597
  38.1 3.8 %arrange.1 = (bf16[512,2176]{1,0:T(8,128)(2,1)}, bf16[128,512]{1,0:T(8,128)(2,1)}) custom-call(s32[32]{0:T(128)} %stack.177.at_ref, bf16[256,2176]{1,0:T(8,128)(2,1)} %constant_dynamic-update-slice_fusion.near, bf16[256,2176]{1,0:T(8,128)(2,1)} %collective-permute-done.6.other), custom_call_target="tpu_custom_call" | custom-call | flops 1050000000 | bytes 1048576 | tf_op jit(solution)/shard_map/arrange/pallas_call | solution.py:531
  41.9 7.4 %dense_forward.2 = (bf16[2,208,1536]{2,1,0:T(8,128)(2,1)}, bf16[2,208,512]{2,1,0:T(8,128)(2,1)}, f32[2,208,512]{2,1,0:T(8,128)}, bf16[2,208,512]{2,1,0:T(8,128)(2,1)}, f32[2,208,128]{2,1,0:T(8,128)}) custom-call(bf16[4,208,512]{2,1,0:T(8,128)(2,1)} %pad.12.tok.refs_0_, bf16[512,2176]{1,0:T(8,128)(2,1)} %get-tuple-element.76.dense.refs_2_, ...), custom_call_target="tpu_custom_call" | custom-call | flops 1750000000 | bytes 1048576 | tf_op jit(solution)/shard_map/dense_forward/pallas_call | solution.py:119
  51.4 7.4 %dense_forward.3 = (bf16[2,208,1536]{2,1,0:T(8,128)(2,1)}, bf16[2,208,512]{2,1,0:T(8,128)(2,1)}, f32[2,208,512]{2,1,0:T(8,128)}, bf16[2,208,512]{2,1,0:T(8,128)(2,1)}, f32[2,208,128]{2,1,0:T(8,128)}) custom-call(bf16[4,208,512]{2,1,0:T(8,128)(2,1)} %pad.12.tok.refs_0_, bf16[512,2176]{1,0:T(8,128)(2,1)} %get-tuple-element.76.dense.refs_2_, ...), custom_call_target="tpu_custom_call" | custom-call | flops 1750000000 | bytes 1048576 | tf_op jit(solution)/shard_map/dense_forward/pallas_call | solution.py:119
  58.8 2.1 collective-permute-start.27
  62.7 8.6 %collective-permute-done.17.refs_6_ = bf16[2,208,512]{2,1,0:T(8,128)(2,1)S(1)} collective-permute-done((bf16[2,208,512]{2,1,0:T(8,128)(2,1)S(1)}, bf16[2,208,512]{2,1,0:T(8,128)(2,1)S(1)}, u32[]{:S(2)}, u32[]{:S(2)}) %collective-permute-start.17) | collective-permute-done | bytes 426016 | tf_op jit(solution)/shard_map/ppermute | solution.py:568
  72.4 7.5 %collective-permute-done.14.refs_2_ = bf16[2,208,512]{2,1,0:T(8,128)(2,1)} collective-permute-done((bf16[2,208,512]{2,1,0:T(8,128)(2,1)}, bf16[2,208,512]{2,1,0:T(8,128)(2,1)}, u32[]{:S(2)}, u32[]{:S(2)}) %collective-permute-start.14) | collective-permute-done | bytes 426016 | tf_op jit(solution)/shard_map/ppermute | solution.py:568
  85.8 23.7 %experts.2 = (bf16[2,864,512]{2,1,0:T(8,128)(2,1)}, bf16[2,864,512]{2,1,0:T(8,128)(2,1)}, bf16[4,384,512]{2,1,0:T(8,128)(2,1)}, bf16[4,384,512]{2,1,0:T(8,128)(2...) custom-call(s32[1]{0:T(128)} %bitcast.6.ei_ref, bf16[2,208,512]{2,1,0:T(8,128)(2,1)} %get-tuple-element.80.refs_0_.refs_7_, ...), custom_call_target="tpu_custom_call" | custom-call | flops 8400000000 | bytes 1048576 | tf_op jit(solution)/shard_map/experts/pallas_call | solution.py:244
  110.9 2.8 collective-permute-done.25.refs_6_
  113.7 24.1 %experts.3 = (bf16[2,864,512]{2,1,0:T(8,128)(2,1)}, bf16[2,864,512]{2,1,0:T(8,128)(2,1)}, bf16[4,384,512]{2,1,0:T(8,128)(2,1)}, bf16[4,384,512]{2,1,0:T(8,128)(2...) custom-call(s32[1]{0:T(128)} %bitcast.6.ei_ref, bf16[2,208,512]{2,1,0:T(8,128)(2,1)} %get-tuple-element.83.refs_0_.refs_7_, ...), custom_call_target="tpu_custom_call" | custom-call | flops 8400000000 | bytes 1048576 | tf_op jit(solution)/shard_map/experts/pallas_call | solution.py:244
  140.7 4.5 %pick_rows.3 = (bf16[4,384,512]{2,1,0:T(8,128)(2,1)}, bf16[4,384,512]{2,1,0:T(8,128)(2,1)}) custom-call(s32[1]{0:T(128)} %bitcast.6.ei_ref, bf16[2,208,512]{2,1,0:T(8,128)(2,1)} %collective-permute-done.27.refs_0_, bf16[2,208,512]{2,1,0:T(8,128)(2,1)} %collective-permute-done.28.refs_1_, bf16[2,208,512]{2,1,0:T(8,128)(2,1)} %collective-permute-done.29.refs_2_, ...), custom_call_target="tpu_custom_call" | custom-call | flops 1750000000 | bytes 1048576 | tf_op jit(solution)/shard_map/pick_rows/pallas_call | solution.py:300
  145.3 4.5 %pick_rows.2 = (bf16[4,384,512]{2,1,0:T(8,128)(2,1)}, bf16[4,384,512]{2,1,0:T(8,128)(2,1)}) custom-call(s32[1]{0:T(128)} %bitcast.6.ei_ref, bf16[2,208,512]{2,1,0:T(8,128)(2,1)} %copy-done.32, bf16[2,208,512]{2,1,0:T(8,128)(2,1)} %collective-permute-done.20.refs_1_, bf16[2,208,512]{2,1,0:T(8,128)(2,1)} %collective-permute-done.21.refs_2_, ...), custom_call_target="tpu_custom_call" | custom-call | flops 1750000000 | bytes 1048576 | tf_op jit(solution)/shard_map/pick_rows/pallas_call | solution.py:300
  149.8 12.8 %weight_grad.4 = (bf16[2,2,256,512]{3,2,1,0:T(8,128)(2,1)}, bf16[2,2,256,512]{3,2,1,0:T(8,128)(2,1)}) custom-call(s32[3]{0:T(128)} %pad_add_fusion.own_ref, bf16[4,384,512]{2,1,0:T(8,128)(2,1)} %get-tuple-element.113.refs_0_, bf16[4,384,512]{2,1,0:T(8,128)(2,1)} %get-tuple-element.86.refs_1_, bf16[4,384,512]{2,1,0:T(8,128)(2,1)} %get-tuple-element.90.refs_2_, ...), custom_call_target="tpu_custom_call" | custom-call | flops 350000000 | bytes 1048576 | tf_op jit(solution)/shard_map/weight_grad/pallas_call | solution.py:343
  166.0 12.7 %weight_grad.5 = (bf16[2,2,256,512]{3,2,1,0:T(8,128)(2,1)}, bf16[2,2,256,512]{3,2,1,0:T(8,128)(2,1)}) custom-call(s32[3]{0:T(128)} %pad_add_fusion.own_ref, bf16[4,384,512]{2,1,0:T(8,128)(2,1)} %get-tuple-element.113.refs_0_, bf16[4,384,512]{2,1,0:T(8,128)(2,1)} %get-tuple-element.86.refs_1_, bf16[4,384,512]{2,1,0:T(8,128)(2,1)} %get-tuple-element.90.refs_2_, ...), custom_call_target="tpu_custom_call" | custom-call | flops 350000000 | bytes 1048576 | tf_op jit(solution)/shard_map/weight_grad/pallas_call | solution.py:343
  180.2 2.0 add_convert_fusion
  184.9 2.8 collective-permute-done.32.refs_10_.refs_12_.refs_14_
  188.7 14.4 %dense_backward.2 = (bf16[2,208,512]{2,1,0:T(8,128)(2,1)}, f32[2,208,512]{2,1,0:T(8,128)}, f32[512,2048]{1,0:T(8,128)}, f32[128,512]{1,0:T(8,128)}) custom-call(s32[1]{0:T(128)} %bitcast.core_ref, bf16[4,208,512]{2,1,0:T(8,128)(2,1)} %pad.12.tok.refs_0_, bf16[4,208,512]{2,1,0:T(8,128)(2,1)} %copy-done, bf16[512,2176]{1,0:T(8,128)(2,1)} %get-tuple-element.76.dense.refs_2_, ...), custom_call_target="tpu_custom_call" | custom-call | flops 350000000 | bytes 1048576 | tf_op jit(solution)/shard_map/dense_backward/pallas_call | solution.py:494
  206.7 12.9 %weight_grad.6 = (bf16[2,2,256,512]{3,2,1,0:T(8,128)(2,1)}, bf16[2,2,256,512]{3,2,1,0:T(8,128)(2,1)}) custom-call(s32[3]{0:T(128)} %pad_add_fusion.own_ref, bf16[4,384,512]{2,1,0:T(8,128)(2,1)} %get-tuple-element.113.refs_0_, bf16[4,384,512]{2,1,0:T(8,128)(2,1)} %get-tuple-element.86.refs_1_, bf16[4,384,512]{2,1,0:T(8,128)(2,1)} %get-tuple-element.90.refs_2_, ...), custom_call_target="tpu_custom_call" | custom-call | flops 350000000 | bytes 1048576 | tf_op jit(solution)/shard_map/weight_grad/pallas_call | solution.py:343
  219.6 12.7 %weight_grad.7 = (bf16[2,2,256,512]{3,2,1,0:T(8,128)(2,1)}, bf16[2,2,256,512]{3,2,1,0:T(8,128)(2,1)}) custom-call(s32[3]{0:T(128)} %pad_add_fusion.own_ref, bf16[4,384,512]{2,1,0:T(8,128)(2,1)} %get-tuple-element.113.refs_0_, bf16[4,384,512]{2,1,0:T(8,128)(2,1)} %get-tuple-element.86.refs_1_, bf16[4,384,512]{2,1,0:T(8,128)(2,1)} %get-tuple-element.90.refs_2_, ...), custom_call_target="tpu_custom_call" | custom-call | flops 350000000 | bytes 1048576 | tf_op jit(solution)/shard_map/weight_grad/pallas_call | solution.py:343
  237.6 2.2 convert_add_fusion.4
  240.7 16.2 %dense_backward.3 = (bf16[2,208,512]{2,1,0:T(8,128)(2,1)}, f32[2,208,512]{2,1,0:T(8,128)}, bf16[256,2176]{1,0:T(8,128)(2,1)}, bf16[256,2176]{1,0:T(8,128)(2,1)}) custom-call(s32[1]{0:T(128)} %bitcast.core_ref, bf16[4,208,512]{2,1,0:T(8,128)(2,1)} %pad.12.tok.refs_0_, bf16[4,208,512]{2,1,0:T(8,128)(2,1)} %copy-done, ...), custom_call_target="tpu_custom_call" | custom-call | flops 350000000 | bytes 1048576 | tf_op jit(solution)/shard_map/dense_backward/pallas_call | solution.py:494
  265.9 2.1 fusion.10
  268.1 10.4 %collective-permute-done.40 = bf16[2,2,256,512]{3,2,1,0:T(8,128)(2,1)} collective-permute-done((bf16[2,2,256,512]{3,2,1,0:T(8,128)(2,1)}, bf16[2,2,256,512]{3,2,1,0:T(8,128)(2,1)}, u32[]{:S(2)}, u32[]{:S(2)}) %collective-permute-start.40) | collective-permute-done | bytes 1048608 | tf_op jit(solution)/shard_map/ppermute | solution.py:572
  284.3 20.6 %collective-permute-done.43 = bf16[2,256,512]{2,1,0:T(8,128)(2,1)S(1)} collective-permute-done((bf16[2,256,512]{2,1,0:T(8,128)(2,1)S(1)}, bf16[2,256,512]{2,1,0:T(8,128)(2,1)S(1)}, u32[]{:S(2)}, u32[]{:S(2)}) %collective-permute-start.43) | collective-permute-done | bytes 524320 | tf_op jit(solution)/shard_map/ppermute | solution.py:584
  306.0 10.0 %collective-permute-done.48 = bf16[2,256,512]{2,1,0:T(8,128)(2,1)S(1)} collective-permute-done((bf16[2,256,512]{2,1,0:T(8,128)(2,1)S(1)}, bf16[2,256,512]{2,1,0:T(8,128)(2,1)S(1)}, u32[]{:S(2)}, u32[]{:S(2)}) %collective-permute-start.48) | collective-permute-done | bytes 524320 | tf_op jit(solution)/shard_map/ppermute | solution.py:584
  319.5 6.0 %collective-permute-done.44 = bf16[4,16,2176]{2,1,0:T(8,128)(2,1)S(1)} collective-permute-done((bf16[4,16,2176]{2,1,0:T(8,128)(2,1)S(1)}, bf16[4,16,2176]{2,1,0:T(8,128)(2,1)S(1)}, u32[]{:S(2)}, u32[]{:S(2)}) %collective-permute-start.44) | collective-permute-done | bytes 278560 | tf_op jit(solution)/shard_map/ppermute | solution.py:572
  325.7 3.8 %collective-permute-start.47 = (bf16[16,2176]{1,0:T(8,128)(2,1)S(1)}, bf16[16,2176]{1,0:T(8,128)(2,1)S(1)}, u32[]{:S(2)}, u32[]{:S(2)}) collective-permute-start(bf16[16,2176]{1,0:T(8,128)(2,1)S(1)} %get-tuple-element.191), channel_id=1, source_target_pairs={{0,24},{4,28},{8,0},{12,4},{16,8},{20,12},{24,16},{28,20},{1,25},{... | collective-permute-start | bytes 208904 | tf_op jit(solution)/shard_map/ppermute | solution.py:576
  329.7 1.8 copy.66
  332.3 2.4 collective-permute-done.46
  (244 shorter events, 73.9 us)
Async XLA Ops:
  15.7 17.0 %collective-permute-start.5 = (bf16[64,2176]{1,0:T(8,128)(2,1)S(1)}, bf16[64,2176]{1,0:T(8,128)(2,1)S(1)}, u32[]{:S(2)}, u32[]{:S(2)}) collective-permute-start(bf16[64,2176]{1,0:T(8,128)(2,1)S(1)} %pad_maximum_fusion.4), channel_id=1, source_target_pairs={{0,6},{1,7},{2,4},{3,5},{4,2},{5,3},{6,0},{7,1},{8,14},{9,15},{10,... | collective-permute-start | bytes 835592 | tf_op jit(solution)/shard_map/ppermute | solution.py:597
  18.2 13.8 %collective-permute-start.4 = (bf16[64,2176]{1,0:T(8,128)(2,1)S(1)}, bf16[64,2176]{1,0:T(8,128)(2,1)S(1)}, u32[]{:S(2)}, u32[]{:S(2)}) collective-permute-start(bf16[64,2176]{1,0:T(8,128)(2,1)S(1)} %pad_maximum_fusion.4), channel_id=1, source_target_pairs={{0,4},{1,5},{2,6},{3,7},{4,0},{5,1},{6,2},{7,3},{8,12},{9,13},{10,... | collective-permute-start | bytes 835592 | tf_op jit(solution)/shard_map/ppermute | solution.py:597
  34.4 17.0 %collective-permute-start.11 = (bf16[2,208,512]{2,1,0:T(8,128)(2,1)S(1)}, bf16[2,208,512]{2,1,0:T(8,128)(2,1)}, u32[]{:S(2)}, u32[]{:S(2)}) collective-permute-start(bf16[2,208,512]{2,1,0:T(8,128)(2,1)S(1)} %get-tuple-element.189.refs_4_), channel_id=1, source_target_pairs={{0,2},{1,3},{2,0},{3,1},{4,6},{5,7},{6,4},{7,5},{8,10},{9,11},{10,... | collective-permute-start | bytes 1277960 | tf_op jit(solution)/shard_map/ppermute | solution.py:568
  35.9 22.8 %collective-permute-start.10 = (bf16[2,208,512]{2,1,0:T(8,128)(2,1)S(1)}, bf16[2,208,512]{2,1,0:T(8,128)(2,1)}, u32[]{:S(2)}, u32[]{:S(2)}) collective-permute-start(bf16[2,208,512]{2,1,0:T(8,128)(2,1)S(1)} %get-tuple-element.189.refs_4_), channel_id=1, source_target_pairs={{0,1},{1,0},{2,3},{3,2},{4,5},{5,4},{6,7},{7,6},{8,9},{9,8},{10,11... | collective-permute-start | bytes 1277960 | tf_op jit(solution)/shard_map/ppermute | solution.py:564
  38.1 33.8 %collective-permute-start.23 = (bf16[4,208,512]{2,1,0:T(8,128)(2,1)S(1)}, bf16[4,208,512]{2,1,0:T(8,128)(2,1)}, u32[]{:S(2)}, u32[]{:S(2)}) collective-permute-start(bf16[4,208,512]{2,1,0:T(8,128)(2,1)S(1)} %maximum_maximum_fusion.refs_1_), channel_id=1, source_target_pairs={{0,8},{4,12},{8,0},{12,4},{16,24},{20,28},{24,16},{28,20},{1,9},{5... | collective-permute-start | bytes 2555912 | tf_op jit(solution)/shard_map/ppermute | solution.py:580
  49.9 21.4 %collective-permute-start.17 = (bf16[2,208,512]{2,1,0:T(8,128)(2,1)S(1)}, bf16[2,208,512]{2,1,0:T(8,128)(2,1)S(1)}, u32[]{:S(2)}, u32[]{:S(2)}) collective-permute-start(bf16[2,208,512]{2,1,0:T(8,128)(2,1)S(1)} %get-tuple-element.85.refs_4_), channel_id=1, source_target_pairs={{0,2},{1,3},{2,0},{3,1},{4,6},{5,7},{6,4},{7,5},{8,10},{9,11},{10,... | collective-permute-start | bytes 1277960 | tf_op jit(solution)/shard_map/ppermute | solution.py:568
  51.4 20.0 %collective-permute-start.16 = (bf16[2,208,512]{2,1,0:T(8,128)(2,1)S(1)}, bf16[2,208,512]{2,1,0:T(8,128)(2,1)S(1)}, u32[]{:S(2)}, u32[]{:S(2)}) collective-permute-start(bf16[2,208,512]{2,1,0:T(8,128)(2,1)S(1)} %get-tuple-element.85.refs_4_), channel_id=1, source_target_pairs={{0,1},{1,0},{2,3},{3,2},{4,5},{5,4},{6,7},{7,6},{8,9},{9,8},{10,11... | collective-permute-start | bytes 1277960 | tf_op jit(solution)/shard_map/ppermute | solution.py:564
  58.8 13.2 %collective-permute-start.27 = (bf16[2,208,512]{2,1,0:T(8,128)(2,1)}, bf16[2,208,512]{2,1,0:T(8,128)(2,1)}, u32[]{:S(2)}, u32[]{:S(2)}) collective-permute-start(bf16[2,208,512]{2,1,0:T(8,128)(2,1)} %get-tuple-element.83.refs_0_.refs_7_), channel_id=1, source_target_pairs={{0,8},{4,12},{8,0},{12,4},{16,24},{20,28},{24,16},{28,20},{1,9},{5... | collective-permute-start | bytes 1277960 | tf_op jit(solution)/shard_map/ppermute | solution.py:580
  62.2 17.7 %collective-permute-start.14 = (bf16[2,208,512]{2,1,0:T(8,128)(2,1)}, bf16[2,208,512]{2,1,0:T(8,128)(2,1)}, u32[]{:S(2)}, u32[]{:S(2)}) collective-permute-start(bf16[2,208,512]{2,1,0:T(8,128)(2,1)} %get-tuple-element.83.refs_0_.refs_7_), channel_id=1, source_target_pairs={{0,2},{1,3},{2,0},{3,1},{4,6},{5,7},{6,4},{7,5},{8,10},{9,11},{10,... | collective-permute-start | bytes 1277960 | tf_op jit(solution)/shard_map/ppermute | solution.py:568
  81.2 28.4 %collective-permute-start.19 = (bf16[2,208,512]{2,1,0:T(8,128)(2,1)S(1)}, bf16[2,208,512]{2,1,0:T(8,128)(2,1)S(1)}, u32[]{:S(2)}, u32[]{:S(2)}) collective-permute-start(bf16[2,208,512]{2,1,0:T(8,128)(2,1)S(1)} %copy-done.24), channel_id=1, source_target_pairs={{0,8},{4,12},{8,0},{12,4},{16,24},{20,28},{24,16},{28,20},{1,9},{5... | collective-permute-start | bytes 1277960 | tf_op jit(solution)/shard_map/ppermute | solution.py:580
  82.9 27.2 %collective-permute-start.29 = (bf16[2,208,512]{2,1,0:T(8,128)(2,1)}, bf16[2,208,512]{2,1,0:T(8,128)(2,1)}, u32[]{:S(2)}, u32[]{:S(2)}) collective-permute-start(bf16[2,208,512]{2,1,0:T(8,128)(2,1)} %collective-permute-done.27.refs_0_), channel_id=1, source_target_pairs={{0,2},{1,3},{2,0},{3,1},{4,6},{5,7},{6,4},{7,5},{8,10},{9,11},{10,... | collective-permute-start | bytes 1277960 | tf_op jit(solution)/shard_map/ppermute | solution.py:568
  83.7 27.2 %collective-permute-start.28 = (bf16[2,208,512]{2,1,0:T(8,128)(2,1)}, bf16[2,208,512]{2,1,0:T(8,128)(2,1)}, u32[]{:S(2)}, u32[]{:S(2)}) collective-permute-start(bf16[2,208,512]{2,1,0:T(8,128)(2,1)} %collective-permute-done.27.refs_0_), channel_id=1, source_target_pairs={{0,1},{1,0},{2,3},{3,2},{4,5},{5,4},{6,7},{7,6},{8,9},{9,8},{10,11... | collective-permute-start | bytes 1277960 | tf_op jit(solution)/shard_map/ppermute | solution.py:564
  83.7 26.1 %collective-permute-start.15 = (bf16[2,208,512]{2,1,0:T(8,128)(2,1)}, bf16[2,208,512]{2,1,0:T(8,128)(2,1)}, u32[]{:S(2)}, u32[]{:S(2)}) collective-permute-start(bf16[2,208,512]{2,1,0:T(8,128)(2,1)} %collective-permute-done.14.refs_2_), channel_id=1, source_target_pairs={{0,1},{1,0},{2,3},{3,2},{4,5},{5,4},{6,7},{7,6},{8,9},{9,8},{10,11... | collective-permute-start | bytes 1277960 | tf_op jit(solution)/shard_map/ppermute | solution.py:564
  84.5 29.2 %collective-permute-start.25 = (bf16[4,208,512]{2,1,0:T(8,128)(2,1)}, bf16[4,208,512]{2,1,0:T(8,128)(2,1)S(1)}, u32[]{:S(2)}, u32[]{:S(2)}) collective-permute-start(bf16[4,208,512]{2,1,0:T(8,128)(2,1)} %collective-permute-done.23.refs_4_), channel_id=1, source_target_pairs={{0,2},{1,3},{2,0},{3,1},{4,6},{5,7},{6,4},{7,5},{8,10},{9,11},{10,... | collective-permute-start | bytes 2555912 | tf_op jit(solution)/shard_map/ppermute | solution.py:568
  109.6 53.6 %collective-permute-start.31 = (bf16[2,864,512]{2,1,0:T(8,128)(2,1)}, bf16[2,864,512]{2,1,0:T(8,128)(2,1)S(1)}, u32[]{:S(2)}, u32[]{:S(2)}) collective-permute-start(bf16[2,864,512]{2,1,0:T(8,128)(2,1)} %get-tuple-element.106), channel_id=1, source_target_pairs={{0,1},{1,0},{2,3},{3,2},{4,5},{5,4},{6,7},{7,6},{8,9},{9,8},{10,11... | collective-permute-start | bytes 5308424 | tf_op jit(solution)/shard_map/ppermute | solution.py:564
  109.8 29.3 %collective-permute-start.24 = (bf16[4,208,512]{2,1,0:T(8,128)(2,1)}, bf16[4,208,512]{2,1,0:T(8,128)(2,1)}, u32[]{:S(2)}, u32[]{:S(2)}) collective-permute-start(bf16[4,208,512]{2,1,0:T(8,128)(2,1)} %collective-permute-done.23.refs_4_), channel_id=1, source_target_pairs={{0,1},{1,0},{2,3},{3,2},{4,5},{5,4},{6,7},{7,6},{8,9},{9,8},{10,11... | collective-permute-start | bytes 2555912 | tf_op jit(solution)/shard_map/ppermute | solution.py:564
  110.2 27.7 %collective-permute-start.21 = (bf16[2,208,512]{2,1,0:T(8,128)(2,1)S(1)}, bf16[2,208,512]{2,1,0:T(8,128)(2,1)}, u32[]{:S(2)}, u32[]{:S(2)}) collective-permute-start(bf16[2,208,512]{2,1,0:T(8,128)(2,1)S(1)} %collective-permute-done.19.refs_0_), channel_id=1, source_target_pairs={{0,2},{1,3},{2,0},{3,1},{4,6},{5,7},{6,4},{7,5},{8,10},{9,11},{10,... | collective-permute-start | bytes 1277960 | tf_op jit(solution)/shard_map/ppermute | solution.py:568
  110.9 27.4 %collective-permute-start.30 = (bf16[2,208,512]{2,1,0:T(8,128)(2,1)}, bf16[2,208,512]{2,1,0:T(8,128)(2,1)S(1)}, u32[]{:S(2)}, u32[]{:S(2)}) collective-permute-start(bf16[2,208,512]{2,1,0:T(8,128)(2,1)} %collective-permute-done.29.refs_2_), channel_id=1, source_target_pairs={{0,1},{1,0},{2,3},{3,2},{4,5},{5,4},{6,7},{7,6},{8,9},{9,8},{10,11... | collective-permute-start | bytes 1277960 | tf_op jit(solution)/shard_map/ppermute | solution.py:564
  113.7 27.0 %collective-permute-start.26 = (bf16[4,208,512]{2,1,0:T(8,128)(2,1)S(1)}, bf16[4,208,512]{2,1,0:T(8,128)(2,1)}, u32[]{:S(2)}, u32[]{:S(2)}) collective-permute-start(bf16[4,208,512]{2,1,0:T(8,128)(2,1)S(1)} %collective-permute-done.25.refs_6_), channel_id=1, source_target_pairs={{0,1},{1,0},{2,3},{3,2},{4,5},{5,4},{6,7},{7,6},{8,9},{9,8},{10,11... | collective-permute-start | bytes 2555912 | tf_op jit(solution)/shard_map/ppermute | solution.py:564
  137.9 42.4 %collective-permute-start.36 = (bf16[2,864,512]{2,1,0:T(8,128)(2,1)}, bf16[2,864,512]{2,1,0:T(8,128)(2,1)}, u32[]{:S(2)}, u32[]{:S(2)}) collective-permute-start(bf16[2,864,512]{2,1,0:T(8,128)(2,1)} %get-tuple-element.123), channel_id=1, source_target_pairs={{0,1},{1,0},{2,3},{3,2},{4,5},{5,4},{6,7},{7,6},{8,9},{9,8},{10,11... | collective-permute-start | bytes 5308424 | tf_op jit(solution)/shard_map/ppermute | solution.py:564
  162.6 40.5 %collective-permute-start.33 = (bf16[2,2,256,512]{3,2,1,0:T(8,128)(2,1)}, bf16[2,2,256,512]{3,2,1,0:T(8,128)(2,1)}, u32[]{:S(2)}, u32[]{:S(2)}) collective-permute-start(bf16[2,2,256,512]{3,2,1,0:T(8,128)(2,1)} %get-tuple-element.110), channel_id=1, source_target_pairs={{0,4},{4,0},{8,12},{12,8},{16,20},{20,16},{24,28},{28,24},{1,5},{5... | collective-permute-start | bytes 3145736 | tf_op jit(solution)/shard_map/ppermute | solution.py:572
  165.0 22.7 %collective-permute-start.32 = (bf16[864,512]{1,0:T(8,128)(2,1)}, bf16[864,512]{1,0:T(8,128)(2,1)S(1)}, u32[]{:S(2)}, u32[]{:S(2)}) collective-permute-start(bf16[864,512]{1,0:T(8,128)(2,1)} %get-tuple-element.176), channel_id=1, source_target_pairs={{0,2},{1,3},{2,0},{3,1},{4,6},{5,7},{6,4},{7,5},{8,10},{9,11},{10,... | collective-permute-start | bytes 2654216 | tf_op jit(solution)/shard_map/ppermute | solution.py:568
  178.7 55.1 %collective-permute-start.34 = (bf16[2,2,256,512]{3,2,1,0:T(8,128)(2,1)}, bf16[2,2,256,512]{3,2,1,0:T(8,128)(2,1)}, u32[]{:S(2)}, u32[]{:S(2)}) collective-permute-start(bf16[2,2,256,512]{3,2,1,0:T(8,128)(2,1)} %get-tuple-element.116), channel_id=1, source_target_pairs={{0,4},{4,0},{8,12},{12,8},{16,20},{20,16},{24,28},{28,24},{1,5},{5... | collective-permute-start | bytes 3145736 | tf_op jit(solution)/shard_map/ppermute | solution.py:572
  183.6 56.2 %collective-permute-start.37 = (bf16[864,512]{1,0:T(8,128)(2,1)}, bf16[864,512]{1,0:T(8,128)(2,1)S(1)}, u32[]{:S(2)}, u32[]{:S(2)}) collective-permute-start(bf16[864,512]{1,0:T(8,128)(2,1)} %get-tuple-element.174), channel_id=1, source_target_pairs={{0,2},{1,3},{2,0},{3,1},{4,6},{5,7},{6,4},{7,5},{8,10},{9,11},{10,... | collective-permute-start | bytes 2654216 | tf_op jit(solution)/shard_map/ppermute | solution.py:568
  205.5 32.1 %collective-permute-start.35 = (bf16[2,256,512]{2,1,0:T(8,128)(2,1)}, bf16[2,256,512]{2,1,0:T(8,128)(2,1)}, u32[]{:S(2)}, u32[]{:S(2)}) collective-permute-start(bf16[2,256,512]{2,1,0:T(8,128)(2,1)} %slice_bitcast_fusion.14), channel_id=1, source_target_pairs={{0,16},{4,20},{8,24},{12,28},{16,0},{20,4},{24,8},{28,12},{1,17},{... | collective-permute-start | bytes 1572872 | tf_op jit(solution)/shard_map/ppermute | solution.py:584
  232.3 28.4 %collective-permute-start.38 = (bf16[2,2,256,512]{3,2,1,0:T(8,128)(2,1)}, bf16[2,2,256,512]{3,2,1,0:T(8,128)(2,1)}, u32[]{:S(2)}, u32[]{:S(2)}) collective-permute-start(bf16[2,2,256,512]{3,2,1,0:T(8,128)(2,1)} %get-tuple-element.131), channel_id=1, source_target_pairs={{0,4},{4,0},{8,12},{12,8},{16,20},{20,16},{24,28},{28,24},{1,5},{5... | collective-permute-start | bytes 3145736 | tf_op jit(solution)/shard_map/ppermute | solution.py:572
  235.4 23.9 %collective-permute-start.41 = (bf16[2,256,512]{2,1,0:T(8,128)(2,1)S(1)}, bf16[2,256,512]{2,1,0:T(8,128)(2,1)S(1)}, u32[]{:S(2)}, u32[]{:S(2)}) collective-permute-start(bf16[2,256,512]{2,1,0:T(8,128)(2,1)S(1)} %slice_bitcast_fusion.12), channel_id=1, source_target_pairs={{0,16},{4,20},{8,24},{12,28},{16,0},{20,4},{24,8},{28,12},{1,17},{... | collective-permute-start | bytes 1572872 | tf_op jit(solution)/shard_map/ppermute | solution.py:584
  237.1 41.4 %collective-permute-start.40 = (bf16[2,2,256,512]{3,2,1,0:T(8,128)(2,1)}, bf16[2,2,256,512]{3,2,1,0:T(8,128)(2,1)}, u32[]{:S(2)}, u32[]{:S(2)}) collective-permute-start(bf16[2,2,256,512]{3,2,1,0:T(8,128)(2,1)} %get-tuple-element.134), channel_id=1, source_target_pairs={{0,4},{4,0},{8,12},{12,8},{16,20},{20,16},{24,28},{28,24},{1,5},{5... | collective-permute-start | bytes 3145736 | tf_op jit(solution)/shard_map/ppermute | solution.py:572
  263.2 18.5 %collective-permute-start.39 = (bf16[256,2176]{1,0:T(8,128)(2,1)}, bf16[256,2176]{1,0:T(8,128)(2,1)}, u32[]{:S(2)}, u32[]{:S(2)}) collective-permute-start(bf16[256,2176]{1,0:T(8,128)(2,1)} %get-tuple-element.132), channel_id=1, source_target_pairs={{0,1},{1,0},{2,3},{3,2},{4,5},{5,4},{6,7},{7,6},{8,9},{9,8},{10,11... | collective-permute-start | bytes 3342344 | tf_op jit(solution)/shard_map/ppermute | solution.py:564
  268.1 36.8 %collective-permute-start.43 = (bf16[2,256,512]{2,1,0:T(8,128)(2,1)S(1)}, bf16[2,256,512]{2,1,0:T(8,128)(2,1)S(1)}, u32[]{:S(2)}, u32[]{:S(2)}) collective-permute-start(bf16[2,256,512]{2,1,0:T(8,128)(2,1)S(1)} %slice_bitcast_fusion.10), channel_id=1, source_target_pairs={{0,16},{4,20},{8,24},{12,28},{16,0},{20,4},{24,8},{28,12},{1,17},{... | collective-permute-start | bytes 1572872 | tf_op jit(solution)/shard_map/ppermute | solution.py:584
  280.1 36.0 %collective-permute-start.48 = (bf16[2,256,512]{2,1,0:T(8,128)(2,1)S(1)}, bf16[2,256,512]{2,1,0:T(8,128)(2,1)S(1)}, u32[]{:S(2)}, u32[]{:S(2)}) collective-permute-start(bf16[2,256,512]{2,1,0:T(8,128)(2,1)S(1)} %slice_bitcast_fusion.5), channel_id=1, source_target_pairs={{0,16},{4,20},{8,24},{12,28},{16,0},{20,4},{24,8},{28,12},{1,17},{... | collective-permute-start | bytes 1572872 | tf_op jit(solution)/shard_map/ppermute | solution.py:584
  283.4 32.8 %collective-permute-start.42 = (bf16[4,2,16,2176]{3,2,0,1:T(8,128)(2,1)S(1)}, bf16[4,2,16,2176]{3,2,0,1:T(8,128)(2,1)S(1)}, u32[]{:S(2)}, u32[]{:S(2)}) collective-permute-start(bf16[4,2,16,2176]{3,2,0,1:T(8,128)(2,1)S(1)} %bitcast.139), channel_id=1, source_target_pairs={{0,2},{1,3},{2,0},{3,1},{4,6},{5,7},{6,4},{7,5},{8,10},{9,11},{10,... | collective-permute-start | bytes 1671176 | tf_op jit(solution)/shard_map/ppermute | solution.py:568
  (58 other events, 661.7 us)

commit v3 on v2

--- a/solution.py
+++ b/solution.py
@@ -128,7 +128,7 @@
         out_shape=[out(3 * width, BF), out(width, BF), out(width, F32), out(width, BF), out(128, F32)],
         name="dense_forward",
         cost_estimate=cost(5),
-        compiler_params=pltpu.CompilerParams(vmem_limit_bytes=60 << 20),
+        compiler_params=pltpu.CompilerParams(vmem_limit_bytes=24 << 20),
     )(tok, dense, tailt)
 
 
@@ -169,7 +169,7 @@
                     gate_ref[j, at : at + slots, :] = jnp.broadcast_to(gates[j], (slots, 128))
 
 
-def expert_kernel(experts, n_src, slots, chunk, ei_ref, *refs):
+def expert_kernel(experts, n_src, slots, chunk, at_ref, *refs):
     acts, refs = refs[:n_src], refs[n_src:]
     dys, refs = refs[:n_src], refs[n_src:]
     wu, bu, wd, bd = refs[:4]
@@ -177,8 +177,7 @@
     raw_ref, gate_ref, p_ref, resg_ref, din_ref, dg_ref = refs[10:]
     local = x_ref.shape[0]
     rows = acts[0].shape[1]
-    hidden = wu.shape[2]
-    ei = ei_ref[0]
+    ei = at_ref[0]
     e = pl.program_id(0)
 
     @pl.when(e == 0)
@@ -189,10 +188,10 @@
 
     x, g = x_ref[e], g_ref[e]
     res = din = None
-    for h in range(0, hidden, chunk):
+    for h in range(0, wu.shape[2], chunk):
         cut = slice(h, h + chunk)
         up, down = wu[0, :, cut], wd[0, cut]
-        pre = dot(x, up, 1, 0) + bu[0, :, cut].astype(F32)
+        pre = dot(x, up, 1, 0) + bu[pl.ds(e, 1), cut]
         cdf, pdf = gelu_parts(pre)
         hid = (pre * cdf).astype(BF)
         dpre = (dot(g, down, 1, 1) * (cdf + pre * pdf)).astype(BF)
@@ -201,7 +200,7 @@
         res = res_part if res is None else res + res_part
         din = din_part if din is None else din + din_part
     gbd[0] = jnp.sum(g.astype(F32), axis=0, keepdims=True)
-    res = (res + bd[0].astype(F32)).astype(BF).astype(F32)
+    res = (res + bd[pl.ds(e, 1), :]).astype(BF).astype(F32)
     dg = jnp.sum(res * raw_ref[e].astype(F32), axis=1, keepdims=True)
     dg_ref[e] = jnp.broadcast_to(dg, dg_ref.shape[1:])
     resg_ref[e] = (gate_ref[e][:, 0:1] * res).astype(BF)
@@ -231,7 +230,7 @@
                 out[s // CORES, to : to + experts, 0:rows] = dprob.astype(BF)
 
 
-def run_experts(place, sources, w_up, b_up, w_down, b_down, experts, slots):
+def run_experts(place, part, sources, w_up, b_up, w_down, b_down, experts, slots):
     local, width, hidden = w_up.shape
     n_src = len(sources)
     span = sources[0][0].shape[1]
@@ -246,12 +245,13 @@
         grid_spec=pltpu.PrefetchScalarGridSpec(
             num_scalar_prefetch=1,
             grid=(local,),
-            in_specs=[keep(HALF, span, width)] * len(flat)
+            in_specs=[keep(HALF, span, width)] * n_src
+            + [pl.BlockSpec((HALF, span, width), lambda e, p: (part, 0, 0))] * n_src
             + [
                 each(width, hidden),
-                each(1, hidden),
+                keep(local, hidden),
                 each(hidden, width),
-                each(1, width),
+                keep(local, width),
             ],
             out_specs=[
                 keep(n_src // CORES, back, width),
@@ -307,19 +307,19 @@
         ),
         out_shape=[jax.ShapeDtypeStruct((local, rows, width), BF)] * 2,
         name="pick_rows",
-        cost_estimate=cost(5),
-        compiler_params=pltpu.CompilerParams(vmem_limit_bytes=60 << 20),
+        cost_estimate=cost(1),
+        compiler_params=pltpu.CompilerParams(vmem_limit_bytes=32 << 20),
     )(place.ei.reshape(1), *flat)
 
 
-def weight_grad_kernel(n_rows, ny, hb, own_ref, *refs):
+def weight_grad_kernel(e, n_rows, ny, hb, own_ref, *refs):
     xs, gs = refs[:n_rows], refs[n_rows : 2 * n_rows]
     wu, bu, wd = refs[2 * n_rows : 2 * n_rows + 3]
     outs, total = refs[2 * n_rows + 3 : -1], refs[-1]
     up = down = None
     for x_ref, g_ref in zip(xs, gs):
         x, g = x_ref[0], g_ref[0]
-        pre = dot(x, wu[0], 1, 0) + bu[0].astype(F32)
+        pre = dot(x, wu[0], 1, 0) + bu[e : e + 1, :]
         cdf, pdf = gelu_parts(pre)
         hid = (pre * cdf).astype(BF)
         dpre = (dot(g, wd[0], 1, 1) * (cdf + pre * pdf)).astype(BF)
@@ -333,15 +333,14 @@
         outs[k][0] = total[:, pl.ds(at, hb), :]
 
 
-def run_weight_grad(place, e, xs, gs, w_up, b_up, w_down):
+def run_weight_grad(place, where, e, xs, gs, w_up, b_up, w_down):
     _, width, hidden = w_up.shape
     cols = hidden // place.nz
     nh, ny = place.nh, place.ny
     hb = cols // ny
-    own = [place.y] + [(place.zh + k) % nh * 2 + place.zl for k in range(nh)]
     row = [pl.BlockSpec((1,) + x.shape[1:], lambda k, p: (e, 0, 0)) for x in xs]
     return pl.pallas_call(
-        functools.partial(weight_grad_kernel, len(xs), ny, hb),
+        functools.partial(weight_grad_kernel, e, len(xs), ny, hb),
         grid_spec=pltpu.PrefetchScalarGridSpec(
             num_scalar_prefetch=1,
             grid=(nh,),
@@ -349,7 +348,7 @@
             + row
             + [
                 pl.BlockSpec((1, width, cols), lambda k, p: (e, 0, p[k + 1])),
-                pl.BlockSpec((1, 1, cols), lambda k, p: (e, 0, p[k + 1])),
+                pl.BlockSpec((b_up.shape[0], cols), lambda k, p: (0, p[k + 1])),
                 pl.BlockSpec((1, cols, width), lambda k, p: (e, p[k + 1], 0)),
             ],
             out_specs=[pl.BlockSpec((1, 2, hb, width), lambda k, p: (k, 0, 0, 0))] * ny,
@@ -358,35 +357,18 @@
         out_shape=[jax.ShapeDtypeStruct((nh, 2, hb, width), BF)] * ny,
         name="weight_grad",
         cost_estimate=cost(1),
-        compiler_params=pltpu.CompilerParams(vmem_limit_bytes=60 << 20),
-    )(jnp.stack(own).astype(jnp.int32), *xs, *gs, w_up, b_up, w_down)
-
-
-def backward_kernel(experts, n_back, first, share, core_ref, *refs):
-    tok, dy, dense, tailt, qkv, mix, resid, act_two, lse = refs[:9]
-    moes, dins, dgs = [refs[9 + k * n_back : 9 + (k + 1) * n_back] for k in range(3)]
-    refs = refs[9 + 3 * n_back :]
-    if not first:
-        before, before_t = refs[:2]
-        refs = refs[2:]
-    if share:
-        out, gtok, keep, send, dqkv, acc, acc_t = refs
-    else:
-        out, gtok, acc, acc_t, dqkv = refs
+        compiler_params=pltpu.CompilerParams(vmem_limit_bytes=32 << 20),
+    )(where, *xs, *gs, w_up, b_up, w_down)
+
+
+def backward_kernel(experts, n_back, *refs):
+    tok, dy, dense, tailt, qkv, resid, act_two, lse = refs[:8]
+    moes, dins, dgs = [refs[8 + k * n_back : 8 + (k + 1) * n_back] for k in range(3)]
+    out, gtok, dattn_o, act_o, dqkv, acc_t = refs[8 + 3 * n_back :]
     width = tok.shape[2]
     rows = tok.shape[1]
     pairs = width // (2 * HEAD)
     scale = HEAD ** (-0.5)
-
-    @pl.when(pl.program_id(0) == 0)
-    def _():
-        if first:
-            acc[...] = jnp.zeros_like(acc)
-            acc_t[...] = jnp.zeros_like(acc_t)
-        else:
-            acc[:, : 4 * width] = before[...]
-            acc_t[...] = before_t[...]
-
     total = lambda parts: functools.reduce(jnp.add, [p[...].astype(F32) for p in parts])
     tail = tailt[...]
     vec = tail.astype(F32)[experts : experts + 7]
@@ -401,7 +383,7 @@
     dyf = jnp.where(iota((rows, width), 0) < SEQ, dy[0].astype(F32), 0.0)
     dresid = dyf + norm_back(dact_two, normed_two, inv_two, vec[1:2])
     dattn = dresid.astype(BF)
-    acc[:, 3 * width : 4 * width] += dot(mix[0], dattn, 0, 0)
+    dattn_o[0] = dattn
     dmixed = dot(dattn, dense[:, 3 * width : 4 * width], 1, 1).astype(BF)
     seen = iota((rows, rows), 1) < SEQ
     for p in range(pairs):
@@ -425,90 +407,155 @@
             dq = dq_s if dq is None else dq + dq_s
             dk = dk_s if dk is None else dk + dk_s
             dv = dv_s if dv is None else dv + dv_s
-        dqkv[:, at : at + 2 * HEAD] = (dq * scale).astype(BF)
-        dqkv[:, width + at : width + at + 2 * HEAD] = (dk * scale).astype(BF)
-        dqkv[:, 2 * width + at : 2 * width + at + 2 * HEAD] = dv.astype(BF)
+        dqkv[0, :, at : at + 2 * HEAD] = (dq * scale).astype(BF)
+        dqkv[0, :, width + at : width + at + 2 * HEAD] = (dk * scale).astype(BF)
+        dqkv[0, :, 2 * width + at : 2 * width + at + 2 * HEAD] = dv.astype(BF)
     normed_one, inv_one = norm_rows(tok[0].astype(F32))
     act_one = (normed_one * vec[0:1] + vec[5:6]).astype(BF)
-    acc[:, : 3 * width] += dot(act_one, dqkv[...], 0, 0)
-    dact_one = dot(dqkv[...], dense[:, : 3 * width], 1, 1)
+    act_o[0] = act_one
+    dact_one = dot(dqkv[0], dense[:, : 3 * width], 1, 1)
     gtok[0] = dresid + norm_back(dact_one, normed_one, inv_one, vec[0:1])
     rowsum = lambda v: jnp.sum(v.astype(F32), axis=0, keepdims=True)
     sums = [
         rowsum(dact_one * normed_one),
         rowsum(dact_two * normed_two),
-        rowsum(dqkv[:, :width]),
-        rowsum(dqkv[:, 2 * width :]),
+        rowsum(dqkv[0, :, :width]),
+        rowsum(dqkv[0, :, 2 * width :]),
         rowsum(dattn),
         rowsum(dact_one),
         rowsum(dact_two),
     ]
-    acc_t[...] += dot(dlogit, act_two[0], 1, 0)
+    acc_t[...] = dot(dlogit, act_two[0], 1, 0)
     for i, row in enumerate(sums):
-        acc_t[experts + i : experts + i + 1, :] += row
-    if share:
-
-        @pl.when(pl.program_id(0) == HALF - 1)
-        def _():
-            last = jnp.transpose(acc_t[...], (1, 0))
-            acc[:, 4 * width : 4 * width + 128] = last
-            core = core_ref[0]
-
-            def body(i, carry):
-                to = pl.multiple_of(i * share, 16)
-                for ref, side in ((keep, core), (send, 1 - core)):
-                    at = pl.multiple_of((i * CORES + side) * share, 16)
-                    ref[pl.ds(to, share), :] = acc[pl.ds(at, share), :].astype(BF)
-                return carry
-
-            lax.fori_loop(0, width // share // CORES, body, 0)
-
-
-def run_backward(place, part, tok, dy, dense, tailt, saved, backs, before, experts, share):
+        acc_t[experts + i : experts + i + 1, :] = row
+
+
+def run_backward(image, tok, dy, dense, tailt, saved, backs, experts):
     _, rows, width = tok.shape
-    whole = lambda a: pl.BlockSpec(a.shape, lambda i, c: (0,) * len(a.shape))
-    at_half = pl.BlockSpec((1, rows, width), lambda i, c: (part * HALF + i, 0, 0))
-    row = lambda n: pl.BlockSpec((1, rows, n), lambda i, c: (i, 0, 0))
+    i = image % HALF
+    whole = lambda a: pl.BlockSpec(a.shape, lambda k: (0,) * len(a.shape))
+    at = lambda j, n: pl.BlockSpec((1, rows, n), lambda k: (j, 0, 0))
     first = 2 * HALF * rows // experts
     back_specs = (
-        [pl.BlockSpec((rows, width), lambda i, c: (i, 0))] * len(backs)
-        + [pl.BlockSpec((rows, width), lambda i, c: (HALF + i, 0))] * len(backs)
-        + [pl.BlockSpec((experts, width), lambda i, c: (first + i, 0))] * len(backs)
+        [pl.BlockSpec((rows, width), lambda k: (i, 0))] * len(backs)
+        + [pl.BlockSpec((rows, width), lambda k: (HALF + i, 0))] * len(backs)
+        + [pl.BlockSpec((experts, width), lambda k: (first + i, 0))] * len(backs)
     )
-    args = [tok, dy, dense, tailt, *saved, *backs, *backs, *backs]
-    specs = [at_half, at_half, whole(dense), whole(tailt)]
-    specs += [row(3 * width), row(width), row(width), row(width), row(128)] + back_specs
-    cols = dense.shape[1]
-    scratch = [pltpu.VMEM((rows, 3 * width), BF)]
-    if share:
-        sums = [jax.ShapeDtypeStruct((width // CORES, cols), BF)] * 2
-        scratch += [pltpu.VMEM((width, cols), F32), pltpu.VMEM((128, width), F32)]
-    else:
-        sums = [
-            jax.ShapeDtypeStruct((width, 4 * width), F32),
-            jax.ShapeDtypeStruct((128, width), F32),
-        ]
-    if before is not None:
-        args += list(before)
-        specs += [whole(b) for b in before]
+    qkv, _, resid, act, lse = saved
+    args = [tok, dy, dense, tailt, qkv, resid, act, lse, *backs, *backs, *backs]
+    specs = [at(image, width), at(image, width), whole(dense), whole(tailt)]
+    specs += [at(i, 3 * width), at(i, width), at(i, width), at(i, 128)] + back_specs
+    out = lambda n, d: jax.ShapeDtypeStruct((1, rows, n), d)
+    outs = [out(width, BF), out(width, F32), out(width, BF), out(width, BF), out(3 * width, BF)]
+    outs += [jax.ShapeDtypeStruct((128, width), F32)]
     return pl.pallas_call(
-        functools.partial(backward_kernel, experts, len(backs), before is None, share),
-        grid_spec=pltpu.PrefetchScalarGridSpec(
-            num_scalar_prefetch=1,
-            grid=(HALF,),
-            in_specs=specs,
-            out_specs=[row(width), row(width), whole(sums[0]), whole(sums[1])],
-            scratch_shapes=scratch,
-        ),
-        out_shape=[
-            jax.ShapeDtypeStruct((HALF, rows, width), BF),
-            jax.ShapeDtypeStruct((HALF, rows, width), F32),
-            *sums,
-        ],
+        functools.partial(backward_kernel, experts, len(backs)),
+        grid=(1,),
+        in_specs=specs,
+        out_specs=[whole(o) for o in outs],
+        out_shape=outs,
         name="dense_backward",
         cost_estimate=cost(1),
-        compiler_params=pltpu.CompilerParams(vmem_limit_bytes=60 << 20),
+        compiler_params=pltpu.CompilerParams(vmem_limit_bytes=24 << 20),
+    )(*args)
+
+
+def dense_grads_kernel(share, core_ref, *refs):
+    acts, dqkvs, dattns, tails = [refs[k * MICRO : (k + 1) * MICRO] for k in range(4)]
+    mixes = refs[4 * MICRO : 4 * MICRO + MICRO // HALF]
+    outs = refs[4 * MICRO + MICRO // HALF :]
+    full = outs[-1]
+    width = acts[0].shape[2]
+    join = lambda parts: jnp.concatenate([p[0] for p in parts], axis=0)
+    act, dqkv, dattn = join(acts), join(dqkvs), join(dattns)
+    mix = jnp.concatenate([m[i] for m in mixes for i in range(HALF)], axis=0)
+    for k in range(3):
+        full[:, k * width : (k + 1) * width] = dot(
+            act, dqkv[:, k * width : (k + 1) * width], 0, 0
+        ).astype(BF)
+    full[:, 3 * width : 4 * width] = dot(mix, dattn, 0, 0).astype(BF)
+    tail = functools.reduce(jnp.add, [t[...] for t in tails])
+    full[:, 4 * width :] = jnp.transpose(tail, (1, 0)).astype(BF)
+    if share:
+        keep, send = outs[:2]
+        core = core_ref[0]
+
+        def body(i, carry):
+            to = pl.multiple_of(i * share, 16)
+            for ref, side in ((keep, core), (send, 1 - core)):
+                at = pl.multiple_of((i * CORES + side) * share, 16)
+                ref[pl.ds(to, share), :] = full[pl.ds(at, share), :]
+            return carry
+
+        lax.fori_loop(0, width // share // CORES, body, 0)
+
+
+def run_dense_grads(place, parts, mixes, wide, share):
+    width = mixes[0].shape[2]
+    args = [p[k] for k in (3, 4, 2, 5) for p in parts] + list(mixes)
+    vmem = pl.BlockSpec(memory_space=pltpu.VMEM)
+    whole = [jax.ShapeDtypeStruct((width, wide), BF)]
+    split = [jax.ShapeDtypeStruct((width // CORES, wide), BF)] * 2
+    return pl.pallas_call(
+        functools.partial(dense_grads_kernel, share),
+        in_specs=[pl.BlockSpec(memory_space=pltpu.SMEM)] + [vmem] * len(args),
+        out_specs=[vmem] * len(split if share else whole),
+        out_shape=split if share else whole,
+        scratch_shapes=[pltpu.VMEM((width, wide), BF)] if share else [],
+        name="dense_grads",
+        cost_estimate=cost(1),
+        compiler_params=pltpu.CompilerParams(vmem_limit_bytes=32 << 20),
     )(place.c.reshape(1), *args)
+
+
+def store_expert_kernel(n, *refs):
+    total = functools.reduce(jnp.add, [r[...].astype(F32) for r in refs[:n]])
+    up, down = refs[-2:]
+    up[0] = jnp.transpose(total[0], (1, 0))
+    down[0] = total[1]
+
+
+def store_expert(e, local, parts, before):
+    _, hb, width = parts[0].shape
+    whole = pl.BlockSpec(parts[0].shape, lambda k: (0, 0, 0))
+    return pl.pallas_call(
+        functools.partial(store_expert_kernel, len(parts)),
+        grid=(1,),
+        in_specs=[whole] * len(parts) + [pl.BlockSpec(memory_space=pl.ANY)] * len(before),
+        out_specs=[
+            pl.BlockSpec((1, width, hb), lambda k: (e, 0, 0)),
+            pl.BlockSpec((1, hb, width), lambda k: (e, 0, 0)),
+        ],
+        out_shape=[
+            jax.ShapeDtypeStruct((local, width, hb), F32),
+            jax.ShapeDtypeStruct((local, hb, width), F32),
+        ],
+        input_output_aliases={len(parts) + k: k for k in range(len(before))},
+        name="store_expert",
+        cost_estimate=cost(1),
+        compiler_params=pltpu.CompilerParams(vmem_limit_bytes=16 << 20),
+    )(*parts, *before)
+
+
+def split_kernel(n, *refs):
+    total = functools.reduce(jnp.add, [r[...].astype(F32) for r in refs[:n]])
+    at = 0
+    for out in refs[n:]:
+        out[...] = total[:, at : at + out.shape[1]]
+        at += out.shape[1]
+
+
+def split_sum(parts, widths):
+    vmem = pl.BlockSpec(memory_space=pltpu.VMEM)
+    return pl.pallas_call(
+        functools.partial(split_kernel, len(parts)),
+        in_specs=[vmem] * len(parts),
+        out_specs=[vmem] * len(widths),
+        out_shape=[jax.ShapeDtypeStruct((parts[0].shape[0], w), F32) for w in widths],
+        name="split_sum",
+        cost_estimate=cost(1),
+        compiler_params=pltpu.CompilerParams(vmem_limit_bytes=16 << 20),
+    )(*parts)
 
 
 def arrange_kernel(n, share, at_ref, near, other, dense, tailt):
@@ -537,8 +584,8 @@
             jax.ShapeDtypeStruct((128, width), BF),
         ],
         name="arrange",
-        compiler_params=pltpu.CompilerParams(vmem_limit_bytes=60 << 20),
-        cost_estimate=cost(3),
+        compiler_params=pltpu.CompilerParams(vmem_limit_bytes=16 << 20),
+        cost_estimate=cost(1),
     )(order, near, other)
 
 
@@ -602,49 +649,37 @@
         return [v for pair in zip(mine, other) for v in pair]
 
 
-def after(val, *deps):
-    return lax.optimization_barrier((val, *deps))[0]
-
-
-def gather_dense(place, piece):
-    share, wide = piece.shape
+def after(deps, *vals):
+    return lax.optimization_barrier((*vals, *deps))[: len(vals)]
+
+
+def place_order(place):
     nz, ny, nx = place.nz, place.ny, place.nx
-    line = jnp.concatenate([piece] + [place.zs(piece, k) for k in range(1, nz)], axis=0)
-    moves = [(ky, kx) for ky in range(ny) for kx in range(nx)]
-    near = jnp.concatenate([line] + [place.xy(line, kx, ky) for ky, kx in moves[1:]], axis=0)
-    other = place.core(near)
     order = []
     for c in (place.c, 1 - place.c):
-        for ky, kx in moves:
-            for kz in range(nz):
-                dp = (place.z - kz) % nz * ny + (place.y - ky) % ny
-                order.append(dp * place.ne + (place.x - kx) % nx * CORES + c)
-    order = jnp.stack(order).astype(jnp.int32)
+        for ky in range(ny):
+            for kx in range(nx):
+                for kz in range(nz):
+                    dp = (place.z - kz) % nz * ny + (place.y - ky) % ny
+                    order.append(dp * place.ne + (place.x - kx) % nx * CORES + c)
+    return jnp.stack(order).astype(jnp.int32)
+
+
+def dense_in_order(place, near, other, order, share):
     if share % 16 == 0:
-        return line, near, *arrange(near, other, order, share)
+        return arrange(near, other, order, share)
+    wide = near.shape[1]
     full = jnp.concatenate([near, other]).reshape(-1, share, wide)
     dense = jnp.zeros_like(full).at[order].set(full).reshape(-1, wide)
-    return line, near, dense, dense[:, wide - 128 :].T
-
-
-def scatter_rows(place, keep, send, small, used, first, second, third):
-    wide = keep.shape[1]
-    add = lambda a, b: (a.astype(F32) + b.astype(F32)).astype(BF)
-
-    def stage(v, n, own, shift, last=False):
-        pick = lambda i: lax.dynamic_index_in_dim(v, i % n, 0, keepdims=False)
-        total = pick(own).astype(F32)
-        for k in range(1, n):
-            total = total + shift(pick(own + k), k).astype(F32)
-        return total if last else total.astype(BF)
-
-    val = after(add(keep, place.core(after(send, *first))), *second)
-    val = val.reshape(place.nz, place.ny, place.nx, -1, wide)
-    val = stage(jnp.moveaxis(val, 2, 0), place.nx, place.x, place.xs)
-    val = after(val, *third)
-    val = jnp.concatenate([val[..., :used], small, val[..., used + small.shape[-1] :]], axis=-1)
-    val = stage(jnp.moveaxis(val, 1, 0), place.ny, place.y, place.ys)
-    return stage(val, place.nz, place.z, place.zs, last=True)
+    return dense, dense[:, wide - 128 :].T
+
+
+def stage(v, n, own, shift, dtype=BF):
+    pick = lambda i: lax.dynamic_index_in_dim(v, i % n, 0, keepdims=False)
+    total = pick(own).astype(F32)
+    for k in range(1, n):
+        total = total + shift(pick(own + k), k).astype(F32)
+    return total.astype(dtype)
 
 
 def on_device(
@@ -679,7 +714,6 @@
     assert used + n_small <= 128 or share % 16
     piece = jnp.concatenate([w_qkv, w_proj, w_router, norm_gains, biases], axis=1)
     piece = jnp.pad(piece, ((0, 0), (0, 4 * width + 128 - piece.shape[1])))
-    line, near, dense, tailt = gather_dense(place, piece)
 
     route_rows = routes.reshape(MICRO, SEQ, 2)
     names = jnp.arange(experts, dtype=jnp.int32)
@@ -694,128 +728,175 @@
     tok = jnp.pad(blocks(tokens_in), ((0, 0), (0, rows - SEQ), (0, 0)))
     gap = jnp.zeros((MICRO, rows - SEQ - experts // 2, width), BF)
     dy = jnp.concatenate([blocks(grad_out), gap, pos], axis=1)
-    bu3, bd3 = b_up[:, None, :], b_down[:, None, :]
-    dys = [dy[h * HALF : (h + 1) * HALF] for h in halves]
-    dy_near = [place.group(dys[0])] + [place.group(after(d, near)) for d in dys[1:]]
-    dy_z = place.zp(after(dy, line))
-
-    saved, acts = [], []
-    for h in halves:
-        *keep, act, lse = run_forward(tok, dense, tailt, h, experts)
-        saved.append((*keep, act, lse))
-        acts.append(act)
-    crossed = [[place.xs(act, k) for k in range(1, place.nx)] for act in acts]
-    near, far = [], []
-    for h in halves:
-        mine = [acts[h], *crossed[h]]
-        other = [place.core(after(v, acts[-1])) for v in mine]
-        near.append([v for pair in zip(mine, other) for v in pair])
-    for h in halves:
-        far.append(place.group(after(place.zp(acts[h]), *crossed[-1])))
-    dy_far = place.group(after(dy_z, *crossed[-1]))
-    results, x_far, g_far = [], [], []
-    for h in halves:
-        src = list(zip(near[h], dy_near[h]))
-        for at in range(0, len(src), 4):
-            results.append(
-                run_experts(place, src[at : at + 4], w_up, bu3, w_down, bd3, experts, slots)
-            )
+    bu3, bd3 = b_up.astype(F32), b_down.astype(F32)
+    across = lambda v: [v] + [place.xs(v, k) for k in range(1, place.nx)]
+    both_cores = lambda mine, other: [v for pair in zip(mine, other) for v in pair]
+    both_cores = lambda mine, other: [v for pair in zip(mine, other) for v in pair]
+    nx, nz = place.nx, place.nz
+
+    line = [piece] + [place.zs(piece, k) for k in range(1, nz)]
+    done = line
+
+    (line,) = after(done, jnp.concatenate(line, axis=0))
+    moves = [(ky, kx) for ky in range(ny) for kx in range(nx)]
+    part = [line] + [place.xy(line, kx, ky) for ky, kx in moves[1:]]
+    own = [(place.zh + k) % nh * 2 + place.zl for k in range(nh)]
+    where = jnp.stack([place.y, *own]).astype(jnp.int32)
+    tok, order, bu3, bd3, where = after(done, tok, place_order(place), bu3, bd3, where)
+    done = [*part, tok, order, bu3, bd3, where]
+
+    dense_near, dy = after(done, jnp.concatenate(part, axis=0), dy)
+    other = place.core(dense_near)
+    dy_mine, dy_z, dy_other = across(dy), place.zp(dy), place.core(dy)
+    dense, tailt = dense_in_order(place, dense_near, other, order, share)
+    saved, act_x, act_z, act_c = [], [], [], []
+    saved.append(run_forward(tok, dense, tailt, 0, experts))
+    done = [saved[0][3], dy_other]
+
+    for h in halves[1:]:
+        act, dense_h = after(done, saved[-1][3], dense)
+        act_x.append(across(act))
+        act_z.append(place.zp(act))
+        act_c.append(place.core(act))
+        saved.append(run_forward(tok, dense_h, tailt, h, experts))
+        done = [*act_x[-1], act_z[-1], act_c[-1], saved[-1][3], dy_z, *dy_mine]
+
+    act, far_dy, *rest = after(done, saved[-1][3], dy_z, *act_x[0][1:], *dy_mine[1:])
+    dy_near = both_cores(dy_mine, [dy_other, *[place.core(v) for v in rest[nx - 1 :]]])
+    rest = rest[: nx - 1]
+    act_x.append(across(act))
+    act_z.append(place.zp(act))
+    act_c.append(place.core(act))
+    dy_far = across(far_dy)
+    near = both_cores(act_x[0], [act_c[0], *[place.core(v) for v in rest]])
+    visit = lambda h, near: [
+        run_experts(place, h, list(zip(near, dy_near))[at : at + 4], w_up, bu3, w_down, bd3, experts, slots)
+        for at in range(0, len(near), 4)
+    ]
+    results = [visit(0, near)]
+    done = [*act_x[-1], *act_z, act_c[-1], *dy_far]
+    done += [r[0] for r in results[0]]
+
+    n_far = len(dy_far)
+    vals = after(done, *dy_far, *act_z, *act_x[1][1:], *[r[1] for r in results[0]])
+    dy_far = both_cores(vals[:n_far], [place.core(v) for v in vals[:n_far]])
+    far = [across(v) for v in vals[n_far : n_far + 2]]
+    rest = vals[n_far + 2 :]
+    near = both_cores(act_x[1], [act_c[1], *[place.core(v) for v in rest[: nx - 1]]])
+    back = [[place.core(v) for v in rest[nx - 1 :]]]
+    results.append(visit(1, near))
+    done = [*dy_far, *[v for f in far for v in f], *back[0], *[r[0] for r in results[1]]]
+
+    add = lambda a, b: (a.astype(F32) + b.astype(F32)).astype(BF)
+    pairs_of = lambda h: [
+        p[k] for p in [add(r[0], b) for r, b in zip(results[h], back[h])] for k in range(p.shape[0])
+    ]
+    home = lambda p: [p[0]] + [place.xs(p[k], nx - k) for k in range(1, nx)]
+    n_all = 2 * n_far
+    vals = after(done, *[v for f in far for v in f], *[r[1] for r in results[1]])
+    far = [vals[:n_far], vals[n_far:n_all]]
+    far = [both_cores(f, [place.core(v) for v in f]) for f in far]
+    back.append([place.core(v) for v in vals[n_all : n_all + len(results[1])]])
+    xs, gs = [[r[k] for rs in results for r in rs] for k in (2, 3)]
     for h in halves:
         src = list(zip(far[h], dy_far))
         for at in range(0, len(src), 4):
             x, g = run_pick(place, h, src[at : at + 4], local, experts, slots)
-            x_far.append(x)
-            g_far.append(g)
-
-    xs = [r[2] for r in results] + x_far
-    gs = [r[3] for r in results] + g_far
-    add = lambda a, b: (a.astype(F32) + b.astype(F32)).astype(BF)
-
-    def to_y(vals, *deps):
-        mine = after(vals[0], *deps) if deps else vals[0]
-        for ky in range(1, ny):
-            mine = add(mine, place.ys(vals[ky], ky))
-        return mine
-
-    def to_z(mine):
-        out = mine[0].astype(F32)
-        for kz in range(1, nh):
-            out = out + place.zhs(mine[kz], kz).astype(F32)
-        return out
-
-    part_b_up = sum(r[4] for r in results).reshape(local, place.nd, -1)
-    part_b_down = sum(r[5] for r in results).reshape(local, place.nd, -1)
+            xs.append(x)
+            gs.append(g)
+    for rs in results[:1]:
+        near_sent = after(xs[2 * len(rs) :], *[r[0] for r in rs])
+        results[0] = [(v, *r[1:]) for v, r in zip(near_sent, rs)]
+    backs = [home(pairs_of(0))]
+    weights = lambda e, x: run_weight_grad(place, where, e, [x, *xs[1:]], gs, w_up, bu3, w_down)
+    tokens_back = lambda i, d, v: run_backward(
+        i, v, d, dense, tailt, saved[i // HALF], backs[i // HALF], experts
+    )
+    sent = weights(0, xs[0])
+    done = [*back[1], *sent]
+
+    sent = list(after(done, *sent))
+    x, grads, rows_in, *pairs = after(done, xs[0], dy, tok, *pairs_of(1))
+    backs.append(home(pairs))
+    images, both, level = [], [], None
+    wide = dense.shape[1]
+    split = share if share % 16 == 0 else 0
+    todo = list(range(MICRO))
+    for e in range(local):
+        crossed = [place.ys(sent[k], k) for k in range(1, ny)]
+        done = list(crossed)
+        if level is not None:
+            moved = [place.zhs(level[k], k) for k in range(1, nh)]
+            both.append([level[0], *moved])
+            done += moved
+        if e + 1 < local:
+            later = weights(e + 1, x)
+            done += later
+        if todo:
+            for i in todo[:2]:
+                images.append(tokens_back(i, grads, rows_in))
+                done += images[-1]
+            todo = todo[2:]
+        elif e + 1 < local:
+            sums = run_dense_grads(place, images, [v[1] for v in saved], wide, split)
+            done += sums
+        else:
+            val = add(sums[0], place.core(sums[1]))
+            val = val.reshape(nz, ny, nx, -1, val.shape[1])
+            val = stage(jnp.moveaxis(val, 2, 0), nx, place.x, place.xs)
+        if e == 0:
+            done += backs[0]
+        level = functools.reduce(add, [sent[0], *crossed])
+        if e + 1 < local:
+            x, grads, rows_in, *sent = after(done, xs[0], dy, tok, *later)
+        if e == local - 2:
+            if not split:
+                full = jnp.moveaxis(sums[0].reshape(-1, CORES, share, wide), 1, 0)
+                side = lambda c: lax.dynamic_index_in_dim(full, c, 0, keepdims=False)
+                sums = [side(c).reshape(-1, wide) for c in (place.c, 1 - place.c)]
+            n_tail = used + n_small
+            if n_tail > 128:
+                sums = [jnp.pad(v, ((0, 0), (0, n_tail - 128))) for v in sums]
+            sums = after([*done, level], *sums)
+
+    across_x = val
+    moved = [place.zhs(level[k], k) for k in range(1, nh)]
+    both.append([level[0], *moved])
+    part_b_up = sum(r[4] for rs in results for r in rs).reshape(local, place.nd, -1)
+    part_b_down = sum(r[5] for rs in results for r in rs).reshape(local, place.nd, -1)
     small = jnp.concatenate([part_b_up, part_b_down], axis=2).transpose(1, 0, 2)
     small = small.reshape(place.nd, -1)
     small = jnp.pad(small, ((0, 0), (0, share * n_small - small.shape[1])))
-    small = small.reshape(place.nz, ny, share, n_small).astype(BF)
-
-    backs = []
-    per = len(results) // len(halves)
-    for h in halves:
-        pair = [add(r[0], place.core(r[1])) for r in results[h * per : (h + 1) * per]]
-        pair = [p[k] for p in pair for k in range(p.shape[0])]
-        backs.append([pair[0]] + [place.xs(pair[k], place.nx - k) for k in range(1, place.nx)])
-
-    sums = None
-    outs, gtoks, sent, summed = [], [], [], []
-
-    def weights(e, *deps):
-        if e >= local:
-            return
-        first = after(xs[0], *deps) if deps else xs[0]
-        sent.append(run_weight_grad(place, e, [first, *xs[1:]], gs, w_up, bu3, w_down))
-
-    def tokens_back(h, *deps):
-        nonlocal sums
-        last = share if h == len(halves) - 1 and share % 16 == 0 else 0
-        grads = after(dy, *deps)
-        out, gtok, *sums = run_backward(
-            place, h, tok, grads, dense, tailt, saved[h], backs[h], sums, experts, last
-        )
-        outs.append(out)
-        gtoks.append(gtok)
-
-    weights(0)
-    weights(1, sent[0][0])
-    tokens_back(0, sent[1][0])
-    summed.append(to_y(sent[0], gtoks[0]))
-    weights(2, gtoks[0], summed[0])
-    weights(3, sent[2][0])
-    summed.append(to_y(sent[1], sent[3][0]))
-    both = [to_z(summed[0])]
-    tokens_back(1, sent[3][0], summed[1], both[0])
-    summed.append(to_y(sent[2], gtoks[1]))
-    summed.append(to_y(sent[3], summed[2]))
-    both += [to_z(v) for v in summed[1:]]
-    grad_up = jnp.stack([b[0].T for b in both])
-    grad_down = jnp.stack([b[1] for b in both])
+    small = small.reshape(nz, ny, share, n_small).astype(BF)
+    at = 4 * width + used
+    val = jnp.concatenate([val[..., :at], small, val[..., at + n_small :]], axis=-1)
+    val = stage(jnp.moveaxis(val, 1, 0), ny, place.y, place.ys)
+    pick = lambda i: lax.dynamic_index_in_dim(val, i % nz, 0, keepdims=False)
+    parts = [pick(place.z)] + [place.zs(pick(place.z + k), k) for k in range(1, nz)]
+    qkv_g, proj_g, router_g, gains_g, biases_g, tiny = split_sum(
+        parts, [3 * width, width, experts, 2, 5, n_small]
+    )
+    stored = []
+    for e, b in enumerate(both):
+        b = after([qkv_g], *b) if e == local - 1 else b
+        stored = store_expert(e, local, b, stored)
+    grad_up, grad_down = stored
+    outs = after([across_x], *[v[0] for v in images])
+    gtoks = after([across_x], *[v[1] for v in images])
     tokens = lambda v: jnp.concatenate(v, axis=0)[:, :SEQ].reshape(-1, width)
-    if share % 16:
-        full = jnp.concatenate([sums[0], sums[1].T], axis=1).astype(BF)
-        full = jnp.moveaxis(full.reshape(-1, CORES, share, full.shape[1]), 1, 0)
-        side = lambda c: lax.dynamic_index_in_dim(full, c, 0, keepdims=False)
-        sums = [side(c).reshape(-1, full.shape[3]) for c in (place.c, 1 - place.c)]
-    if used + n_small > 128:
-        sums = [jnp.pad(v, ((0, 0), (0, used + n_small - 128))) for v in sums]
-    waits = [summed[2]], [summed[3], both[1]], [both[2]]
-    grads = scatter_rows(place, *sums, small, 4 * width + used, *waits)
-    tiny = grads[:, 4 * width + used : 4 * width + used + n_small].reshape(-1)
-    tiny = tiny[: local * (hb + width // place.nd)].reshape(local, -1)
-    grad_b_up, grad_b_down = tiny[:, :hb], tiny[:, hb:]
-    at = 4 * width
+    tiny = tiny.reshape(-1)[: local * (hb + width // place.nd)].reshape(local, -1)
     return (
         tokens(outs),
         tokens(gtoks),
-        grads[:, at + experts : at + experts + 2],
-        grads[:, at + experts + 2 : at + experts + 7],
-        grads[:, : 3 * width],
-        grads[:, 3 * width : at],
-        grads[:, at : at + experts],
+        gains_g,
+        biases_g,
+        qkv_g,
+        proj_g,
+        router_g,
         grad_up,
-        grad_b_up,
+        tiny[:, :hb],
         grad_down,
-        grad_b_down,
+        tiny[:, hb:],
     )
 
 

time: 343 us -> 314 us (0.915)
  Pallas kernels: 157 us -> 137 us
  waiting for transfers between devices: 90.5 us -> 84.6 us
  starting transfers between devices: 40.1 us -> 35.4 us
    ppermute x6, waiting for transfers between devices: 8.94 us -> 24.8 us  [zs(): lax.ppermute(val, 'dp', [(i, (i // m + k) % n * m + i % m) for i in range...]
    ppermute x4, waiting for transfers between devices: 32 us -> 17 us  [zhs(): lax.ppermute(val, 'dp', [(i, ((i // m // 2 + k) % n * 2 + i // m % 2) * m...]
    ppermute x10 -> x9, waiting for transfers between devices: 23.1 us -> 10.9 us  [xs(): lax.ppermute(val, 'expert', [(i, (i // c + k) % n * c + i % c) for i in r...]
    ppermute x5, waiting for transfers between devices: 16.4 us -> 6.53 us  [ys(): lax.ppermute(val, 'dp', [(i, i // n * n + (i + k) % n) for i in range(sel...]
    ppermute x3, waiting for transfers between devices: 0.01 us -> 9.51 us  [zp(): lax.ppermute(val, 'dp', [(i, (i // m ^ 1) * m + i % m) for i in range(sel...]
    pallas_call x6 -> x14, Pallas kernels: 81.7 us -> 72.7 us  [the longest x4 44.3 us: run_weight_grad(): pl.pallas_call(functools.partial(weight_grad_kernel, e, len(xs), ny, hb),...]
    ppermute x18 -> x16, waiting for transfers between devices: 0.05 us -> 8.66 us  [core(): return lax.ppermute(val, 'expert', [(i, i ^ 1) for i in range(self.ne)])]
    slice x14 -> x3, local copies, waits for them, and re-layouts: 7.69 us -> 1.25 us  [the longest x1 0.59 us: on_device(): tiny[:, :hb]]
  transfers between devices with their start and end apart: 49 -> 46, of which waited for: 15 -> 19; matrix products, arithmetic and copies ran while one was open for 11% -> 11% of each run, Pallas kernels for 46% -> 44%
where the time goes in v3:
time: 314 us; the launch traced here: 310 us
  Pallas kernels  137 us (44%)
  waiting for transfers between devices  84.6 us (27%)
  starting transfers between devices  35.4 us (11%)
  local copies, waits for them, and re-layouts  32.6 us (10%)
  other arithmetic  18.7 us (6%)
    pallas_call x2, Pallas kernels, run_experts(): pl.pallas_call(functools.partial(expert_kernel, experts, n_src, slots, mi...  47.6 us
    pallas_call x4, Pallas kernels, run_weight_grad(): pl.pallas_call(functools.partial(weight_grad_kernel, e, len(xs), ny, hb),...  44.3 us
    ppermute x6, waiting for transfers between devices, zs(): lax.ppermute(val, 'dp', [(i, (i // m + k) % n * m + i % m) for i in range...  24.8 us
    pallas_call x4, Pallas kernels, run_backward(): pl.pallas_call(functools.partial(backward_kernel, experts, len(backs)), g...  18.2 us
    ppermute x4, waiting for transfers between devices, zhs(): lax.ppermute(val, 'dp', [(i, ((i // m // 2 + k) % n * 2 + i // m % 2) * m...  17 us
    unnamed x125, local copies, waits for them, and re-layouts  14.3 us
    ppermute x9, waiting for transfers between devices, xs(): lax.ppermute(val, 'expert', [(i, (i // c + k) % n * c + i % c) for i in r...  10.9 us
    convert_element_type x7, other arithmetic, on_device(): add = lambda a, b: (a.astype(F32) + b.astype(F32)).astype(BF)  10.9 us
  transfers between devices with their start and end apart: 46, of which 19 were waited for; matrix products, arithmetic and copies ran while one was open for 11% of the time, Pallas kernels for 44%

profile of v3, /device:TPU:0, one launch (start us, length us, event | category | flops | bytes accessed | tf_op | source)
XLA Modules:
  0.0 310.3 jit_solution(9811690599693364784)
XLA Ops:
  3.2 5.1 %collective-permute-start.2 = (bf16[16,2176]{1,0:T(8,128)(2,1)S(1)}, bf16[16,2176]{1,0:T(8,128)(2,1)S(1)}, u32[]{:S(2)}, u32[]{:S(2)}) collective-permute-start(bf16[16,2176]{1,0:T(8,128)(2,1)S(1)} %pad.13), channel_id=1, source_target_pairs={{0,24},{4,28},{8,0},{12,4},{16,8},{20,12},{24,16},{28,20},{1,25},{... | collective-permute-start | bytes 208904 | tf_op jit(solution)/shard_map/ppermute | solution.py:623
  10.9 4.2 %collective-permute-done.1 = bf16[16,2176]{1,0:T(8,128)(2,1)S(1)} collective-permute-done((bf16[16,2176]{1,0:T(8,128)(2,1)S(1)}, bf16[16,2176]{1,0:T(8,128)(2,1)S(1)}, u32[]{:S(2)}, u32[]{:S(2)}) %collective-permute-start.1) | collective-permute-done | bytes 69664 | tf_op jit(solution)/shard_map/ppermute | solution.py:623
  15.1 2.5 collective-permute-start.5
  25.6 4.9 %collective-permute-done.4 = bf16[64,2176]{1,0:T(8,128)(2,1)S(1)} collective-permute-done((bf16[64,2176]{1,0:T(8,128)(2,1)S(1)}, bf16[64,2176]{1,0:T(8,128)(2,1)S(1)}, u32[]{:S(2)}, u32[]{:S(2)}) %collective-permute-start.4) | collective-permute-done | bytes 278560 | tf_op jit(solution)/shard_map/ppermute | solution.py:644
  35.7 4.9 %dense_forward.2 = (bf16[2,208,1536]{2,1,0:T(8,128)(2,1)S(1)}, bf16[2,208,512]{2,1,0:T(8,128)(2,1)S(1)}, f32[2,208,512]{2,1,0:T(8,128)S(1)}, bf16[2,208,512]{2,1,0:T(8,128)(2,1)S(1)}, f32[2,208,128]{2,1,0:T(8,128)S(1)}) custom-call(bf16[4,208,512]{2,1,0:T(8,128)(2,1)S(1)} %pad.12.tok.refs_0_, bf16[512,2176]{1,0:T(8,128)(2,1)S(1)} %get-tuple-element.154.dense.refs_2_, ...), custom_call_target="tpu_custom_call" | custom-call | flops 1750000000 | bytes 1048576 | tf_op jit(solution)/shard_map/dense_forward/pallas_call | solution.py:119
  45.2 5.5 %dense_forward.3 = (bf16[2,208,1536]{2,1,0:T(8,128)(2,1)S(1)}, bf16[2,208,512]{2,1,0:T(8,128)(2,1)S(1)}, f32[2,208,512]{2,1,0:T(8,128)S(1)}, bf16[2,208,512]{2,1,0:T(8,128)(2,1)}, f32[2,208,128]{2,1,0:T(8,128)S(1)}) custom-call(bf16[4,208,512]{2,1,0:T(8,128)(2,1)S(1)} %pad.12.tok.refs_0_, bf16[512,2176]{1,0:T(8,128)(2,1)S(1)} %get-tuple-element.154.dense.refs_2_, ...), custom_call_target="tpu_custom_call" | custom-call | flops 1750000000 | bytes 1048576 | tf_op jit(solution)/shard_map/dense_forward/pallas_call | solution.py:119
  55.8 7.9 %collective-permute-done.12.refs_0_ = bf16[2,208,512]{2,1,0:T(8,128)(2,1)} collective-permute-done((bf16[2,208,512]{2,1,0:T(8,128)(2,1)S(1)}, bf16[2,208,512]{2,1,0:T(8,128)(2,1)}, u32[]{:S(2)}, u32[]{:S(2)}) %collective-permute-start.12) | collective-permute-done | bytes 426016 | tf_op jit(solution)/shard_map/ppermute | solution.py:627
  68.5 23.6 %experts.2 = (bf16[2,864,512]{2,1,0:T(8,128)(2,1)}, bf16[2,864,512]{2,1,0:T(8,128)(2,1)}, bf16[4,384,512]{2,1,0:T(8,128)(2,1)}, bf16[4,384,512]{2,1,0:T(8,128)(2...) custom-call(s32[1]{0:T(128)} %bitcast.at_ref.ei_ref, bf16[2,208,512]{2,1,0:T(8,128)(2,1)} %copy-done.14, ...), custom_call_target="tpu_custom_call" | custom-call | flops 8400000000 | bytes 1048576 | tf_op jit(solution)/shard_map/experts/pallas_call | solution.py:243
  92.1 2.6 collective-permute-done.16.refs_2_
  96.3 3.7 %collective-permute-done.19.refs_3_ = bf16[2,208,512]{2,1,0:T(8,128)(2,1)} collective-permute-done((bf16[2,208,512]{2,1,0:T(8,128)(2,1)}, bf16[2,208,512]{2,1,0:T(8,128)(2,1)}, u32[]{:S(2)}, u32[]{:S(2)}) %collective-permute-start.19) | collective-permute-done | bytes 426016 | tf_op jit(solution)/shard_map/ppermute | solution.py:611
  100.5 24.0 %experts.3 = (bf16[2,864,512]{2,1,0:T(8,128)(2,1)}, bf16[2,864,512]{2,1,0:T(8,128)(2,1)}, bf16[4,384,512]{2,1,0:T(8,128)(2,1)}, bf16[4,384,512]{2,1,0:T(8,128)(2...) custom-call(s32[1]{0:T(128)} %bitcast.at_ref.ei_ref, bf16[2,208,512]{2,1,0:T(8,128)(2,1)} %get-tuple-element.159.refs_0_.refs_6_, ...), custom_call_target="tpu_custom_call" | custom-call | flops 8400000000 | bytes 1048576 | tf_op jit(solution)/shard_map/experts/pallas_call | solution.py:243
  125.7 3.4 %collective-permute-done.28.refs_1_ = bf16[2,208,512]{2,1,0:T(8,128)(2,1)S(1)} collective-permute-done((bf16[2,208,512]{2,1,0:T(8,128)(2,1)}, bf16[2,208,512]{2,1,0:T(8,128)(2,1)S(1)}, u32[]{:S(2)}, u32[]{:S(2)}) %collective-permute-start.28) | collective-permute-done | bytes 426016 | tf_op jit(solution)/shard_map/ppermute | solution.py:611
  129.8 2.7 pick_rows.3
  132.5 2.7 pick_rows.2
  135.4 10.7 %weight_grad.4 = (bf16[2,2,256,512]{3,2,1,0:T(8,128)(2,1)S(1)}, bf16[2,2,256,512]{3,2,1,0:T(8,128)(2,1)S(1)}) custom-call(s32[3]{0:T(128)S(1)} %pad_add_fusion.own_ref, bf16[4,384,512]{2,1,0:T(8,128)(2,1)S(1)} %copy-done, bf16[4,384,512]{2,1,0:T(8,128)(2,1)S(1)} %copy-done.2, bf16[4,384,512]{2,1,0:T(8,128)(2,1)S(1)} %get-tuple-element.175.refs_2_, ...), custom_call_target="tpu_custom_call" | custom-call | flops 350000000 | bytes 1048576 | tf_op jit(solution)/shard_map/weight_grad/pallas_call | solution.py:342
  153.5 10.5 %weight_grad.5 = (bf16[2,2,256,512]{3,2,1,0:T(8,128)(2,1)S(1)}, bf16[2,2,256,512]{3,2,1,0:T(8,128)(2,1)S(1)}) custom-call(s32[3]{0:T(128)S(1)} %pad_add_fusion.own_ref, bf16[4,384,512]{2,1,0:T(8,128)(2,1)S(1)} %copy-done, bf16[4,384,512]{2,1,0:T(8,128)(2,1)S(1)} %copy-done.2, bf16[4,384,512]{2,1,0:T(8,128)(2,1)S(1)} %get-tuple-element.175.refs_2_, ...), custom_call_target="tpu_custom_call" | custom-call | flops 350000000 | bytes 1048576 | tf_op jit(solution)/shard_map/weight_grad/pallas_call | solution.py:342
  164.0 8.3 %collective-permute-done.30.refs_9_.refs_11_.refs_13_ = bf16[864,512]{1,0:T(8,128)(2,1)S(1)} collective-permute-done((bf16[864,512]{1,0:T(8,128)(2,1)S(1)}, bf16[864,512]{1,0:T(8,128)(2,1)S(1)}, u32[]{:S(2)}, u32[]{:S(2)}) %collective-permute-start.30) | collective-permute-done | bytes 884768 | tf_op jit(solution)/shard_map/ppermute | solution.py:615
  172.4 4.1 %dense_backward.5 = (bf16[1,208,512]{2,1,0:T(8,128)(2,1)S(1)}, f32[1,208,512]{2,1,0:T(8,128)S(1)}, bf16[1,208,512]{2,1,0:T(8,128)(2,1)S(1)}, bf16[1,208,512]{2,1...) custom-call(bf16[4,208,512]{2,1,0:T(8,128)(2,1)S(1)} %pad.12.tok.refs_0_, ...), custom_call_target="tpu_custom_call" | custom-call | flops 350000000 | bytes 1048576 | tf_op jit(solution)/shard_map/dense_backward/pallas_call | solution.py:451
  177.2 4.1 %dense_backward.4 = (bf16[1,208,512]{2,1,0:T(8,128)(2,1)S(1)}, f32[1,208,512]{2,1,0:T(8,128)S(1)}, bf16[1,208,512]{2,1,0:T(8,128)(2,1)S(1)}, bf16[1,208,512]{2,1...) custom-call(bf16[4,208,512]{2,1,0:T(8,128)(2,1)S(1)} %pad.12.tok.refs_0_, ...), custom_call_target="tpu_custom_call" | custom-call | flops 350000000 | bytes 1048576 | tf_op jit(solution)/shard_map/dense_backward/pallas_call | solution.py:451
  186.0 11.5 %weight_grad.6 = (bf16[2,2,256,512]{3,2,1,0:T(8,128)(2,1)S(1)}, bf16[2,2,256,512]{3,2,1,0:T(8,128)(2,1)}) custom-call(s32[3]{0:T(128)S(1)} %pad_add_fusion.own_ref, bf16[4,384,512]{2,1,0:T(8,128)(2,1)S(1)} %copy-done, bf16[4,384,512]{2,1,0:T(8,128)(2,1)S(1)} %copy-done.2, bf16[4,384,512]{2,1,0:T(8,128)(2,1)S(1)} %get-tuple-element.175.refs_2_, ...), custom_call_target="tpu_custom_call" | custom-call | flops 350000000 | bytes 1048576 | tf_op jit(solution)/shard_map/weight_grad/pallas_call | solution.py:342
  197.6 5.0 %dense_backward.7 = (bf16[1,208,512]{2,1,0:T(8,128)(2,1)S(1)}, f32[1,208,512]{2,1,0:T(8,128)S(1)}, bf16[1,208,512]{2,1,0:T(8,128)(2,1)S(1)}, bf16[1,208,512]{2,1...) custom-call(bf16[4,208,512]{2,1,0:T(8,128)(2,1)S(1)} %pad.12.tok.refs_0_, ...), custom_call_target="tpu_custom_call" | custom-call | flops 350000000 | bytes 1048576 | tf_op jit(solution)/shard_map/dense_backward/pallas_call | solution.py:451
  203.3 5.1 %dense_backward.6 = (bf16[1,208,512]{2,1,0:T(8,128)(2,1)S(1)}, f32[1,208,512]{2,1,0:T(8,128)S(1)}, bf16[1,208,512]{2,1,0:T(8,128)(2,1)S(1)}, bf16[1,208,512]{2,1...) custom-call(bf16[4,208,512]{2,1,0:T(8,128)(2,1)S(1)} %pad.12.tok.refs_0_, ...), custom_call_target="tpu_custom_call" | custom-call | flops 350000000 | bytes 1048576 | tf_op jit(solution)/shard_map/dense_backward/pallas_call | solution.py:451
  213.3 3.6 %dense_grads.1 = (bf16[256,2176]{1,0:T(8,128)(2,1)S(1)}, bf16[256,2176]{1,0:T(8,128)(2,1)}) custom-call(s32[1]{0:T(128)} %bitcast.42.core_ref, bf16[1,208,512]{2,1,0:T(8,128)(2,1)S(1)} %get-tuple-element.199.refs_0_, bf16[1,208,512]{2,1,0:T(8,128)(2,1)S(1)} %get-tuple-element.204.refs_1_, bf16[1,208,512]{2,1,0:T(8,128)(2,1)S(1)} %get-tuple-element.216.refs_2_, ...), custom_call_target="tpu_custom_call" | custom-call | flops 350000000 | bytes 1048576 | tf_op jit(solution)/shard_map/dense_grads/pallas_call | solution.py:499
  216.9 11.6 %weight_grad.7 = (bf16[2,2,256,512]{3,2,1,0:T(8,128)(2,1)S(1)}, bf16[2,2,256,512]{3,2,1,0:T(8,128)(2,1)}) custom-call(s32[3]{0:T(128)S(1)} %pad_add_fusion.own_ref, bf16[4,384,512]{2,1,0:T(8,128)(2,1)S(1)} %copy-done, bf16[4,384,512]{2,1,0:T(8,128)(2,1)S(1)} %copy-done.2, bf16[4,384,512]{2,1,0:T(8,128)(2,1)S(1)} %get-tuple-element.175.refs_2_, ...), custom_call_target="tpu_custom_call" | custom-call | flops 350000000 | bytes 1048576 | tf_op jit(solution)/shard_map/weight_grad/pallas_call | solution.py:342
  228.5 5.1 %collective-permute-done.35 = bf16[2,2,256,512]{3,2,1,0:T(8,128)(2,1)S(1)} collective-permute-done((bf16[2,2,256,512]{3,2,1,0:T(8,128)(2,1)}, bf16[2,2,256,512]{3,2,1,0:T(8,128)(2,1)S(1)}, u32[]{:S(2)}, u32[]{:S(2)}) %collective-permute-start.35) | collective-permute-done | bytes 1048608 | tf_op jit(solution)/shard_map/ppermute | solution.py:619
  235.8 2.1 slice_bitcast_fusion.6
  247.3 17.0 %collective-permute-done.45.refs_1_ = bf16[2,256,512]{2,1,0:T(8,128)(2,1)} collective-permute-done((bf16[2,256,512]{2,1,0:T(8,128)(2,1)}, bf16[2,256,512]{2,1,0:T(8,128)(2,1)}, u32[]{:S(2)}, u32[]{:S(2)}) %collective-permute-start.45) | collective-permute-done | bytes 524320 | tf_op jit(solution)/shard_map/ppermute | solution.py:631
  264.2 2.2 store_expert.6
  266.5 2.5 add_convert_fusion.3
  276.0 2.9 reshape.77
  285.6 3.2 %collective-permute-done.42.refs_3_ = bf16[16,2176]{1,0:T(8,128)(2,1)S(1)} collective-permute-done((bf16[16,2176]{1,0:T(8,128)(2,1)S(1)}, bf16[16,2176]{1,0:T(8,128)(2,1)S(1)}, u32[]{:S(2)}, u32[]{:S(2)}) %collective-permute-start.42) | collective-permute-done | bytes 69664 | tf_op jit(solution)/shard_map/ppermute | solution.py:623
  288.8 16.9 %collective-permute-done.41.refs_2_ = bf16[16,2176]{1,0:T(8,128)(2,1)S(1)} collective-permute-done((bf16[16,2176]{1,0:T(8,128)(2,1)S(1)}, bf16[16,2176]{1,0:T(8,128)(2,1)S(1)}, u32[]{:S(2)}, u32[]{:S(2)}) %collective-permute-start.41) | collective-permute-done | bytes 69664 | tf_op jit(solution)/shard_map/ppermute | solution.py:623
  (260 shorter events, 84.4 us)
Async XLA Ops:
  15.1 10.5 %collective-permute-start.5 = (bf16[64,2176]{1,0:T(8,128)(2,1)S(1)}, bf16[64,2176]{1,0:T(8,128)(2,1)S(1)}, u32[]{:S(2)}, u32[]{:S(2)}) collective-permute-start(bf16[64,2176]{1,0:T(8,128)(2,1)S(1)} %pad_maximum_fusion.7), channel_id=1, source_target_pairs={{0,6},{1,7},{2,4},{3,5},{4,2},{5,3},{6,0},{7,1},{8,14},{9,15},{10,... | collective-permute-start | bytes 835592 | tf_op jit(solution)/shard_map/ppermute | solution.py:644
  17.6 12.9 %collective-permute-start.4 = (bf16[64,2176]{1,0:T(8,128)(2,1)S(1)}, bf16[64,2176]{1,0:T(8,128)(2,1)S(1)}, u32[]{:S(2)}, u32[]{:S(2)}) collective-permute-start(bf16[64,2176]{1,0:T(8,128)(2,1)S(1)} %pad_maximum_fusion.7), channel_id=1, source_target_pairs={{0,4},{1,5},{2,6},{3,7},{4,0},{5,1},{6,2},{7,3},{8,12},{9,13},{10,... | collective-permute-start | bytes 835592 | tf_op jit(solution)/shard_map/ppermute | solution.py:644
  18.1 12.6 %collective-permute-start.3 = (bf16[64,2176]{1,0:T(8,128)(2,1)S(1)}, bf16[64,2176]{1,0:T(8,128)(2,1)}, u32[]{:S(2)}, u32[]{:S(2)}) collective-permute-start(bf16[64,2176]{1,0:T(8,128)(2,1)S(1)} %pad_maximum_fusion.7), channel_id=1, source_target_pairs={{0,2},{1,3},{2,0},{3,1},{4,6},{5,7},{6,4},{7,5},{8,10},{9,11},{10,... | collective-permute-start | bytes 835592 | tf_op jit(solution)/shard_map/ppermute | solution.py:644
  31.8 11.5 %collective-permute-start.7 = (bf16[4,208,512]{2,1,0:T(8,128)(2,1)S(1)}, bf16[4,208,512]{2,1,0:T(8,128)(2,1)S(1)}, u32[]{:S(2)}, u32[]{:S(2)}) collective-permute-start(bf16[4,208,512]{2,1,0:T(8,128)(2,1)S(1)} %maximum_maximum_fusion.refs_4_.refs_1_), channel_id=1, source_target_pairs={{0,1},{1,0},{2,3},{3,2},{4,5},{5,4},{6,7},{7,6},{8,9},{9,8},{10,11... | collective-permute-start | bytes 2555912 | tf_op jit(solution)/shard_map/ppermute | solution.py:611
  32.3 21.9 %collective-permute-start.11 = (bf16[4,208,512]{2,1,0:T(8,128)(2,1)S(1)}, bf16[4,208,512]{2,1,0:T(8,128)(2,1)S(1)}, u32[]{:S(2)}, u32[]{:S(2)}) collective-permute-start(bf16[4,208,512]{2,1,0:T(8,128)(2,1)S(1)} %maximum_maximum_fusion.refs_4_.refs_1_), channel_id=1, source_target_pairs={{0,2},{1,3},{2,0},{3,1},{4,6},{5,7},{6,4},{7,5},{8,10},{9,11},{10,... | collective-permute-start | bytes 2555912 | tf_op jit(solution)/shard_map/ppermute | solution.py:615
  33.8 21.9 %collective-permute-start.10 = (bf16[4,208,512]{2,1,0:T(8,128)(2,1)S(1)}, bf16[4,208,512]{2,1,0:T(8,128)(2,1)}, u32[]{:S(2)}, u32[]{:S(2)}) collective-permute-start(bf16[4,208,512]{2,1,0:T(8,128)(2,1)S(1)} %maximum_maximum_fusion.refs_4_.refs_1_), channel_id=1, source_target_pairs={{0,8},{4,12},{8,0},{12,4},{16,24},{20,28},{24,16},{28,20},{1,9},{5... | collective-permute-start | bytes 2555912 | tf_op jit(solution)/shard_map/ppermute | solution.py:627
  43.3 20.4 %collective-permute-start.12 = (bf16[2,208,512]{2,1,0:T(8,128)(2,1)S(1)}, bf16[2,208,512]{2,1,0:T(8,128)(2,1)}, u32[]{:S(2)}, u32[]{:S(2)}) collective-permute-start(bf16[2,208,512]{2,1,0:T(8,128)(2,1)S(1)} %get-tuple-element.153.refs_0_.refs_6_), channel_id=1, source_target_pairs={{0,8},{4,12},{8,0},{12,4},{16,24},{20,28},{24,16},{28,20},{1,9},{5... | collective-permute-start | bytes 1277960 | tf_op jit(solution)/shard_map/ppermute | solution.py:627
  44.7 19.1 %collective-permute-start.9 = (bf16[2,208,512]{2,1,0:T(8,128)(2,1)S(1)}, bf16[2,208,512]{2,1,0:T(8,128)(2,1)S(1)}, u32[]{:S(2)}, u32[]{:S(2)}) collective-permute-start(bf16[2,208,512]{2,1,0:T(8,128)(2,1)S(1)} %get-tuple-element.153.refs_0_.refs_6_), channel_id=1, source_target_pairs={{0,2},{1,3},{2,0},{3,1},{4,6},{5,7},{6,4},{7,5},{8,10},{9,11},{10,... | collective-permute-start | bytes 1277960 | tf_op jit(solution)/shard_map/ppermute | solution.py:615
  45.2 18.5 %collective-permute-start.8 = (bf16[2,208,512]{2,1,0:T(8,128)(2,1)S(1)}, bf16[2,208,512]{2,1,0:T(8,128)(2,1)S(1)}, u32[]{:S(2)}, u32[]{:S(2)}) collective-permute-start(bf16[2,208,512]{2,1,0:T(8,128)(2,1)S(1)} %get-tuple-element.153.refs_0_.refs_6_), channel_id=1, source_target_pairs={{0,1},{1,0},{2,3},{3,2},{4,5},{5,4},{6,7},{7,6},{8,9},{9,8},{10,11... | collective-permute-start | bytes 1277960 | tf_op jit(solution)/shard_map/ppermute | solution.py:611
  64.3 30.4 %collective-permute-start.17 = (bf16[4,208,512]{2,1,0:T(8,128)(2,1)}, bf16[4,208,512]{2,1,0:T(8,128)(2,1)S(1)}, u32[]{:S(2)}, u32[]{:S(2)}) collective-permute-start(bf16[4,208,512]{2,1,0:T(8,128)(2,1)} %collective-permute-done.10.refs_4_), channel_id=1, source_target_pairs={{0,2},{1,3},{2,0},{3,1},{4,6},{5,7},{6,4},{7,5},{8,10},{9,11},{10,... | collective-permute-start | bytes 2555912 | tf_op jit(solution)/shard_map/ppermute | solution.py:615
  64.9 27.2 %collective-permute-start.18 = (bf16[2,208,512]{2,1,0:T(8,128)(2,1)}, bf16[2,208,512]{2,1,0:T(8,128)(2,1)}, u32[]{:S(2)}, u32[]{:S(2)}) collective-permute-start(bf16[2,208,512]{2,1,0:T(8,128)(2,1)} %get-tuple-element.159.refs_0_.refs_6_), channel_id=1, source_target_pairs={{0,8},{4,12},{8,0},{12,4},{16,24},{20,28},{24,16},{28,20},{1,9},{5... | collective-permute-start | bytes 1277960 | tf_op jit(solution)/shard_map/ppermute | solution.py:627
  65.1 29.6 %collective-permute-start.16 = (bf16[2,208,512]{2,1,0:T(8,128)(2,1)}, bf16[2,208,512]{2,1,0:T(8,128)(2,1)}, u32[]{:S(2)}, u32[]{:S(2)}) collective-permute-start(bf16[2,208,512]{2,1,0:T(8,128)(2,1)} %get-tuple-element.159.refs_0_.refs_6_), channel_id=1, source_target_pairs={{0,2},{1,3},{2,0},{3,1},{4,6},{5,7},{6,4},{7,5},{8,10},{9,11},{10,... | collective-permute-start | bytes 1277960 | tf_op jit(solution)/shard_map/ppermute | solution.py:615
  66.8 27.9 %collective-permute-start.15 = (bf16[2,208,512]{2,1,0:T(8,128)(2,1)}, bf16[2,208,512]{2,1,0:T(8,128)(2,1)}, u32[]{:S(2)}, u32[]{:S(2)}) collective-permute-start(bf16[2,208,512]{2,1,0:T(8,128)(2,1)} %get-tuple-element.159.refs_0_.refs_6_), channel_id=1, source_target_pairs={{0,1},{1,0},{2,3},{3,2},{4,5},{5,4},{6,7},{7,6},{8,9},{9,8},{10,11... | collective-permute-start | bytes 1277960 | tf_op jit(solution)/shard_map/ppermute | solution.py:611
  94.7 29.9 %collective-permute-start.24 = (bf16[2,864,512]{2,1,0:T(8,128)(2,1)}, bf16[2,864,512]{2,1,0:T(8,128)(2,1)}, u32[]{:S(2)}, u32[]{:S(2)}) collective-permute-start(bf16[2,864,512]{2,1,0:T(8,128)(2,1)} %get-tuple-element.170), channel_id=1, source_target_pairs={{0,1},{1,0},{2,3},{3,2},{4,5},{5,4},{6,7},{7,6},{8,9},{9,8},{10,11... | collective-permute-start | bytes 5308424 | tf_op jit(solution)/shard_map/ppermute | solution.py:611
  95.2 29.3 %collective-permute-start.22 = (bf16[4,208,512]{2,1,0:T(8,128)(2,1)}, bf16[4,208,512]{2,1,0:T(8,128)(2,1)}, u32[]{:S(2)}, u32[]{:S(2)}) collective-permute-start(bf16[4,208,512]{2,1,0:T(8,128)(2,1)} %collective-permute-done.10.refs_4_), channel_id=1, source_target_pairs={{0,1},{1,0},{2,3},{3,2},{4,5},{5,4},{6,7},{7,6},{8,9},{9,8},{10,11... | collective-permute-start | bytes 2555912 | tf_op jit(solution)/shard_map/ppermute | solution.py:611
  95.3 29.3 %collective-permute-start.23 = (bf16[4,208,512]{2,1,0:T(8,128)(2,1)S(1)}, bf16[4,208,512]{2,1,0:T(8,128)(2,1)}, u32[]{:S(2)}, u32[]{:S(2)}) collective-permute-start(bf16[4,208,512]{2,1,0:T(8,128)(2,1)S(1)} %collective-permute-done.17.refs_6_), channel_id=1, source_target_pairs={{0,1},{1,0},{2,3},{3,2},{4,5},{5,4},{6,7},{7,6},{8,9},{9,8},{10,11... | collective-permute-start | bytes 2555912 | tf_op jit(solution)/shard_map/ppermute | solution.py:611
  95.7 28.8 %collective-permute-start.20 = (bf16[2,208,512]{2,1,0:T(8,128)(2,1)}, bf16[2,208,512]{2,1,0:T(8,128)(2,1)}, u32[]{:S(2)}, u32[]{:S(2)}) collective-permute-start(bf16[2,208,512]{2,1,0:T(8,128)(2,1)} %collective-permute-done.12.refs_0_), channel_id=1, source_target_pairs={{0,2},{1,3},{2,0},{3,1},{4,6},{5,7},{6,4},{7,5},{8,10},{9,11},{10,... | collective-permute-start | bytes 1277960 | tf_op jit(solution)/shard_map/ppermute | solution.py:615
  100.0 24.6 %collective-permute-start.21 = (bf16[2,208,512]{2,1,0:T(8,128)(2,1)}, bf16[2,208,512]{2,1,0:T(8,128)(2,1)}, u32[]{:S(2)}, u32[]{:S(2)}) collective-permute-start(bf16[2,208,512]{2,1,0:T(8,128)(2,1)} %collective-permute-done.18.refs_0_), channel_id=1, source_target_pairs={{0,2},{1,3},{2,0},{3,1},{4,6},{5,7},{6,4},{7,5},{8,10},{9,11},{10,... | collective-permute-start | bytes 1277960 | tf_op jit(solution)/shard_map/ppermute | solution.py:615
  124.6 23.6 %collective-permute-start.25 = (bf16[2,864,512]{2,1,0:T(8,128)(2,1)}, bf16[2,864,512]{2,1,0:T(8,128)(2,1)S(1)}, u32[]{:S(2)}, u32[]{:S(2)}) collective-permute-start(bf16[2,864,512]{2,1,0:T(8,128)(2,1)} %get-tuple-element.171), channel_id=1, source_target_pairs={{0,1},{1,0},{2,3},{3,2},{4,5},{5,4},{6,7},{7,6},{8,9},{9,8},{10,11... | collective-permute-start | bytes 5308424 | tf_op jit(solution)/shard_map/ppermute | solution.py:611
  148.2 33.2 %collective-permute-start.31 = (bf16[2,2,256,512]{3,2,1,0:T(8,128)(2,1)S(1)}, bf16[2,2,256,512]{3,2,1,0:T(8,128)(2,1)}, u32[]{:S(2)}, u32[]{:S(2)}) collective-permute-start(bf16[2,2,256,512]{3,2,1,0:T(8,128)(2,1)S(1)} %get-tuple-element.196), channel_id=1, source_target_pairs={{0,4},{4,0},{8,12},{12,8},{16,20},{20,16},{24,28},{28,24},{1,5},{5... | collective-permute-start | bytes 3145736 | tf_op jit(solution)/shard_map/ppermute | solution.py:619
  149.7 22.6 %collective-permute-start.30 = (bf16[864,512]{1,0:T(8,128)(2,1)S(1)}, bf16[864,512]{1,0:T(8,128)(2,1)S(1)}, u32[]{:S(2)}, u32[]{:S(2)}) collective-permute-start(bf16[864,512]{1,0:T(8,128)(2,1)S(1)} %get-tuple-element.306), channel_id=1, source_target_pairs={{0,2},{1,3},{2,0},{3,1},{4,6},{5,7},{6,4},{7,5},{8,10},{9,11},{10,... | collective-permute-start | bytes 2654216 | tf_op jit(solution)/shard_map/ppermute | solution.py:615
  152.2 45.4 %collective-permute-start.32 = (bf16[864,512]{1,0:T(8,128)(2,1)}, bf16[864,512]{1,0:T(8,128)(2,1)S(1)}, u32[]{:S(2)}, u32[]{:S(2)}) collective-permute-start(bf16[864,512]{1,0:T(8,128)(2,1)} %get-tuple-element.213), channel_id=1, source_target_pairs={{0,2},{1,3},{2,0},{3,1},{4,6},{5,7},{6,4},{7,5},{8,10},{9,11},{10,... | collective-permute-start | bytes 2654216 | tf_op jit(solution)/shard_map/ppermute | solution.py:615
  181.4 27.1 %collective-permute-start.33 = (bf16[2,2,256,512]{3,2,1,0:T(8,128)(2,1)S(1)}, bf16[2,2,256,512]{3,2,1,0:T(8,128)(2,1)}, u32[]{:S(2)}, u32[]{:S(2)}) collective-permute-start(bf16[2,2,256,512]{3,2,1,0:T(8,128)(2,1)S(1)} %get-tuple-element.231), channel_id=1, source_target_pairs={{0,4},{4,0},{8,12},{12,8},{16,20},{20,16},{24,28},{28,24},{1,5},{5... | collective-permute-start | bytes 3145736 | tf_op jit(solution)/shard_map/ppermute | solution.py:619
  184.7 23.8 %collective-permute-start.34 = (bf16[2,256,512]{2,1,0:T(8,128)(2,1)}, bf16[2,256,512]{2,1,0:T(8,128)(2,1)S(1)}, u32[]{:S(2)}, u32[]{:S(2)}) collective-permute-start(bf16[2,256,512]{2,1,0:T(8,128)(2,1)} %get-tuple-element.313), channel_id=1, source_target_pairs={{0,16},{4,20},{8,24},{12,28},{16,0},{20,4},{24,8},{28,12},{1,17},{... | collective-permute-start | bytes 1572872 | tf_op jit(solution)/shard_map/ppermute | solution.py:631
  208.5 25.1 %collective-permute-start.35 = (bf16[2,2,256,512]{3,2,1,0:T(8,128)(2,1)}, bf16[2,2,256,512]{3,2,1,0:T(8,128)(2,1)S(1)}, u32[]{:S(2)}, u32[]{:S(2)}) collective-permute-start(bf16[2,2,256,512]{3,2,1,0:T(8,128)(2,1)} %get-tuple-element.235), channel_id=1, source_target_pairs={{0,4},{4,0},{8,12},{12,8},{16,20},{20,16},{24,28},{28,24},{1,5},{5... | collective-permute-start | bytes 3145736 | tf_op jit(solution)/shard_map/ppermute | solution.py:619
  211.5 23.3 %collective-permute-start.36 = (bf16[2,256,512]{2,1,0:T(8,128)(2,1)S(1)}, bf16[2,256,512]{2,1,0:T(8,128)(2,1)S(1)}, u32[]{:S(2)}, u32[]{:S(2)}) collective-permute-start(bf16[2,256,512]{2,1,0:T(8,128)(2,1)S(1)} %get-tuple-element.315), channel_id=1, source_target_pairs={{0,16},{4,20},{8,24},{12,28},{16,0},{20,4},{24,8},{28,12},{1,17},{... | collective-permute-start | bytes 1572872 | tf_op jit(solution)/shard_map/ppermute | solution.py:631
  237.9 26.4 %collective-permute-start.45 = (bf16[2,256,512]{2,1,0:T(8,128)(2,1)}, bf16[2,256,512]{2,1,0:T(8,128)(2,1)}, u32[]{:S(2)}, u32[]{:S(2)}) collective-permute-start(bf16[2,256,512]{2,1,0:T(8,128)(2,1)} %get-tuple-element.316), channel_id=1, source_target_pairs={{0,16},{4,20},{8,24},{12,28},{16,0},{20,4},{24,8},{28,12},{1,17},{... | collective-permute-start | bytes 1572872 | tf_op jit(solution)/shard_map/ppermute | solution.py:631
  237.9 28.6 %collective-permute-start.43 = (bf16[2,2,256,512]{3,2,1,0:T(8,128)(2,1)}, bf16[2,2,256,512]{3,2,1,0:T(8,128)(2,1)}, u32[]{:S(2)}, u32[]{:S(2)}) collective-permute-start(bf16[2,2,256,512]{3,2,1,0:T(8,128)(2,1)} %get-tuple-element.261), channel_id=1, source_target_pairs={{0,4},{4,0},{8,12},{12,8},{16,20},{20,16},{24,28},{28,24},{1,5},{5... | collective-permute-start | bytes 3145736 | tf_op jit(solution)/shard_map/ppermute | solution.py:619
  242.5 26.5 %collective-permute-start.38 = (bf16[4,2,16,2176]{3,2,0,1:T(8,128)(2,1)}, bf16[4,2,16,2176]{3,2,0,1:T(8,128)(2,1)}, u32[]{:S(2)}, u32[]{:S(2)}) collective-permute-start(bf16[4,2,16,2176]{3,2,0,1:T(8,128)(2,1)} %bitcast.95), channel_id=1, source_target_pairs={{0,2},{1,3},{2,0},{3,1},{4,6},{5,7},{6,4},{7,5},{8,10},{9,11},{10,... | collective-permute-start | bytes 1671176 | tf_op jit(solution)/shard_map/ppermute | solution.py:615
  274.1 34.2 %collective-permute-start.44 = (bf16[2,256,512]{2,1,0:T(8,128)(2,1)}, bf16[2,256,512]{2,1,0:T(8,128)(2,1)S(1)}, u32[]{:S(2)}, u32[]{:S(2)}) collective-permute-start(bf16[2,256,512]{2,1,0:T(8,128)(2,1)} %get-tuple-element.318), channel_id=1, source_target_pairs={{0,16},{4,20},{8,24},{12,28},{16,0},{20,4},{24,8},{28,12},{1,17},{... | collective-permute-start | bytes 1572872 | tf_op jit(solution)/shard_map/ppermute | solution.py:631
  283.0 22.7 %collective-permute-start.41 = (bf16[16,2176]{1,0:T(8,128)(2,1)S(1)}, bf16[16,2176]{1,0:T(8,128)(2,1)S(1)}, u32[]{:S(2)}, u32[]{:S(2)}) collective-permute-start(bf16[16,2176]{1,0:T(8,128)(2,1)S(1)} %get-tuple-element.321), channel_id=1, source_target_pairs={{0,16},{4,20},{8,24},{12,28},{16,0},{20,4},{24,8},{28,12},{1,17},{... | collective-permute-start | bytes 208904 | tf_op jit(solution)/shard_map/ppermute | solution.py:623
  283.7 21.9 %collective-permute-start.40 = (bf16[16,2176]{1,0:T(8,128)(2,1)S(1)}, bf16[16,2176]{1,0:T(8,128)(2,1)S(1)}, u32[]{:S(2)}, u32[]{:S(2)}) collective-permute-start(bf16[16,2176]{1,0:T(8,128)(2,1)S(1)} %get-tuple-element.322), channel_id=1, source_target_pairs={{0,8},{4,12},{8,16},{12,20},{16,24},{20,28},{24,0},{28,4},{1,9},{5... | collective-permute-start | bytes 208904 | tf_op jit(solution)/shard_map/ppermute | solution.py:623
  (74 other events, 440.6 us)

commit v4 on v3

--- a/solution.py
+++ b/solution.py
@@ -302,7 +302,7 @@
         grid_spec=pltpu.PrefetchScalarGridSpec(
             num_scalar_prefetch=1,
             grid=(1,),
-            in_specs=[half(0)] * n_src + [half(part)] * n_src,
+            in_specs=[half(part)] * (2 * n_src),
             out_specs=[keep] * 2,
         ),
         out_shape=[jax.ShapeDtypeStruct((local, rows, width), BF)] * 2,
@@ -749,23 +749,22 @@
     other = place.core(dense_near)
     dy_mine, dy_z, dy_other = across(dy), place.zp(dy), place.core(dy)
     dense, tailt = dense_in_order(place, dense_near, other, order, share)
-    saved, act_x, act_z, act_c = [], [], [], []
+    saved, act_x, act_c = [], [], []
     saved.append(run_forward(tok, dense, tailt, 0, experts))
     done = [saved[0][3], dy_other]
 
     for h in halves[1:]:
         act, dense_h = after(done, saved[-1][3], dense)
         act_x.append(across(act))
-        act_z.append(place.zp(act))
         act_c.append(place.core(act))
         saved.append(run_forward(tok, dense_h, tailt, h, experts))
-        done = [*act_x[-1], act_z[-1], act_c[-1], saved[-1][3], dy_z, *dy_mine]
+        done = [*act_x[-1], act_c[-1], saved[-1][3], dy_z, *dy_mine]
 
     act, far_dy, *rest = after(done, saved[-1][3], dy_z, *act_x[0][1:], *dy_mine[1:])
     dy_near = both_cores(dy_mine, [dy_other, *[place.core(v) for v in rest[nx - 1 :]]])
     rest = rest[: nx - 1]
     act_x.append(across(act))
-    act_z.append(place.zp(act))
+    act_z = place.zp(jnp.concatenate([*[v[0] for v in act_x[:-1]], act], axis=0))
     act_c.append(place.core(act))
     dy_far = across(far_dy)
     near = both_cores(act_x[0], [act_c[0], *[place.core(v) for v in rest]])
@@ -774,46 +773,41 @@
         for at in range(0, len(near), 4)
     ]
     results = [visit(0, near)]
-    done = [*act_x[-1], *act_z, act_c[-1], *dy_far]
+    done = [*act_x[-1], act_z, act_c[-1], *dy_far]
     done += [r[0] for r in results[0]]
 
     n_far = len(dy_far)
-    vals = after(done, *dy_far, *act_z, *act_x[1][1:], *[r[1] for r in results[0]])
+    vals = after(done, *dy_far, act_z, *act_x[1][1:], *[r[1] for r in results[0]])
     dy_far = both_cores(vals[:n_far], [place.core(v) for v in vals[:n_far]])
-    far = [across(v) for v in vals[n_far : n_far + 2]]
-    rest = vals[n_far + 2 :]
+    far = across(vals[n_far])
+    rest = vals[n_far + 1 :]
     near = both_cores(act_x[1], [act_c[1], *[place.core(v) for v in rest[: nx - 1]]])
     back = [[place.core(v) for v in rest[nx - 1 :]]]
     results.append(visit(1, near))
-    done = [*dy_far, *[v for f in far for v in f], *back[0], *[r[0] for r in results[1]]]
+    done = [*dy_far, *far, *back[0], *[r[0] for r in results[1]]]
 
     add = lambda a, b: (a.astype(F32) + b.astype(F32)).astype(BF)
     pairs_of = lambda h: [
-        p[k] for p in [add(r[0], b) for r, b in zip(results[h], back[h])] for k in range(p.shape[0])
+        add(r[0][k], b[k]) for r, b in zip(results[h], back[h]) for k in range(b.shape[0])
     ]
     home = lambda p: [p[0]] + [place.xs(p[k], nx - k) for k in range(1, nx)]
-    n_all = 2 * n_far
-    vals = after(done, *[v for f in far for v in f], *[r[1] for r in results[1]])
-    far = [vals[:n_far], vals[n_far:n_all]]
-    far = [both_cores(f, [place.core(v) for v in f]) for f in far]
-    back.append([place.core(v) for v in vals[n_all : n_all + len(results[1])]])
+    backs = [home(pairs_of(0))]
+    vals = after(done, *far, *[r[1] for r in results[1]])
+    far = both_cores(vals[:n_far], [place.core(v) for v in vals[:n_far]])
+    back.append([place.core(v) for v in vals[n_far:]])
     xs, gs = [[r[k] for rs in results for r in rs] for k in (2, 3)]
     for h in halves:
-        src = list(zip(far[h], dy_far))
+        src = list(zip(far, dy_far))
         for at in range(0, len(src), 4):
             x, g = run_pick(place, h, src[at : at + 4], local, experts, slots)
             xs.append(x)
             gs.append(g)
-    for rs in results[:1]:
-        near_sent = after(xs[2 * len(rs) :], *[r[0] for r in rs])
-        results[0] = [(v, *r[1:]) for v, r in zip(near_sent, rs)]
-    backs = [home(pairs_of(0))]
     weights = lambda e, x: run_weight_grad(place, where, e, [x, *xs[1:]], gs, w_up, bu3, w_down)
     tokens_back = lambda i, d, v: run_backward(
         i, v, d, dense, tailt, saved[i // HALF], backs[i // HALF], experts
     )
     sent = weights(0, xs[0])
-    done = [*back[1], *sent]
+    done = [*back[1], *backs[0], *sent]
 
     sent = list(after(done, *sent))
     x, grads, rows_in, *pairs = after(done, xs[0], dy, tok, *pairs_of(1))
@@ -844,8 +838,6 @@
             val = add(sums[0], place.core(sums[1]))
             val = val.reshape(nz, ny, nx, -1, val.shape[1])
             val = stage(jnp.moveaxis(val, 2, 0), nx, place.x, place.xs)
-        if e == 0:
-            done += backs[0]
         level = functools.reduce(add, [sent[0], *crossed])
         if e + 1 < local:
             x, grads, rows_in, *sent = after(done, xs[0], dy, tok, *later)
@@ -878,7 +870,7 @@
     )
     stored = []
     for e, b in enumerate(both):
-        b = after([qkv_g], *b) if e == local - 1 else b
+        b = after([qkv_g] if e == local - 1 else [val], *b)
         stored = store_expert(e, local, b, stored)
     grad_up, grad_down = stored
     outs = after([across_x], *[v[0] for v in images])

time: 314 us -> 300 us (0.955)
  waiting for transfers between devices: 84.6 us -> 66.7 us
  local copies, waits for them, and re-layouts: 32.6 us -> 36.3 us
    ppermute x5, waiting for transfers between devices: 6.53 us -> 28 us  [ys(): lax.ppermute(val, 'dp', [(i, i // n * n + (i + k) % n) for i in range(sel...]
    ppermute x6, waiting for transfers between devices: 24.8 us -> 9.12 us  [zs(): lax.ppermute(val, 'dp', [(i, (i // m + k) % n * m + i % m) for i in range...]
    ppermute x4, waiting for transfers between devices: 17 us -> 3.02 us  [zhs(): lax.ppermute(val, 'dp', [(i, ((i // m // 2 + k) % n * 2 + i // m % 2) * m...]
    ppermute x3 -> x2, waiting for transfers between devices: 9.51 us -> 0.45 us  [zp(): lax.ppermute(val, 'dp', [(i, (i // m ^ 1) * m + i % m) for i in range(sel...]
    ppermute x16 -> x14, waiting for transfers between devices: 8.66 us -> 4.56 us  [core(): return lax.ppermute(val, 'expert', [(i, i ^ 1) for i in range(self.ne)])]
    unnamed x125 -> x135, local copies, waits for them, and re-layouts: 14.3 us -> 18.4 us
    ppermute x9 -> x8, waiting for transfers between devices: 10.9 us -> 14.4 us  [xs(): lax.ppermute(val, 'expert', [(i, (i // c + k) % n * c + i % c) for i in r...]
    ppermute x9 -> x8, starting transfers between devices: 8.35 us -> 9.38 us  [xs(): lax.ppermute(val, 'expert', [(i, (i // c + k) % n * c + i % c) for i in r...]
  transfers between devices with their start and end apart: 46 -> 42, of which waited for: 19 -> 20; matrix products, arithmetic and copies ran while one was open for 11% -> 13% of each run, Pallas kernels for 44% -> 45%
where the time goes in v4:
time: 300 us; the launch traced here: 297 us
  Pallas kernels  135 us (45%)
  waiting for transfers between devices  66.7 us (22%)
  local copies, waits for them, and re-layouts  36.3 us (12%)
  starting transfers between devices  35.2 us (12%)
  other arithmetic  21.8 us (7%)
    pallas_call x2, Pallas kernels, run_experts(): pl.pallas_call(functools.partial(expert_kernel, experts, n_src, slots, mi...  47.5 us
    pallas_call x4, Pallas kernels, run_weight_grad(): pl.pallas_call(functools.partial(weight_grad_kernel, e, len(xs), ny, hb),...  43.3 us
    ppermute x5, waiting for transfers between devices, ys(): lax.ppermute(val, 'dp', [(i, i // n * n + (i + k) % n) for i in range(sel...  28 us
    unnamed x135, local copies, waits for them, and re-layouts  18.4 us
    pallas_call x4, Pallas kernels, run_backward(): pl.pallas_call(functools.partial(backward_kernel, experts, len(backs)), g...  18.1 us
    ppermute x8, waiting for transfers between devices, xs(): lax.ppermute(val, 'expert', [(i, (i // c + k) % n * c + i % c) for i in r...  14.4 us
    pallas_call x2, Pallas kernels, run_forward(): pl.pallas_call(functools.partial(forward_kernel, experts), grid=(HALF,),...  10.4 us
    convert_element_type x7, other arithmetic, on_device(): add = lambda a, b: (a.astype(F32) + b.astype(F32)).astype(BF)  10 us
  transfers between devices with their start and end apart: 42, of which 20 were waited for; matrix products, arithmetic and copies ran while one was open for 13% of the time, Pallas kernels for 45%

profile of v4, /device:TPU:0, one launch (start us, length us, event | category | flops | bytes accessed | tf_op | source)
XLA Modules:
  0.0 296.8 jit_solution(3772377863851995176)
XLA Ops:
  3.2 5.1 %collective-permute-start.2 = (bf16[16,2176]{1,0:T(8,128)(2,1)S(1)}, bf16[16,2176]{1,0:T(8,128)(2,1)S(1)}, u32[]{:S(2)}, u32[]{:S(2)}) collective-permute-start(bf16[16,2176]{1,0:T(8,128)(2,1)S(1)} %pad.13), channel_id=1, source_target_pairs={{0,24},{4,28},{8,0},{12,4},{16,8},{20,12},{24,16},{28,20},{1,25},{... | collective-permute-start | bytes 208904 | tf_op jit(solution)/shard_map/ppermute | solution.py:623
  10.9 4.2 %collective-permute-done.1 = bf16[16,2176]{1,0:T(8,128)(2,1)S(1)} collective-permute-done((bf16[16,2176]{1,0:T(8,128)(2,1)S(1)}, bf16[16,2176]{1,0:T(8,128)(2,1)S(1)}, u32[]{:S(2)}, u32[]{:S(2)}) %collective-permute-start.1) | collective-permute-done | bytes 69664 | tf_op jit(solution)/shard_map/ppermute | solution.py:623
  15.1 2.5 collective-permute-start.5
  23.6 2.0 collective-permute-done.5
  25.6 4.9 %collective-permute-done.4 = bf16[64,2176]{1,0:T(8,128)(2,1)S(1)} collective-permute-done((bf16[64,2176]{1,0:T(8,128)(2,1)S(1)}, bf16[64,2176]{1,0:T(8,128)(2,1)S(1)}, u32[]{:S(2)}, u32[]{:S(2)}) %collective-permute-start.4) | collective-permute-done | bytes 278560 | tf_op jit(solution)/shard_map/ppermute | solution.py:644
  35.7 4.9 %dense_forward.2 = (bf16[2,208,1536]{2,1,0:T(8,128)(2,1)S(1)}, bf16[2,208,512]{2,1,0:T(8,128)(2,1)S(1)}, f32[2,208,512]{2,1,0:T(8,128)S(1)}, bf16[2,208,512]{2,1,0:T(8,128)(2,1)S(1)}, f32[2,208,128]{2,1,0:T(8,128)S(1)}) custom-call(bf16[4,208,512]{2,1,0:T(8,128)(2,1)S(1)} %pad.12.tok.refs_0_, bf16[512,2176]{1,0:T(8,128)(2,1)S(1)} %get-tuple-element.156.dense.refs_2_, ...), custom_call_target="tpu_custom_call" | custom-call | flops 1750000000 | bytes 1048576 | tf_op jit(solution)/shard_map/dense_forward/pallas_call | solution.py:119
  45.5 5.5 %dense_forward.3 = (bf16[2,208,1536]{2,1,0:T(8,128)(2,1)S(1)}, bf16[2,208,512]{2,1,0:T(8,128)(2,1)S(1)}, f32[2,208,512]{2,1,0:T(8,128)S(1)}, bf16[2,208,512]{2,1,0:T(8,128)(2,1)}, f32[2,208,128]{2,1,0:T(8,128)S(1)}) custom-call(bf16[4,208,512]{2,1,0:T(8,128)(2,1)S(1)} %pad.12.tok.refs_0_, bf16[512,2176]{1,0:T(8,128)(2,1)S(1)} %get-tuple-element.156.dense.refs_2_, ...), custom_call_target="tpu_custom_call" | custom-call | flops 1750000000 | bytes 1048576 | tf_op jit(solution)/shard_map/dense_forward/pallas_call | solution.py:119
  54.6 7.8 %collective-permute-done.9.refs_2_ = bf16[2,208,512]{2,1,0:T(8,128)(2,1)S(1)} collective-permute-done((bf16[2,208,512]{2,1,0:T(8,128)(2,1)S(1)}, bf16[2,208,512]{2,1,0:T(8,128)(2,1)S(1)}, u32[]{:S(2)}, u32[]{:S(2)}) %collective-permute-start.9) | collective-permute-done | bytes 426016 | tf_op jit(solution)/shard_map/ppermute | solution.py:615
  69.5 23.7 %experts.2 = (bf16[2,864,512]{2,1,0:T(8,128)(2,1)}, bf16[2,864,512]{2,1,0:T(8,128)(2,1)}, bf16[4,384,512]{2,1,0:T(8,128)(2,1)}, bf16[4,384,512]{2,1,0:T(8,128)(2...) custom-call(s32[1]{0:T(128)} %bitcast.at_ref.ei_ref, bf16[2,208,512]{2,1,0:T(8,128)(2,1)} %copy-done.10, ...), custom_call_target="tpu_custom_call" | custom-call | flops 8400000000 | bytes 1048576 | tf_op jit(solution)/shard_map/experts/pallas_call | solution.py:243
  93.2 2.8 collective-permute-done.15.refs_2_
  98.7 2.1 collective-permute-done.18.refs_3_
  100.8 23.8 %experts.3 = (bf16[2,864,512]{2,1,0:T(8,128)(2,1)}, bf16[2,864,512]{2,1,0:T(8,128)(2,1)}, bf16[4,384,512]{2,1,0:T(8,128)(2,1)}, bf16[4,384,512]{2,1,0:T(8,128)(2...) custom-call(s32[1]{0:T(128)} %bitcast.at_ref.ei_ref, bf16[2,208,512]{2,1,0:T(8,128)(2,1)} %get-tuple-element.161.refs_0_.refs_6_, ...), custom_call_target="tpu_custom_call" | custom-call | flops 8400000000 | bytes 1048576 | tf_op jit(solution)/shard_map/experts/pallas_call | solution.py:243
  125.4 2.5 fusion.6
  131.1 2.5 pick_rows.3
  133.7 2.7 pick_rows.2
  137.1 11.0 %weight_grad.4 = (bf16[2,2,256,512]{3,2,1,0:T(8,128)(2,1)S(1)}, bf16[2,2,256,512]{3,2,1,0:T(8,128)(2,1)S(1)}) custom-call(s32[3]{0:T(128)S(1)} %pad_add_fusion.own_ref, bf16[4,384,512]{2,1,0:T(8,128)(2,1)S(1)} %copy-done, bf16[4,384,512]{2,1,0:T(8,128)(2,1)S(1)} %copy-done.2, bf16[4,384,512]{2,1,0:T(8,128)(2,1)S(1)} %get-tuple-element.176.refs_2_, ...), custom_call_target="tpu_custom_call" | custom-call | flops 350000000 | bytes 1048576 | tf_op jit(solution)/shard_map/weight_grad/pallas_call | solution.py:342
  153.5 10.7 %weight_grad.5 = (bf16[2,2,256,512]{3,2,1,0:T(8,128)(2,1)S(1)}, bf16[2,2,256,512]{3,2,1,0:T(8,128)(2,1)S(1)}) custom-call(s32[3]{0:T(128)S(1)} %pad_add_fusion.own_ref, bf16[4,384,512]{2,1,0:T(8,128)(2,1)S(1)} %copy-done, bf16[4,384,512]{2,1,0:T(8,128)(2,1)S(1)} %copy-done.2, bf16[4,384,512]{2,1,0:T(8,128)(2,1)S(1)} %get-tuple-element.176.refs_2_, ...), custom_call_target="tpu_custom_call" | custom-call | flops 350000000 | bytes 1048576 | tf_op jit(solution)/shard_map/weight_grad/pallas_call | solution.py:342
  164.3 4.0 %dense_backward.5 = (bf16[1,208,512]{2,1,0:T(8,128)(2,1)S(1)}, f32[1,208,512]{2,1,0:T(8,128)S(1)}, bf16[1,208,512]{2,1,0:T(8,128)(2,1)S(1)}, bf16[1,208,512]{2,1...) custom-call(bf16[4,208,512]{2,1,0:T(8,128)(2,1)S(1)} %pad.12.tok.refs_0_, ...), custom_call_target="tpu_custom_call" | custom-call | flops 350000000 | bytes 1048576 | tf_op jit(solution)/shard_map/dense_backward/pallas_call | solution.py:451
  169.8 4.1 %dense_backward.4 = (bf16[1,208,512]{2,1,0:T(8,128)(2,1)S(1)}, f32[1,208,512]{2,1,0:T(8,128)S(1)}, bf16[1,208,512]{2,1,0:T(8,128)(2,1)S(1)}, bf16[1,208,512]{2,1...) custom-call(bf16[4,208,512]{2,1,0:T(8,128)(2,1)S(1)} %pad.12.tok.refs_0_, ...), custom_call_target="tpu_custom_call" | custom-call | flops 350000000 | bytes 1048576 | tf_op jit(solution)/shard_map/dense_backward/pallas_call | solution.py:451
  179.8 10.8 %weight_grad.6 = (bf16[2,2,256,512]{3,2,1,0:T(8,128)(2,1)S(1)}, bf16[2,2,256,512]{3,2,1,0:T(8,128)(2,1)S(1)}) custom-call(s32[3]{0:T(128)S(1)} %pad_add_fusion.own_ref, bf16[4,384,512]{2,1,0:T(8,128)(2,1)S(1)} %copy-done, bf16[4,384,512]{2,1,0:T(8,128)(2,1)S(1)} %copy-done.2, bf16[4,384,512]{2,1,0:T(8,128)(2,1)S(1)} %get-tuple-element.176.refs_2_, ...), custom_call_target="tpu_custom_call" | custom-call | flops 350000000 | bytes 1048576 | tf_op jit(solution)/shard_map/weight_grad/pallas_call | solution.py:342
  190.6 5.0 %dense_backward.7 = (bf16[1,208,512]{2,1,0:T(8,128)(2,1)S(1)}, f32[1,208,512]{2,1,0:T(8,128)S(1)}, bf16[1,208,512]{2,1,0:T(8,128)(2,1)S(1)}, bf16[1,208,512]{2,1...) custom-call(bf16[4,208,512]{2,1,0:T(8,128)(2,1)S(1)} %pad.12.tok.refs_0_, ...), custom_call_target="tpu_custom_call" | custom-call | flops 350000000 | bytes 1048576 | tf_op jit(solution)/shard_map/dense_backward/pallas_call | solution.py:451
  196.4 5.0 %dense_backward.6 = (bf16[1,208,512]{2,1,0:T(8,128)(2,1)S(1)}, f32[1,208,512]{2,1,0:T(8,128)S(1)}, bf16[1,208,512]{2,1,0:T(8,128)(2,1)S(1)}, bf16[1,208,512]{2,1...) custom-call(bf16[4,208,512]{2,1,0:T(8,128)(2,1)S(1)} %pad.12.tok.refs_0_, ...), custom_call_target="tpu_custom_call" | custom-call | flops 350000000 | bytes 1048576 | tf_op jit(solution)/shard_map/dense_backward/pallas_call | solution.py:451
  206.3 3.6 %dense_grads.1 = (bf16[256,2176]{1,0:T(8,128)(2,1)S(1)}, bf16[256,2176]{1,0:T(8,128)(2,1)}) custom-call(s32[1]{0:T(128)} %bitcast.42.core_ref, bf16[1,208,512]{2,1,0:T(8,128)(2,1)S(1)} %copy-done.47, bf16[1,208,512]{2,1,0:T(8,128)(2,1)S(1)} %copy-done.43, bf16[1,208,512]{2,1,0:T(8,128)(2,1)S(1)} %get-tuple-element.214.refs_2_, ...), custom_call_target="tpu_custom_call" | custom-call | flops 350000000 | bytes 1048576 | tf_op jit(solution)/shard_map/dense_grads/pallas_call | solution.py:499
  209.9 10.8 %weight_grad.7 = (bf16[2,2,256,512]{3,2,1,0:T(8,128)(2,1)S(1)}, bf16[2,2,256,512]{3,2,1,0:T(8,128)(2,1)S(1)}) custom-call(s32[3]{0:T(128)S(1)} %pad_add_fusion.own_ref, bf16[4,384,512]{2,1,0:T(8,128)(2,1)S(1)} %copy-done, bf16[4,384,512]{2,1,0:T(8,128)(2,1)S(1)} %copy-done.2, bf16[4,384,512]{2,1,0:T(8,128)(2,1)S(1)} %get-tuple-element.176.refs_2_, ...), custom_call_target="tpu_custom_call" | custom-call | flops 350000000 | bytes 1048576 | tf_op jit(solution)/shard_map/weight_grad/pallas_call | solution.py:342
  221.7 5.4 %collective-permute-done.31 = bf16[2,2,256,512]{3,2,1,0:T(8,128)(2,1)S(1)} collective-permute-done((bf16[2,2,256,512]{3,2,1,0:T(8,128)(2,1)S(1)}, bf16[2,2,256,512]{3,2,1,0:T(8,128)(2,1)S(1)}, u32[]{:S(2)}, u32[]{:S(2)}) %collective-permute-start.31) | collective-permute-done | bytes 1048608 | tf_op jit(solution)/shard_map/ppermute | solution.py:619
  231.2 2.2 slice_bitcast_fusion.2
  237.0 21.9 %collective-permute-done.39 = bf16[2,2,256,512]{3,2,1,0:T(8,128)(2,1)S(1)} collective-permute-done((bf16[2,2,256,512]{3,2,1,0:T(8,128)(2,1)S(1)}, bf16[2,2,256,512]{3,2,1,0:T(8,128)(2,1)S(1)}, u32[]{:S(2)}, u32[]{:S(2)}) %collective-permute-start.39) | collective-permute-done | bytes 1048608 | tf_op jit(solution)/shard_map/ppermute | solution.py:619
  260.2 2.6 collective-permute-start.40
  269.0 2.6 pad_maximum_fusion
  271.5 2.8 reshape.93
  276.3 2.3 reshape.92
  287.7 4.4 %collective-permute-done.37.refs_2_ = bf16[16,2176]{1,0:T(8,128)(2,1)S(1)} collective-permute-done((bf16[16,2176]{1,0:T(8,128)(2,1)S(1)}, bf16[16,2176]{1,0:T(8,128)(2,1)S(1)}, u32[]{:S(2)}, u32[]{:S(2)}) %collective-permute-start.37) | collective-permute-done | bytes 69664 | tf_op jit(solution)/shard_map/ppermute | solution.py:623
  (261 shorter events, 88.4 us)
Async XLA Ops:
  15.1 10.5 %collective-permute-start.5 = (bf16[64,2176]{1,0:T(8,128)(2,1)S(1)}, bf16[64,2176]{1,0:T(8,128)(2,1)S(1)}, u32[]{:S(2)}, u32[]{:S(2)}) collective-permute-start(bf16[64,2176]{1,0:T(8,128)(2,1)S(1)} %pad_maximum_fusion.8), channel_id=1, source_target_pairs={{0,6},{1,7},{2,4},{3,5},{4,2},{5,3},{6,0},{7,1},{8,14},{9,15},{10,... | collective-permute-start | bytes 835592 | tf_op jit(solution)/shard_map/ppermute | solution.py:644
  17.6 12.9 %collective-permute-start.4 = (bf16[64,2176]{1,0:T(8,128)(2,1)S(1)}, bf16[64,2176]{1,0:T(8,128)(2,1)S(1)}, u32[]{:S(2)}, u32[]{:S(2)}) collective-permute-start(bf16[64,2176]{1,0:T(8,128)(2,1)S(1)} %pad_maximum_fusion.8), channel_id=1, source_target_pairs={{0,4},{1,5},{2,6},{3,7},{4,0},{5,1},{6,2},{7,3},{8,12},{9,13},{10,... | collective-permute-start | bytes 835592 | tf_op jit(solution)/shard_map/ppermute | solution.py:644
  18.1 12.6 %collective-permute-start.3 = (bf16[64,2176]{1,0:T(8,128)(2,1)S(1)}, bf16[64,2176]{1,0:T(8,128)(2,1)}, u32[]{:S(2)}, u32[]{:S(2)}) collective-permute-start(bf16[64,2176]{1,0:T(8,128)(2,1)S(1)} %pad_maximum_fusion.8), channel_id=1, source_target_pairs={{0,2},{1,3},{2,0},{3,1},{4,6},{5,7},{6,4},{7,5},{8,10},{9,11},{10,... | collective-permute-start | bytes 835592 | tf_op jit(solution)/shard_map/ppermute | solution.py:644
  31.8 12.2 %collective-permute-start.7 = (bf16[4,208,512]{2,1,0:T(8,128)(2,1)S(1)}, bf16[4,208,512]{2,1,0:T(8,128)(2,1)S(1)}, u32[]{:S(2)}, u32[]{:S(2)}) collective-permute-start(bf16[4,208,512]{2,1,0:T(8,128)(2,1)S(1)} %maximum_maximum_fusion.refs_4_.refs_1_), channel_id=1, source_target_pairs={{0,1},{1,0},{2,3},{3,2},{4,5},{5,4},{6,7},{7,6},{8,9},{9,8},{10,11... | collective-permute-start | bytes 2555912 | tf_op jit(solution)/shard_map/ppermute | solution.py:611
  32.3 21.8 %collective-permute-start.11 = (bf16[4,208,512]{2,1,0:T(8,128)(2,1)S(1)}, bf16[4,208,512]{2,1,0:T(8,128)(2,1)S(1)}, u32[]{:S(2)}, u32[]{:S(2)}) collective-permute-start(bf16[4,208,512]{2,1,0:T(8,128)(2,1)S(1)} %maximum_maximum_fusion.refs_4_.refs_1_), channel_id=1, source_target_pairs={{0,2},{1,3},{2,0},{3,1},{4,6},{5,7},{6,4},{7,5},{8,10},{9,11},{10,... | collective-permute-start | bytes 2555912 | tf_op jit(solution)/shard_map/ppermute | solution.py:615
  33.8 20.8 %collective-permute-start.10 = (bf16[4,208,512]{2,1,0:T(8,128)(2,1)S(1)}, bf16[4,208,512]{2,1,0:T(8,128)(2,1)}, u32[]{:S(2)}, u32[]{:S(2)}) collective-permute-start(bf16[4,208,512]{2,1,0:T(8,128)(2,1)S(1)} %maximum_maximum_fusion.refs_4_.refs_1_), channel_id=1, source_target_pairs={{0,8},{4,12},{8,0},{12,4},{16,24},{20,28},{24,16},{28,20},{1,9},{5... | collective-permute-start | bytes 2555912 | tf_op jit(solution)/shard_map/ppermute | solution.py:627
  44.0 18.4 %collective-permute-start.9 = (bf16[2,208,512]{2,1,0:T(8,128)(2,1)S(1)}, bf16[2,208,512]{2,1,0:T(8,128)(2,1)S(1)}, u32[]{:S(2)}, u32[]{:S(2)}) collective-permute-start(bf16[2,208,512]{2,1,0:T(8,128)(2,1)S(1)} %get-tuple-element.155.refs_0_.refs_6_), channel_id=1, source_target_pairs={{0,2},{1,3},{2,0},{3,1},{4,6},{5,7},{6,4},{7,5},{8,10},{9,11},{10,... | collective-permute-start | bytes 1277960 | tf_op jit(solution)/shard_map/ppermute | solution.py:615
  45.5 16.9 %collective-permute-start.8 = (bf16[2,208,512]{2,1,0:T(8,128)(2,1)S(1)}, bf16[2,208,512]{2,1,0:T(8,128)(2,1)S(1)}, u32[]{:S(2)}, u32[]{:S(2)}) collective-permute-start(bf16[2,208,512]{2,1,0:T(8,128)(2,1)S(1)} %get-tuple-element.155.refs_0_.refs_6_), channel_id=1, source_target_pairs={{0,1},{1,0},{2,3},{3,2},{4,5},{5,4},{6,7},{7,6},{8,9},{9,8},{10,11... | collective-permute-start | bytes 1277960 | tf_op jit(solution)/shard_map/ppermute | solution.py:611
  65.7 30.4 %collective-permute-start.17 = (bf16[4,208,512]{2,1,0:T(8,128)(2,1)}, bf16[4,208,512]{2,1,0:T(8,128)(2,1)S(1)}, u32[]{:S(2)}, u32[]{:S(2)}) collective-permute-start(bf16[4,208,512]{2,1,0:T(8,128)(2,1)} %pad_maximum_fusion.4), channel_id=1, source_target_pairs={{0,8},{4,12},{8,0},{12,4},{16,24},{20,28},{24,16},{28,20},{1,9},{5... | collective-permute-start | bytes 2555912 | tf_op jit(solution)/shard_map/ppermute | solution.py:627
  65.7 30.4 %collective-permute-start.16 = (bf16[4,208,512]{2,1,0:T(8,128)(2,1)}, bf16[4,208,512]{2,1,0:T(8,128)(2,1)}, u32[]{:S(2)}, u32[]{:S(2)}) collective-permute-start(bf16[4,208,512]{2,1,0:T(8,128)(2,1)} %collective-permute-done.10.refs_4_), channel_id=1, source_target_pairs={{0,2},{1,3},{2,0},{3,1},{4,6},{5,7},{6,4},{7,5},{8,10},{9,11},{10,... | collective-permute-start | bytes 2555912 | tf_op jit(solution)/shard_map/ppermute | solution.py:615
  67.3 28.8 %collective-permute-start.15 = (bf16[2,208,512]{2,1,0:T(8,128)(2,1)}, bf16[2,208,512]{2,1,0:T(8,128)(2,1)}, u32[]{:S(2)}, u32[]{:S(2)}) collective-permute-start(bf16[2,208,512]{2,1,0:T(8,128)(2,1)} %get-tuple-element.161.refs_0_.refs_6_), channel_id=1, source_target_pairs={{0,2},{1,3},{2,0},{3,1},{4,6},{5,7},{6,4},{7,5},{8,10},{9,11},{10,... | collective-permute-start | bytes 1277960 | tf_op jit(solution)/shard_map/ppermute | solution.py:615
  67.8 28.3 %collective-permute-start.14 = (bf16[2,208,512]{2,1,0:T(8,128)(2,1)}, bf16[2,208,512]{2,1,0:T(8,128)(2,1)}, u32[]{:S(2)}, u32[]{:S(2)}) collective-permute-start(bf16[2,208,512]{2,1,0:T(8,128)(2,1)} %get-tuple-element.161.refs_0_.refs_6_), channel_id=1, source_target_pairs={{0,1},{1,0},{2,3},{3,2},{4,5},{5,4},{6,7},{7,6},{8,9},{9,8},{10,11... | collective-permute-start | bytes 1277960 | tf_op jit(solution)/shard_map/ppermute | solution.py:611
  96.1 28.6 %collective-permute-start.22 = (bf16[2,864,512]{2,1,0:T(8,128)(2,1)}, bf16[2,864,512]{2,1,0:T(8,128)(2,1)}, u32[]{:S(2)}, u32[]{:S(2)}) collective-permute-start(bf16[2,864,512]{2,1,0:T(8,128)(2,1)} %get-tuple-element.171), channel_id=1, source_target_pairs={{0,1},{1,0},{2,3},{3,2},{4,5},{5,4},{6,7},{7,6},{8,9},{9,8},{10,11... | collective-permute-start | bytes 5308424 | tf_op jit(solution)/shard_map/ppermute | solution.py:611
  96.7 28.0 %collective-permute-start.19 = (bf16[4,208,512]{2,1,0:T(8,128)(2,1)S(1)}, bf16[4,208,512]{2,1,0:T(8,128)(2,1)}, u32[]{:S(2)}, u32[]{:S(2)}) collective-permute-start(bf16[4,208,512]{2,1,0:T(8,128)(2,1)S(1)} %collective-permute-done.17.refs_0_), channel_id=1, source_target_pairs={{0,2},{1,3},{2,0},{3,1},{4,6},{5,7},{6,4},{7,5},{8,10},{9,11},{10,... | collective-permute-start | bytes 2555912 | tf_op jit(solution)/shard_map/ppermute | solution.py:615
  98.2 26.5 %collective-permute-start.20 = (bf16[4,208,512]{2,1,0:T(8,128)(2,1)}, bf16[4,208,512]{2,1,0:T(8,128)(2,1)}, u32[]{:S(2)}, u32[]{:S(2)}) collective-permute-start(bf16[4,208,512]{2,1,0:T(8,128)(2,1)} %collective-permute-done.10.refs_4_), channel_id=1, source_target_pairs={{0,1},{1,0},{2,3},{3,2},{4,5},{5,4},{6,7},{7,6},{8,9},{9,8},{10,11... | collective-permute-start | bytes 2555912 | tf_op jit(solution)/shard_map/ppermute | solution.py:611
  98.2 26.5 %collective-permute-start.21 = (bf16[4,208,512]{2,1,0:T(8,128)(2,1)}, bf16[4,208,512]{2,1,0:T(8,128)(2,1)}, u32[]{:S(2)}, u32[]{:S(2)}) collective-permute-start(bf16[4,208,512]{2,1,0:T(8,128)(2,1)} %collective-permute-done.16.refs_6_), channel_id=1, source_target_pairs={{0,1},{1,0},{2,3},{3,2},{4,5},{5,4},{6,7},{7,6},{8,9},{9,8},{10,11... | collective-permute-start | bytes 2555912 | tf_op jit(solution)/shard_map/ppermute | solution.py:611
  124.7 25.2 %collective-permute-start.23 = (bf16[2,864,512]{2,1,0:T(8,128)(2,1)}, bf16[2,864,512]{2,1,0:T(8,128)(2,1)S(1)}, u32[]{:S(2)}, u32[]{:S(2)}) collective-permute-start(bf16[2,864,512]{2,1,0:T(8,128)(2,1)} %get-tuple-element.172), channel_id=1, source_target_pairs={{0,1},{1,0},{2,3},{3,2},{4,5},{5,4},{6,7},{7,6},{8,9},{9,8},{10,11... | collective-permute-start | bytes 5308424 | tf_op jit(solution)/shard_map/ppermute | solution.py:611
  127.8 22.0 %collective-permute-start.24 = (bf16[864,512]{1,0:T(8,128)(2,1)S(1)}, bf16[864,512]{1,0:T(8,128)(2,1)S(1)}, u32[]{:S(2)}, u32[]{:S(2)}) collective-permute-start(bf16[864,512]{1,0:T(8,128)(2,1)S(1)} %get-tuple-element.310), channel_id=1, source_target_pairs={{0,2},{1,3},{2,0},{3,1},{4,6},{5,7},{6,4},{7,5},{8,10},{9,11},{10,... | collective-permute-start | bytes 2654216 | tf_op jit(solution)/shard_map/ppermute | solution.py:615
  149.8 24.7 %collective-permute-start.27 = (bf16[2,2,256,512]{3,2,1,0:T(8,128)(2,1)S(1)}, bf16[2,2,256,512]{3,2,1,0:T(8,128)(2,1)}, u32[]{:S(2)}, u32[]{:S(2)}) collective-permute-start(bf16[2,2,256,512]{3,2,1,0:T(8,128)(2,1)S(1)} %get-tuple-element.194), channel_id=1, source_target_pairs={{0,4},{4,0},{8,12},{12,8},{16,20},{20,16},{24,28},{28,24},{1,5},{5... | collective-permute-start | bytes 3145736 | tf_op jit(solution)/shard_map/ppermute | solution.py:619
  152.6 37.9 %collective-permute-start.28 = (bf16[864,512]{1,0:T(8,128)(2,1)}, bf16[864,512]{1,0:T(8,128)(2,1)S(1)}, u32[]{:S(2)}, u32[]{:S(2)}) collective-permute-start(bf16[864,512]{1,0:T(8,128)(2,1)} %get-tuple-element.211), channel_id=1, source_target_pairs={{0,2},{1,3},{2,0},{3,1},{4,6},{5,7},{6,4},{7,5},{8,10},{9,11},{10,... | collective-permute-start | bytes 2654216 | tf_op jit(solution)/shard_map/ppermute | solution.py:615
  174.6 28.4 %collective-permute-start.29 = (bf16[2,2,256,512]{3,2,1,0:T(8,128)(2,1)S(1)}, bf16[2,2,256,512]{3,2,1,0:T(8,128)(2,1)}, u32[]{:S(2)}, u32[]{:S(2)}) collective-permute-start(bf16[2,2,256,512]{3,2,1,0:T(8,128)(2,1)S(1)} %get-tuple-element.229), channel_id=1, source_target_pairs={{0,4},{4,0},{8,12},{12,8},{16,20},{20,16},{24,28},{28,24},{1,5},{5... | collective-permute-start | bytes 3145736 | tf_op jit(solution)/shard_map/ppermute | solution.py:619
  178.5 24.5 %collective-permute-start.30 = (bf16[2,256,512]{2,1,0:T(8,128)(2,1)S(1)}, bf16[2,256,512]{2,1,0:T(8,128)(2,1)S(1)}, u32[]{:S(2)}, u32[]{:S(2)}) collective-permute-start(bf16[2,256,512]{2,1,0:T(8,128)(2,1)S(1)} %get-tuple-element.317), channel_id=1, source_target_pairs={{0,16},{4,20},{8,24},{12,28},{16,0},{20,4},{24,8},{28,12},{1,17},{... | collective-permute-start | bytes 1572872 | tf_op jit(solution)/shard_map/ppermute | solution.py:631
  203.0 24.2 %collective-permute-start.31 = (bf16[2,2,256,512]{3,2,1,0:T(8,128)(2,1)S(1)}, bf16[2,2,256,512]{3,2,1,0:T(8,128)(2,1)S(1)}, u32[]{:S(2)}, u32[]{:S(2)}) collective-permute-start(bf16[2,2,256,512]{3,2,1,0:T(8,128)(2,1)S(1)} %get-tuple-element.233), channel_id=1, source_target_pairs={{0,4},{4,0},{8,12},{12,8},{16,20},{20,16},{24,28},{28,24},{1,5},{5... | collective-permute-start | bytes 3145736 | tf_op jit(solution)/shard_map/ppermute | solution.py:619
  205.1 24.9 %collective-permute-start.32 = (bf16[2,256,512]{2,1,0:T(8,128)(2,1)S(1)}, bf16[2,256,512]{2,1,0:T(8,128)(2,1)S(1)}, u32[]{:S(2)}, u32[]{:S(2)}) collective-permute-start(bf16[2,256,512]{2,1,0:T(8,128)(2,1)S(1)} %get-tuple-element.319), channel_id=1, source_target_pairs={{0,16},{4,20},{8,24},{12,28},{16,0},{20,4},{24,8},{28,12},{1,17},{... | collective-permute-start | bytes 1572872 | tf_op jit(solution)/shard_map/ppermute | solution.py:631
  233.4 52.0 %collective-permute-start.41 = (bf16[2,256,512]{2,1,0:T(8,128)(2,1)}, bf16[2,256,512]{2,1,0:T(8,128)(2,1)S(1)}, u32[]{:S(2)}, u32[]{:S(2)}) collective-permute-start(bf16[2,256,512]{2,1,0:T(8,128)(2,1)} %get-tuple-element.320), channel_id=1, source_target_pairs={{0,16},{4,20},{8,24},{12,28},{16,0},{20,4},{24,8},{28,12},{1,17},{... | collective-permute-start | bytes 1572872 | tf_op jit(solution)/shard_map/ppermute | solution.py:631
  233.4 25.6 %collective-permute-start.39 = (bf16[2,2,256,512]{3,2,1,0:T(8,128)(2,1)S(1)}, bf16[2,2,256,512]{3,2,1,0:T(8,128)(2,1)S(1)}, u32[]{:S(2)}, u32[]{:S(2)}) collective-permute-start(bf16[2,2,256,512]{3,2,1,0:T(8,128)(2,1)S(1)} %copy-done.49), channel_id=1, source_target_pairs={{0,4},{4,0},{8,12},{12,8},{16,20},{20,16},{24,28},{28,24},{1,5},{5... | collective-permute-start | bytes 3145736 | tf_op jit(solution)/shard_map/ppermute | solution.py:619
  236.6 26.2 %collective-permute-start.34 = (bf16[4,2,16,2176]{3,2,0,1:T(8,128)(2,1)S(1)}, bf16[4,2,16,2176]{3,2,0,1:T(8,128)(2,1)S(1)}, u32[]{:S(2)}, u32[]{:S(2)}) collective-permute-start(bf16[4,2,16,2176]{3,2,0,1:T(8,128)(2,1)S(1)} %bitcast.100), channel_id=1, source_target_pairs={{0,2},{1,3},{2,0},{3,1},{4,6},{5,7},{6,4},{7,5},{8,10},{9,11},{10,... | collective-permute-start | bytes 1671176 | tf_op jit(solution)/shard_map/ppermute | solution.py:615
  260.2 34.5 %collective-permute-start.40 = (bf16[2,256,512]{2,1,0:T(8,128)(2,1)}, bf16[2,256,512]{2,1,0:T(8,128)(2,1)S(1)}, u32[]{:S(2)}, u32[]{:S(2)}) collective-permute-start(bf16[2,256,512]{2,1,0:T(8,128)(2,1)} %get-tuple-element.322), channel_id=1, source_target_pairs={{0,16},{4,20},{8,24},{12,28},{16,0},{20,4},{24,8},{28,12},{1,17},{... | collective-permute-start | bytes 1572872 | tf_op jit(solution)/shard_map/ppermute | solution.py:631
  267.4 11.2 %collective-permute-start.35 = (bf16[4,16,2176]{2,1,0:T(8,128)(2,1)}, bf16[4,16,2176]{2,1,0:T(8,128)(2,1)}, u32[]{:S(2)}, u32[]{:S(2)}) collective-permute-start(bf16[4,16,2176]{2,1,0:T(8,128)(2,1)} %dynamic-slice_bitcast_fusion), channel_id=1, source_target_pairs={{0,4},{4,0},{8,12},{12,8},{16,20},{20,16},{24,28},{28,24},{1,5},{5... | collective-permute-start | bytes 835592 | tf_op jit(solution)/shard_map/ppermute | solution.py:619
  279.7 8.0 %collective-permute-start.38 = (bf16[16,2176]{1,0:T(8,128)(2,1)S(1)}, bf16[16,2176]{1,0:T(8,128)(2,1)S(1)}, u32[]{:S(2)}, u32[]{:S(2)}) collective-permute-start(bf16[16,2176]{1,0:T(8,128)(2,1)S(1)} %get-tuple-element.324), channel_id=1, source_target_pairs={{0,24},{4,28},{8,0},{12,4},{16,8},{20,12},{24,16},{28,20},{1,25},{... | collective-permute-start | bytes 208904 | tf_op jit(solution)/shard_map/ppermute | solution.py:623
  281.0 11.1 %collective-permute-start.37 = (bf16[16,2176]{1,0:T(8,128)(2,1)S(1)}, bf16[16,2176]{1,0:T(8,128)(2,1)S(1)}, u32[]{:S(2)}, u32[]{:S(2)}) collective-permute-start(bf16[16,2176]{1,0:T(8,128)(2,1)S(1)} %get-tuple-element.325), channel_id=1, source_target_pairs={{0,16},{4,20},{8,24},{12,28},{16,0},{20,4},{24,8},{28,12},{1,17},{... | collective-permute-start | bytes 208904 | tf_op jit(solution)/shard_map/ppermute | solution.py:623
  281.0 11.1 %collective-permute-start.36 = (bf16[16,2176]{1,0:T(8,128)(2,1)S(1)}, bf16[16,2176]{1,0:T(8,128)(2,1)S(1)}, u32[]{:S(2)}, u32[]{:S(2)}) collective-permute-start(bf16[16,2176]{1,0:T(8,128)(2,1)S(1)} %get-tuple-element.326), channel_id=1, source_target_pairs={{0,8},{4,12},{8,16},{12,20},{16,24},{20,28},{24,0},{28,4},{1,9},{5... | collective-permute-start | bytes 208904 | tf_op jit(solution)/shard_map/ppermute | solution.py:623
  (75 other events, 469.9 us)

commit v5 on v4

--- a/solution.py
+++ b/solution.py
@@ -230,6 +230,11 @@
                 out[s // CORES, to : to + experts, 0:rows] = dprob.astype(BF)
 
 
+def half_spec(a, part):
+    at = part if a.shape[0] > HALF else 0
+    return pl.BlockSpec((HALF, *a.shape[1:]), lambda e, p: (at, 0, 0))
+
+
 def run_experts(place, part, sources, w_up, b_up, w_down, b_down, experts, slots):
     local, width, hidden = w_up.shape
     n_src = len(sources)
@@ -239,14 +244,14 @@
     back = HALF * (2 * span + experts)
     flat = [s[i] for i in range(2) for s in sources]
     keep = lambda *s: pl.BlockSpec(s, lambda e, p: (0,) * len(s))
+    half = lambda a: half_spec(a, part)
     each = lambda *s: pl.BlockSpec((1,) + s, lambda e, p: (e, 0, 0))
     return pl.pallas_call(
         functools.partial(expert_kernel, experts, n_src, slots, min(hidden, 1024)),
         grid_spec=pltpu.PrefetchScalarGridSpec(
             num_scalar_prefetch=1,
             grid=(local,),
-            in_specs=[keep(HALF, span, width)] * n_src
-            + [pl.BlockSpec((HALF, span, width), lambda e, p: (part, 0, 0))] * n_src
+            in_specs=[half(a) for a in flat]
             + [
                 each(width, hidden),
                 keep(local, hidden),
@@ -280,7 +285,7 @@
         ],
         name="experts",
         cost_estimate=cost(24),
-        compiler_params=pltpu.CompilerParams(vmem_limit_bytes=60 << 20),
+        compiler_params=pltpu.CompilerParams(vmem_limit_bytes=50 << 20),
     )(place.ei.reshape(1), *flat, w_up, b_up, w_down, b_down)
 
 
@@ -295,14 +300,13 @@
     n_src = len(sources)
     rows = n_src * HALF * slots
     flat = [s[i] for i in range(2) for s in sources]
-    half = lambda h: pl.BlockSpec((HALF, span, width), lambda i, p: (h, 0, 0))
     keep = pl.BlockSpec((local, rows, width), lambda i, p: (0, 0, 0))
     return pl.pallas_call(
         functools.partial(pick_kernel, experts, n_src, slots),
         grid_spec=pltpu.PrefetchScalarGridSpec(
             num_scalar_prefetch=1,
             grid=(1,),
-            in_specs=[half(part)] * (2 * n_src),
+            in_specs=[half_spec(a, part) for a in flat],
             out_specs=[keep] * 2,
         ),
         out_shape=[jax.ShapeDtypeStruct((local, rows, width), BF)] * 2,
@@ -504,7 +508,7 @@
         scratch_shapes=[pltpu.VMEM((width, wide), BF)] if share else [],
         name="dense_grads",
         cost_estimate=cost(1),
-        compiler_params=pltpu.CompilerParams(vmem_limit_bytes=32 << 20),
+        compiler_params=pltpu.CompilerParams(vmem_limit_bytes=24 << 20),
     )(place.c.reshape(1), *args)
 
 
@@ -745,9 +749,13 @@
     tok, order, bu3, bd3, where = after(done, tok, place_order(place), bu3, bd3, where)
     done = [*part, tok, order, bu3, bd3, where]
 
-    dense_near, dy = after(done, jnp.concatenate(part, axis=0), dy)
+    cut = lambda v, h: v[h * HALF : (h + 1) * HALF]
+    dense_near, dy, *dys = after(
+        done, jnp.concatenate(part, axis=0), dy, *[cut(dy, h) for h in halves]
+    )
     other = place.core(dense_near)
-    dy_mine, dy_z, dy_other = across(dy), place.zp(dy), place.core(dy)
+    dy_z, dy_other = place.zp(dy), place.core(dy)
+    dy_x = [across(dys[0])[1:]]
     dense, tailt = dense_in_order(place, dense_near, other, order, share)
     saved, act_x, act_c = [], [], []
     saved.append(run_forward(tok, dense, tailt, 0, experts))
@@ -758,33 +766,43 @@
         act_x.append(across(act))
         act_c.append(place.core(act))
         saved.append(run_forward(tok, dense_h, tailt, h, experts))
-        done = [*act_x[-1], act_c[-1], saved[-1][3], dy_z, *dy_mine]
-
-    act, far_dy, *rest = after(done, saved[-1][3], dy_z, *act_x[0][1:], *dy_mine[1:])
-    dy_near = both_cores(dy_mine, [dy_other, *[place.core(v) for v in rest[nx - 1 :]]])
+        done = [*act_x[-1], act_c[-1], saved[-1][3], dy_z, *dy_x[0]]
+
+    act, dy_next, dy_z, *rest = after(
+        done, saved[-1][3], dys[1], dy_z, *act_x[0][1:], *dy_x[0]
+    )
+    dy_all = lambda h, crossed: both_cores(
+        [dy, *dy_x[h]], [dy_other, *[place.core(v) for v in crossed]]
+    )
+    dy_near = [dy_all(0, rest[nx - 1 :])]
     rest = rest[: nx - 1]
     act_x.append(across(act))
     act_z = place.zp(jnp.concatenate([*[v[0] for v in act_x[:-1]], act], axis=0))
     act_c.append(place.core(act))
-    dy_far = across(far_dy)
+    dy_x.append(across(dy_next)[1:])
+    dz_x = [across(cut(dy_z, 0))[1:]]
     near = both_cores(act_x[0], [act_c[0], *[place.core(v) for v in rest]])
     visit = lambda h, near: [
-        run_experts(place, h, list(zip(near, dy_near))[at : at + 4], w_up, bu3, w_down, bd3, experts, slots)
+        run_experts(place, h, list(zip(near, dy_near[h]))[at : at + 4], w_up, bu3, w_down, bd3, experts, slots)
         for at in range(0, len(near), 4)
     ]
     results = [visit(0, near)]
-    done = [*act_x[-1], act_z, act_c[-1], *dy_far]
+    done = [*act_x[-1], act_z, act_c[-1], *dy_x[1], *dz_x[0]]
     done += [r[0] for r in results[0]]
 
-    n_far = len(dy_far)
-    vals = after(done, *dy_far, act_z, *act_x[1][1:], *[r[1] for r in results[0]])
-    dy_far = both_cores(vals[:n_far], [place.core(v) for v in vals[:n_far]])
-    far = across(vals[n_far])
-    rest = vals[n_far + 1 :]
-    near = both_cores(act_x[1], [act_c[1], *[place.core(v) for v in rest[: nx - 1]]])
-    back = [[place.core(v) for v in rest[nx - 1 :]]]
+    n = nx - 1
+    far, next_z, *rest = after(
+        done, act_z, cut(dy_z, 1), *act_x[1][1:], *dy_x[1], *dz_x[0], *[r[1] for r in results[0]]
+    )
+    near = both_cores(act_x[1], [act_c[1], *[place.core(v) for v in rest[:n]]])
+    dy_near.append(dy_all(1, rest[n : 2 * n]))
+    far = across(far)
+    dz_x.append(across(next_z)[1:])
+    dz_c = [[place.core(v) for v in rest[2 * n : 3 * n]]]
+    dz_own = place.core(dy_z)
+    back = [[place.core(v) for v in rest[3 * n :]]]
     results.append(visit(1, near))
-    done = [*dy_far, *far, *back[0], *[r[0] for r in results[1]]]
+    done = [dz_own, *dz_x[1], *dz_c[0], *far, *back[0], *[r[0] for r in results[1]]]
 
     add = lambda a, b: (a.astype(F32) + b.astype(F32)).astype(BF)
     pairs_of = lambda h: [
@@ -792,12 +810,14 @@
     ]
     home = lambda p: [p[0]] + [place.xs(p[k], nx - k) for k in range(1, nx)]
     backs = [home(pairs_of(0))]
-    vals = after(done, *far, *[r[1] for r in results[1]])
-    far = both_cores(vals[:n_far], [place.core(v) for v in vals[:n_far]])
-    back.append([place.core(v) for v in vals[n_far:]])
+    vals = after(done, *far, *dz_x[1], *[r[1] for r in results[1]])
+    far = both_cores(vals[:nx], [place.core(v) for v in vals[:nx]])
+    dz_c.append([place.core(v) for v in vals[nx : nx + n]])
+    back.append([place.core(v) for v in vals[nx + n :]])
+    dy_far = [both_cores([dy_z, *dz_x[h]], [dz_own, *dz_c[h]]) for h in halves]
     xs, gs = [[r[k] for rs in results for r in rs] for k in (2, 3)]
     for h in halves:
-        src = list(zip(far, dy_far))
+        src = list(zip(far, dy_far[h]))
         for at in range(0, len(src), 4):
             x, g = run_pick(place, h, src[at : at + 4], local, experts, slots)
             xs.append(x)

time: 300 us -> 289 us (0.963)
  Pallas kernels: 135 us -> 126 us
  other arithmetic: 21.8 us -> 14.9 us
  starting transfers between devices: 35.2 us -> 39 us
    ppermute x8 -> x10, waiting for transfers between devices: 14.4 us -> 7.99 us  [xs(): lax.ppermute(val, 'expert', [(i, (i // c + k) % n * c + i % c) for i in r...]
    ppermute x8 -> x10, starting transfers between devices: 9.38 us -> 13.4 us  [xs(): lax.ppermute(val, 'expert', [(i, (i // c + k) % n * c + i % c) for i in r...]
    pallas_call x2, Pallas kernels: 5.21 us -> 2.01 us  [run_pick(): pl.pallas_call(functools.partial(pick_kernel, experts, n_src, slots), gri...]
    ppermute x3, waiting for transfers between devices: 7.16 us -> 10.2 us  [xy(): lax.ppermute(val, ('dp', 'expert'), [(i, move(i)) for i in range(self.nd...]
    unnamed x135 -> x121, local copies, waits for them, and re-layouts: 18.4 us -> 17 us
  transfers between devices with their start and end apart: 42 -> 46, of which waited for: 20 -> 17; matrix products, arithmetic and copies ran while one was open for 13% -> 12% of each run, Pallas kernels for 45% -> 44%
where the time goes in v5:
time: 289 us; the launch traced here: 286 us
  Pallas kernels  126 us (44%)
  waiting for transfers between devices  66.3 us (23%)
  starting transfers between devices  39 us (13%)
  local copies, waits for them, and re-layouts  37.1 us (13%)
  other arithmetic  14.9 us (5%)
    pallas_call x2, Pallas kernels, run_experts(): pl.pallas_call(functools.partial(expert_kernel, experts, n_src, slots, mi...  45.7 us
    pallas_call x4, Pallas kernels, run_weight_grad(): pl.pallas_call(functools.partial(weight_grad_kernel, e, len(xs), ny, hb),...  42.7 us
    ppermute x5, waiting for transfers between devices, ys(): lax.ppermute(val, 'dp', [(i, i // n * n + (i + k) % n) for i in range(sel...  30 us
    unnamed x121, local copies, waits for them, and re-layouts  17 us
    pallas_call x4, Pallas kernels, run_backward(): pl.pallas_call(functools.partial(backward_kernel, experts, len(backs)), g...  16.1 us
    ppermute x10, starting transfers between devices, xs(): lax.ppermute(val, 'expert', [(i, (i // c + k) % n * c + i % c) for i in r...  13.4 us
    ppermute x3, waiting for transfers between devices, xy(): lax.ppermute(val, ('dp', 'expert'), [(i, move(i)) for i in range(self.nd...  10.2 us
    pallas_call x2, Pallas kernels, run_forward(): pl.pallas_call(functools.partial(forward_kernel, experts), grid=(HALF,),...  9.74 us
  transfers between devices with their start and end apart: 46, of which 17 were waited for; matrix products, arithmetic and copies ran while one was open for 12% of the time, Pallas kernels for 44%

profile of v5, /device:TPU:0, one launch (start us, length us, event | category | flops | bytes accessed | tf_op | source)
XLA Modules:
  0.0 285.9 jit_solution(5535797096596388179)
XLA Ops:
  3.1 5.1 %collective-permute-start.2 = (bf16[16,2176]{1,0:T(8,128)(2,1)S(1)}, bf16[16,2176]{1,0:T(8,128)(2,1)S(1)}, u32[]{:S(2)}, u32[]{:S(2)}) collective-permute-start(bf16[16,2176]{1,0:T(8,128)(2,1)S(1)} %pad.13), channel_id=1, source_target_pairs={{0,24},{4,28},{8,0},{12,4},{16,8},{20,12},{24,16},{28,20},{1,25},{... | collective-permute-start | bytes 208904 | tf_op jit(solution)/shard_map/ppermute | solution.py:627
  12.0 3.0 %collective-permute-done.1 = bf16[16,2176]{1,0:T(8,128)(2,1)S(1)} collective-permute-done((bf16[16,2176]{1,0:T(8,128)(2,1)S(1)}, bf16[16,2176]{1,0:T(8,128)(2,1)S(1)}, u32[]{:S(2)}, u32[]{:S(2)}) %collective-permute-start.1) | collective-permute-done | bytes 69664 | tf_op jit(solution)/shard_map/ppermute | solution.py:627
  15.0 2.5 collective-permute-start.5
  20.5 5.1 %collective-permute-done.5 = bf16[64,2176]{1,0:T(8,128)(2,1)S(1)} collective-permute-done((bf16[64,2176]{1,0:T(8,128)(2,1)S(1)}, bf16[64,2176]{1,0:T(8,128)(2,1)S(1)}, u32[]{:S(2)}, u32[]{:S(2)}) %collective-permute-start.5) | collective-permute-done | bytes 278560 | tf_op jit(solution)/shard_map/ppermute | solution.py:648
  25.5 4.9 %collective-permute-done.4 = bf16[64,2176]{1,0:T(8,128)(2,1)S(1)} collective-permute-done((bf16[64,2176]{1,0:T(8,128)(2,1)S(1)}, bf16[64,2176]{1,0:T(8,128)(2,1)S(1)}, u32[]{:S(2)}, u32[]{:S(2)}) %collective-permute-start.4) | collective-permute-done | bytes 278560 | tf_op jit(solution)/shard_map/ppermute | solution.py:648
  35.6 4.9 %dense_forward.2 = (bf16[2,208,1536]{2,1,0:T(8,128)(2,1)S(1)}, bf16[2,208,512]{2,1,0:T(8,128)(2,1)S(1)}, f32[2,208,512]{2,1,0:T(8,128)S(1)}, bf16[2,208,512]{2,1,0:T(8,128)(2,1)S(1)}, f32[2,208,128]{2,1,0:T(8,128)S(1)}) custom-call(bf16[4,208,512]{2,1,0:T(8,128)(2,1)S(1)} %pad.12.tok.refs_0_, bf16[512,2176]{1,0:T(8,128)(2,1)S(1)} %get-tuple-element.161.dense.refs_2_, ...), custom_call_target="tpu_custom_call" | custom-call | flops 1750000000 | bytes 1048576 | tf_op jit(solution)/shard_map/dense_forward/pallas_call | solution.py:119
  44.0 4.9 %dense_forward.3 = (bf16[2,208,1536]{2,1,0:T(8,128)(2,1)S(1)}, bf16[2,208,512]{2,1,0:T(8,128)(2,1)S(1)}, f32[2,208,512]{2,1,0:T(8,128)S(1)}, bf16[2,208,512]{2,1,0:T(8,128)(2,1)S(1)}, f32[2,208,128]{2,1,0:T(8,128)S(1)}) custom-call(bf16[4,208,512]{2,1,0:T(8,128)(2,1)S(1)} %pad.12.tok.refs_0_, bf16[512,2176]{1,0:T(8,128)(2,1)S(1)} %get-tuple-element.161.dense.refs_2_, ...), custom_call_target="tpu_custom_call" | custom-call | flops 1750000000 | bytes 1048576 | tf_op jit(solution)/shard_map/dense_forward/pallas_call | solution.py:119
  49.8 3.4 %collective-permute-done.10.refs_4_ = bf16[4,208,512]{2,1,0:T(8,128)(2,1)S(1)} collective-permute-done((bf16[4,208,512]{2,1,0:T(8,128)(2,1)S(1)}, bf16[4,208,512]{2,1,0:T(8,128)(2,1)S(1)}, u32[]{:S(2)}, u32[]{:S(2)}) %collective-permute-start.10) | collective-permute-done | bytes 852000 | tf_op jit(solution)/shard_map/ppermute | solution.py:631
  60.0 22.8 %experts.2 = (bf16[2,864,512]{2,1,0:T(8,128)(2,1)}, bf16[2,864,512]{2,1,0:T(8,128)(2,1)}, bf16[4,384,512]{2,1,0:T(8,128)(2,1)}, bf16[4,384,512]{2,1,0:T(8,128)(2...) custom-call(s32[1]{0:T(128)} %bitcast.at_ref.ei_ref, ...), custom_call_target="tpu_custom_call" | custom-call | flops 8400000000 | bytes 1048576 | tf_op jit(solution)/shard_map/experts/pallas_call | solution.py:249
  90.4 22.9 %experts.3 = (bf16[2,864,512]{2,1,0:T(8,128)(2,1)}, bf16[2,864,512]{2,1,0:T(8,128)(2,1)}, bf16[4,384,512]{2,1,0:T(8,128)(2,1)}, bf16[4,384,512]{2,1,0:T(8,128)(2...) custom-call(s32[1]{0:T(128)} %bitcast.at_ref.ei_ref, ...), custom_call_target="tpu_custom_call" | custom-call | flops 8400000000 | bytes 1048576 | tf_op jit(solution)/shard_map/experts/pallas_call | solution.py:249
  113.3 2.6 collective-permute-done.22.refs_6_
  116.6 2.5 fusion.6
  128.2 10.8 %weight_grad.4 = (bf16[2,2,256,512]{3,2,1,0:T(8,128)(2,1)S(1)}, bf16[2,2,256,512]{3,2,1,0:T(8,128)(2,1)S(1)}) custom-call(s32[3]{0:T(128)S(1)} %pad_add_fusion.own_ref, bf16[4,384,512]{2,1,0:T(8,128)(2,1)S(1)} %copy-done, bf16[4,384,512]{2,1,0:T(8,128)(2,1)S(1)} %copy-done.2, bf16[4,384,512]{2,1,0:T(8,128)(2,1)S(1)} %get-tuple-element.185.refs_2_, ...), custom_call_target="tpu_custom_call" | custom-call | flops 350000000 | bytes 1048576 | tf_op jit(solution)/shard_map/weight_grad/pallas_call | solution.py:346
  144.7 10.6 %weight_grad.5 = (bf16[2,2,256,512]{3,2,1,0:T(8,128)(2,1)S(1)}, bf16[2,2,256,512]{3,2,1,0:T(8,128)(2,1)S(1)}) custom-call(s32[3]{0:T(128)S(1)} %pad_add_fusion.own_ref, bf16[4,384,512]{2,1,0:T(8,128)(2,1)S(1)} %copy-done, bf16[4,384,512]{2,1,0:T(8,128)(2,1)S(1)} %copy-done.2, bf16[4,384,512]{2,1,0:T(8,128)(2,1)S(1)} %get-tuple-element.185.refs_2_, ...), custom_call_target="tpu_custom_call" | custom-call | flops 350000000 | bytes 1048576 | tf_op jit(solution)/shard_map/weight_grad/pallas_call | solution.py:346
  155.4 4.0 %dense_backward.5 = (bf16[1,208,512]{2,1,0:T(8,128)(2,1)S(1)}, f32[1,208,512]{2,1,0:T(8,128)S(1)}, bf16[1,208,512]{2,1,0:T(8,128)(2,1)S(1)}, bf16[1,208,512]{2,1...) custom-call(bf16[4,208,512]{2,1,0:T(8,128)(2,1)S(1)} %pad.12.tok.refs_0_, ...), custom_call_target="tpu_custom_call" | custom-call | flops 350000000 | bytes 1048576 | tf_op jit(solution)/shard_map/dense_backward/pallas_call | solution.py:455
  160.9 4.0 %dense_backward.4 = (bf16[1,208,512]{2,1,0:T(8,128)(2,1)S(1)}, f32[1,208,512]{2,1,0:T(8,128)S(1)}, bf16[1,208,512]{2,1,0:T(8,128)(2,1)S(1)}, bf16[1,208,512]{2,1...) custom-call(bf16[4,208,512]{2,1,0:T(8,128)(2,1)S(1)} %pad.12.tok.refs_0_, ...), custom_call_target="tpu_custom_call" | custom-call | flops 350000000 | bytes 1048576 | tf_op jit(solution)/shard_map/dense_backward/pallas_call | solution.py:455
  169.6 10.6 %weight_grad.6 = (bf16[2,2,256,512]{3,2,1,0:T(8,128)(2,1)S(1)}, bf16[2,2,256,512]{3,2,1,0:T(8,128)(2,1)S(1)}) custom-call(s32[3]{0:T(128)S(1)} %pad_add_fusion.own_ref, bf16[4,384,512]{2,1,0:T(8,128)(2,1)S(1)} %copy-done, bf16[4,384,512]{2,1,0:T(8,128)(2,1)S(1)} %copy-done.2, bf16[4,384,512]{2,1,0:T(8,128)(2,1)S(1)} %get-tuple-element.185.refs_2_, ...), custom_call_target="tpu_custom_call" | custom-call | flops 350000000 | bytes 1048576 | tf_op jit(solution)/shard_map/weight_grad/pallas_call | solution.py:346
  180.2 4.0 %dense_backward.7 = (bf16[1,208,512]{2,1,0:T(8,128)(2,1)S(1)}, f32[1,208,512]{2,1,0:T(8,128)S(1)}, bf16[1,208,512]{2,1,0:T(8,128)(2,1)S(1)}, bf16[1,208,512]{2,1...) custom-call(bf16[4,208,512]{2,1,0:T(8,128)(2,1)S(1)} %pad.12.tok.refs_0_, ...), custom_call_target="tpu_custom_call" | custom-call | flops 350000000 | bytes 1048576 | tf_op jit(solution)/shard_map/dense_backward/pallas_call | solution.py:455
  185.7 4.0 %dense_backward.6 = (bf16[1,208,512]{2,1,0:T(8,128)(2,1)S(1)}, f32[1,208,512]{2,1,0:T(8,128)S(1)}, bf16[1,208,512]{2,1,0:T(8,128)(2,1)S(1)}, bf16[1,208,512]{2,1...) custom-call(bf16[4,208,512]{2,1,0:T(8,128)(2,1)S(1)} %pad.12.tok.refs_0_, ...), custom_call_target="tpu_custom_call" | custom-call | flops 350000000 | bytes 1048576 | tf_op jit(solution)/shard_map/dense_backward/pallas_call | solution.py:455
  189.8 2.9 collective-permute-done.34.refs_1_
  195.9 2.6 dense_grads.1
  198.5 10.7 %weight_grad.7 = (bf16[2,2,256,512]{3,2,1,0:T(8,128)(2,1)S(1)}, bf16[2,2,256,512]{3,2,1,0:T(8,128)(2,1)S(1)}) custom-call(s32[3]{0:T(128)S(1)} %pad_add_fusion.own_ref, bf16[4,384,512]{2,1,0:T(8,128)(2,1)S(1)} %copy-done, bf16[4,384,512]{2,1,0:T(8,128)(2,1)S(1)} %copy-done.2, bf16[4,384,512]{2,1,0:T(8,128)(2,1)S(1)} %get-tuple-element.185.refs_2_, ...), custom_call_target="tpu_custom_call" | custom-call | flops 350000000 | bytes 1048576 | tf_op jit(solution)/shard_map/weight_grad/pallas_call | solution.py:346
  210.2 7.5 %collective-permute-done.35 = bf16[2,2,256,512]{3,2,1,0:T(8,128)(2,1)S(1)} collective-permute-done((bf16[2,2,256,512]{3,2,1,0:T(8,128)(2,1)S(1)}, bf16[2,2,256,512]{3,2,1,0:T(8,128)(2,1)S(1)}, u32[]{:S(2)}, u32[]{:S(2)}) %collective-permute-start.35) | collective-permute-done | bytes 1048608 | tf_op jit(solution)/shard_map/ppermute | solution.py:623
  220.1 2.2 slice_bitcast_fusion.2
  226.3 21.6 %collective-permute-done.43 = bf16[2,2,256,512]{3,2,1,0:T(8,128)(2,1)S(1)} collective-permute-done((bf16[2,2,256,512]{3,2,1,0:T(8,128)(2,1)S(1)}, bf16[2,2,256,512]{3,2,1,0:T(8,128)(2,1)S(1)}, u32[]{:S(2)}, u32[]{:S(2)}) %collective-permute-start.43) | collective-permute-done | bytes 1048608 | tf_op jit(solution)/shard_map/ppermute | solution.py:623
  249.1 2.6 collective-permute-start.44
  257.1 2.3 pad_maximum_fusion
  259.5 2.9 reshape.93
  263.3 2.3 reshape.92
  266.8 2.7 collective-permute-start.42
  273.6 2.2 store_expert.6
  275.8 5.4 %collective-permute-done.41.refs_2_ = bf16[16,2176]{1,0:T(8,128)(2,1)S(1)} collective-permute-done((bf16[16,2176]{1,0:T(8,128)(2,1)S(1)}, bf16[16,2176]{1,0:T(8,128)(2,1)S(1)}, u32[]{:S(2)}, u32[]{:S(2)}) %collective-permute-start.41) | collective-permute-done | bytes 69664 | tf_op jit(solution)/shard_map/ppermute | solution.py:627
  (257 shorter events, 83.3 us)
Async XLA Ops:
  15.0 10.5 %collective-permute-start.5 = (bf16[64,2176]{1,0:T(8,128)(2,1)S(1)}, bf16[64,2176]{1,0:T(8,128)(2,1)S(1)}, u32[]{:S(2)}, u32[]{:S(2)}) collective-permute-start(bf16[64,2176]{1,0:T(8,128)(2,1)S(1)} %pad_maximum_fusion.8), channel_id=1, source_target_pairs={{0,6},{1,7},{2,4},{3,5},{4,2},{5,3},{6,0},{7,1},{8,14},{9,15},{10,... | collective-permute-start | bytes 835592 | tf_op jit(solution)/shard_map/ppermute | solution.py:648
  17.5 12.9 %collective-permute-start.4 = (bf16[64,2176]{1,0:T(8,128)(2,1)S(1)}, bf16[64,2176]{1,0:T(8,128)(2,1)S(1)}, u32[]{:S(2)}, u32[]{:S(2)}) collective-permute-start(bf16[64,2176]{1,0:T(8,128)(2,1)S(1)} %pad_maximum_fusion.8), channel_id=1, source_target_pairs={{0,4},{1,5},{2,6},{3,7},{4,0},{5,1},{6,2},{7,3},{8,12},{9,13},{10,... | collective-permute-start | bytes 835592 | tf_op jit(solution)/shard_map/ppermute | solution.py:648
  18.0 12.6 %collective-permute-start.3 = (bf16[64,2176]{1,0:T(8,128)(2,1)S(1)}, bf16[64,2176]{1,0:T(8,128)(2,1)}, u32[]{:S(2)}, u32[]{:S(2)}) collective-permute-start(bf16[64,2176]{1,0:T(8,128)(2,1)S(1)} %pad_maximum_fusion.8), channel_id=1, source_target_pairs={{0,2},{1,3},{2,0},{3,1},{4,6},{5,7},{6,4},{7,5},{8,10},{9,11},{10,... | collective-permute-start | bytes 835592 | tf_op jit(solution)/shard_map/ppermute | solution.py:648
  31.8 10.7 %collective-permute-start.7 = (bf16[4,208,512]{2,1,0:T(8,128)(2,1)S(1)}, bf16[4,208,512]{2,1,0:T(8,128)(2,1)S(1)}, u32[]{:S(2)}, u32[]{:S(2)}) collective-permute-start(bf16[4,208,512]{2,1,0:T(8,128)(2,1)S(1)} %maximum_maximum_fusion.refs_4_.refs_1_), channel_id=1, source_target_pairs={{0,1},{1,0},{2,3},{3,2},{4,5},{5,4},{6,7},{7,6},{8,9},{9,8},{10,11... | collective-permute-start | bytes 2555912 | tf_op jit(solution)/shard_map/ppermute | solution.py:615
  32.3 20.9 %collective-permute-start.10 = (bf16[4,208,512]{2,1,0:T(8,128)(2,1)S(1)}, bf16[4,208,512]{2,1,0:T(8,128)(2,1)S(1)}, u32[]{:S(2)}, u32[]{:S(2)}) collective-permute-start(bf16[4,208,512]{2,1,0:T(8,128)(2,1)S(1)} %maximum_maximum_fusion.refs_4_.refs_1_), channel_id=1, source_target_pairs={{0,8},{4,12},{8,0},{12,4},{16,24},{20,28},{24,16},{28,20},{1,9},{5... | collective-permute-start | bytes 2555912 | tf_op jit(solution)/shard_map/ppermute | solution.py:631
  32.3 17.5 %collective-permute-start.11 = (bf16[2,208,512]{2,1,0:T(8,128)(2,1)S(1)}, bf16[2,208,512]{2,1,0:T(8,128)(2,1)S(1)}, u32[]{:S(2)}, u32[]{:S(2)}) collective-permute-start(bf16[2,208,512]{2,1,0:T(8,128)(2,1)S(1)} %get-tuple-element.164), channel_id=1, source_target_pairs={{0,2},{1,3},{2,0},{3,1},{4,6},{5,7},{6,4},{7,5},{8,10},{9,11},{10,... | collective-permute-start | bytes 1277960 | tf_op jit(solution)/shard_map/ppermute | solution.py:619
  42.4 11.9 %collective-permute-start.9 = (bf16[2,208,512]{2,1,0:T(8,128)(2,1)S(1)}, bf16[2,208,512]{2,1,0:T(8,128)(2,1)S(1)}, u32[]{:S(2)}, u32[]{:S(2)}) collective-permute-start(bf16[2,208,512]{2,1,0:T(8,128)(2,1)S(1)} %get-tuple-element.160.refs_0_.refs_6_), channel_id=1, source_target_pairs={{0,2},{1,3},{2,0},{3,1},{4,6},{5,7},{6,4},{7,5},{8,10},{9,11},{10,... | collective-permute-start | bytes 1277960 | tf_op jit(solution)/shard_map/ppermute | solution.py:619
  44.0 10.4 %collective-permute-start.8 = (bf16[2,208,512]{2,1,0:T(8,128)(2,1)S(1)}, bf16[2,208,512]{2,1,0:T(8,128)(2,1)S(1)}, u32[]{:S(2)}, u32[]{:S(2)}) collective-permute-start(bf16[2,208,512]{2,1,0:T(8,128)(2,1)S(1)} %get-tuple-element.160.refs_0_.refs_6_), channel_id=1, source_target_pairs={{0,1},{1,0},{2,3},{3,2},{4,5},{5,4},{6,7},{7,6},{8,9},{9,8},{10,11... | collective-permute-start | bytes 1277960 | tf_op jit(solution)/shard_map/ppermute | solution.py:615
  54.9 27.9 %collective-permute-start.15 = (bf16[2,208,512]{2,1,0:T(8,128)(2,1)S(1)}, bf16[2,208,512]{2,1,0:T(8,128)(2,1)S(1)}, u32[]{:S(2)}, u32[]{:S(2)}) collective-permute-start(bf16[2,208,512]{2,1,0:T(8,128)(2,1)S(1)} %get-tuple-element.168.refs_0_.refs_6_), channel_id=1, source_target_pairs={{0,2},{1,3},{2,0},{3,1},{4,6},{5,7},{6,4},{7,5},{8,10},{9,11},{10,... | collective-permute-start | bytes 1277960 | tf_op jit(solution)/shard_map/ppermute | solution.py:619
  56.4 26.4 %collective-permute-start.14 = (bf16[2,208,512]{2,1,0:T(8,128)(2,1)S(1)}, bf16[2,208,512]{2,1,0:T(8,128)(2,1)S(1)}, u32[]{:S(2)}, u32[]{:S(2)}) collective-permute-start(bf16[2,208,512]{2,1,0:T(8,128)(2,1)S(1)} %get-tuple-element.168.refs_0_.refs_6_), channel_id=1, source_target_pairs={{0,1},{1,0},{2,3},{3,2},{4,5},{5,4},{6,7},{7,6},{8,9},{9,8},{10,11... | collective-permute-start | bytes 1277960 | tf_op jit(solution)/shard_map/ppermute | solution.py:615
  56.4 28.4 %collective-permute-start.16 = (bf16[4,208,512]{2,1,0:T(8,128)(2,1)S(1)}, bf16[4,208,512]{2,1,0:T(8,128)(2,1)S(1)}, u32[]{:S(2)}, u32[]{:S(2)}) collective-permute-start(bf16[4,208,512]{2,1,0:T(8,128)(2,1)S(1)} %pad_maximum_fusion.4), channel_id=1, source_target_pairs={{0,8},{4,12},{8,0},{12,4},{16,24},{20,28},{24,16},{28,20},{1,9},{5... | collective-permute-start | bytes 2555912 | tf_op jit(solution)/shard_map/ppermute | solution.py:631
  57.9 24.8 %collective-permute-start.17 = (bf16[2,208,512]{2,1,0:T(8,128)(2,1)S(1)}, bf16[2,208,512]{2,1,0:T(8,128)(2,1)S(1)}, u32[]{:S(2)}, u32[]{:S(2)}) collective-permute-start(bf16[2,208,512]{2,1,0:T(8,128)(2,1)S(1)} %get-tuple-element.170), channel_id=1, source_target_pairs={{0,2},{1,3},{2,0},{3,1},{4,6},{5,7},{6,4},{7,5},{8,10},{9,11},{10,... | collective-permute-start | bytes 1277960 | tf_op jit(solution)/shard_map/ppermute | solution.py:619
  58.5 26.3 %collective-permute-start.18 = (bf16[2,208,512]{2,1,0:T(8,128)(2,1)}, bf16[2,208,512]{2,1,0:T(8,128)(2,1)S(1)}, u32[]{:S(2)}, u32[]{:S(2)}) collective-permute-start(bf16[2,208,512]{2,1,0:T(8,128)(2,1)} %get-tuple-element.334), channel_id=1, source_target_pairs={{0,2},{1,3},{2,0},{3,1},{4,6},{5,7},{6,4},{7,5},{8,10},{9,11},{10,... | collective-permute-start | bytes 1277960 | tf_op jit(solution)/shard_map/ppermute | solution.py:619
  84.9 31.1 %collective-permute-start.25 = (bf16[2,864,512]{2,1,0:T(8,128)(2,1)}, bf16[2,864,512]{2,1,0:T(8,128)(2,1)}, u32[]{:S(2)}, u32[]{:S(2)}) collective-permute-start(bf16[2,864,512]{2,1,0:T(8,128)(2,1)} %get-tuple-element.180), channel_id=1, source_target_pairs={{0,1},{1,0},{2,3},{3,2},{4,5},{5,4},{6,7},{7,6},{8,9},{9,8},{10,11... | collective-permute-start | bytes 5308424 | tf_op jit(solution)/shard_map/ppermute | solution.py:615
  85.4 27.9 %collective-permute-start.23 = (bf16[4,208,512]{2,1,0:T(8,128)(2,1)S(1)}, bf16[4,208,512]{2,1,0:T(8,128)(2,1)S(1)}, u32[]{:S(2)}, u32[]{:S(2)}) collective-permute-start(bf16[4,208,512]{2,1,0:T(8,128)(2,1)S(1)} %collective-permute-done.10.refs_4_), channel_id=1, source_target_pairs={{0,1},{1,0},{2,3},{3,2},{4,5},{5,4},{6,7},{7,6},{8,9},{9,8},{10,11... | collective-permute-start | bytes 2555912 | tf_op jit(solution)/shard_map/ppermute | solution.py:615
  85.9 30.1 %collective-permute-start.21 = (bf16[4,208,512]{2,1,0:T(8,128)(2,1)S(1)}, bf16[4,208,512]{2,1,0:T(8,128)(2,1)S(1)}, u32[]{:S(2)}, u32[]{:S(2)}) collective-permute-start(bf16[4,208,512]{2,1,0:T(8,128)(2,1)S(1)} %collective-permute-done.16.refs_0_), channel_id=1, source_target_pairs={{0,2},{1,3},{2,0},{3,1},{4,6},{5,7},{6,4},{7,5},{8,10},{9,11},{10,... | collective-permute-start | bytes 2555912 | tf_op jit(solution)/shard_map/ppermute | solution.py:619
  88.8 27.1 %collective-permute-start.22 = (bf16[2,208,512]{2,1,0:T(8,128)(2,1)S(1)}, bf16[2,208,512]{2,1,0:T(8,128)(2,1)S(1)}, u32[]{:S(2)}, u32[]{:S(2)}) collective-permute-start(bf16[2,208,512]{2,1,0:T(8,128)(2,1)S(1)} %get-tuple-element.177), channel_id=1, source_target_pairs={{0,2},{1,3},{2,0},{3,1},{4,6},{5,7},{6,4},{7,5},{8,10},{9,11},{10,... | collective-permute-start | bytes 1277960 | tf_op jit(solution)/shard_map/ppermute | solution.py:619
  90.3 25.6 %collective-permute-start.24 = (bf16[2,208,512]{2,1,0:T(8,128)(2,1)S(1)}, bf16[2,208,512]{2,1,0:T(8,128)(2,1)S(1)}, u32[]{:S(2)}, u32[]{:S(2)}) collective-permute-start(bf16[2,208,512]{2,1,0:T(8,128)(2,1)S(1)} %collective-permute-done.18.refs_6_), channel_id=1, source_target_pairs={{0,1},{1,0},{2,3},{3,2},{4,5},{5,4},{6,7},{7,6},{8,9},{9,8},{10,11... | collective-permute-start | bytes 1277960 | tf_op jit(solution)/shard_map/ppermute | solution.py:615
  116.0 25.2 %collective-permute-start.26 = (bf16[2,864,512]{2,1,0:T(8,128)(2,1)}, bf16[2,864,512]{2,1,0:T(8,128)(2,1)S(1)}, u32[]{:S(2)}, u32[]{:S(2)}) collective-permute-start(bf16[2,864,512]{2,1,0:T(8,128)(2,1)} %get-tuple-element.181), channel_id=1, source_target_pairs={{0,1},{1,0},{2,3},{3,2},{4,5},{5,4},{6,7},{7,6},{8,9},{9,8},{10,11... | collective-permute-start | bytes 5308424 | tf_op jit(solution)/shard_map/ppermute | solution.py:615
  119.2 22.0 %collective-permute-start.27 = (bf16[864,512]{1,0:T(8,128)(2,1)S(1)}, bf16[864,512]{1,0:T(8,128)(2,1)S(1)}, u32[]{:S(2)}, u32[]{:S(2)}) collective-permute-start(bf16[864,512]{1,0:T(8,128)(2,1)S(1)} %get-tuple-element.320), channel_id=1, source_target_pairs={{0,2},{1,3},{2,0},{3,1},{4,6},{5,7},{6,4},{7,5},{8,10},{9,11},{10,... | collective-permute-start | bytes 2654216 | tf_op jit(solution)/shard_map/ppermute | solution.py:619
  141.1 24.6 %collective-permute-start.31 = (bf16[2,2,256,512]{3,2,1,0:T(8,128)(2,1)S(1)}, bf16[2,2,256,512]{3,2,1,0:T(8,128)(2,1)S(1)}, u32[]{:S(2)}, u32[]{:S(2)}) collective-permute-start(bf16[2,2,256,512]{3,2,1,0:T(8,128)(2,1)S(1)} %get-tuple-element.204), channel_id=1, source_target_pairs={{0,4},{4,0},{8,12},{12,8},{16,20},{20,16},{24,28},{28,24},{1,5},{5... | collective-permute-start | bytes 3145736 | tf_op jit(solution)/shard_map/ppermute | solution.py:623
  143.9 36.3 %collective-permute-start.32 = (bf16[864,512]{1,0:T(8,128)(2,1)}, bf16[864,512]{1,0:T(8,128)(2,1)S(1)}, u32[]{:S(2)}, u32[]{:S(2)}) collective-permute-start(bf16[864,512]{1,0:T(8,128)(2,1)} %get-tuple-element.221), channel_id=1, source_target_pairs={{0,2},{1,3},{2,0},{3,1},{4,6},{5,7},{6,4},{7,5},{8,10},{9,11},{10,... | collective-permute-start | bytes 2654216 | tf_op jit(solution)/shard_map/ppermute | solution.py:619
  165.7 26.9 %collective-permute-start.33 = (bf16[2,2,256,512]{3,2,1,0:T(8,128)(2,1)S(1)}, bf16[2,2,256,512]{3,2,1,0:T(8,128)(2,1)}, u32[]{:S(2)}, u32[]{:S(2)}) collective-permute-start(bf16[2,2,256,512]{3,2,1,0:T(8,128)(2,1)S(1)} %get-tuple-element.239), channel_id=1, source_target_pairs={{0,4},{4,0},{8,12},{12,8},{16,20},{20,16},{24,28},{28,24},{1,5},{5... | collective-permute-start | bytes 3145736 | tf_op jit(solution)/shard_map/ppermute | solution.py:623
  168.2 24.4 %collective-permute-start.34 = (bf16[2,256,512]{2,1,0:T(8,128)(2,1)S(1)}, bf16[2,256,512]{2,1,0:T(8,128)(2,1)S(1)}, u32[]{:S(2)}, u32[]{:S(2)}) collective-permute-start(bf16[2,256,512]{2,1,0:T(8,128)(2,1)S(1)} %get-tuple-element.327), channel_id=1, source_target_pairs={{0,16},{4,20},{8,24},{12,28},{16,0},{20,4},{24,8},{28,12},{1,17},{... | collective-permute-start | bytes 1572872 | tf_op jit(solution)/shard_map/ppermute | solution.py:635
  192.6 25.1 %collective-permute-start.35 = (bf16[2,2,256,512]{3,2,1,0:T(8,128)(2,1)S(1)}, bf16[2,2,256,512]{3,2,1,0:T(8,128)(2,1)S(1)}, u32[]{:S(2)}, u32[]{:S(2)}) collective-permute-start(bf16[2,2,256,512]{3,2,1,0:T(8,128)(2,1)S(1)} %get-tuple-element.243), channel_id=1, source_target_pairs={{0,4},{4,0},{8,12},{12,8},{16,20},{20,16},{24,28},{28,24},{1,5},{5... | collective-permute-start | bytes 3145736 | tf_op jit(solution)/shard_map/ppermute | solution.py:623
  195.0 24.0 %collective-permute-start.36 = (bf16[2,256,512]{2,1,0:T(8,128)(2,1)S(1)}, bf16[2,256,512]{2,1,0:T(8,128)(2,1)S(1)}, u32[]{:S(2)}, u32[]{:S(2)}) collective-permute-start(bf16[2,256,512]{2,1,0:T(8,128)(2,1)S(1)} %get-tuple-element.329), channel_id=1, source_target_pairs={{0,16},{4,20},{8,24},{12,28},{16,0},{20,4},{24,8},{28,12},{1,17},{... | collective-permute-start | bytes 1572872 | tf_op jit(solution)/shard_map/ppermute | solution.py:635
  222.3 50.0 %collective-permute-start.45 = (bf16[2,256,512]{2,1,0:T(8,128)(2,1)}, bf16[2,256,512]{2,1,0:T(8,128)(2,1)}, u32[]{:S(2)}, u32[]{:S(2)}) collective-permute-start(bf16[2,256,512]{2,1,0:T(8,128)(2,1)} %get-tuple-element.330), channel_id=1, source_target_pairs={{0,16},{4,20},{8,24},{12,28},{16,0},{20,4},{24,8},{28,12},{1,17},{... | collective-permute-start | bytes 1572872 | tf_op jit(solution)/shard_map/ppermute | solution.py:635
  222.3 25.6 %collective-permute-start.43 = (bf16[2,2,256,512]{3,2,1,0:T(8,128)(2,1)S(1)}, bf16[2,2,256,512]{3,2,1,0:T(8,128)(2,1)S(1)}, u32[]{:S(2)}, u32[]{:S(2)}) collective-permute-start(bf16[2,2,256,512]{3,2,1,0:T(8,128)(2,1)S(1)} %copy-done.50), channel_id=1, source_target_pairs={{0,4},{4,0},{8,12},{12,8},{16,20},{20,16},{24,28},{28,24},{1,5},{5... | collective-permute-start | bytes 3145736 | tf_op jit(solution)/shard_map/ppermute | solution.py:623
  224.8 26.9 %collective-permute-start.38 = (bf16[4,2,16,2176]{3,2,0,1:T(8,128)(2,1)S(1)}, bf16[4,2,16,2176]{3,2,0,1:T(8,128)(2,1)S(1)}, u32[]{:S(2)}, u32[]{:S(2)}) collective-permute-start(bf16[4,2,16,2176]{3,2,0,1:T(8,128)(2,1)S(1)} %bitcast.100), channel_id=1, source_target_pairs={{0,2},{1,3},{2,0},{3,1},{4,6},{5,7},{6,4},{7,5},{8,10},{9,11},{10,... | collective-permute-start | bytes 1671176 | tf_op jit(solution)/shard_map/ppermute | solution.py:619
  249.1 34.6 %collective-permute-start.44 = (bf16[2,256,512]{2,1,0:T(8,128)(2,1)}, bf16[2,256,512]{2,1,0:T(8,128)(2,1)S(1)}, u32[]{:S(2)}, u32[]{:S(2)}) collective-permute-start(bf16[2,256,512]{2,1,0:T(8,128)(2,1)} %get-tuple-element.332), channel_id=1, source_target_pairs={{0,16},{4,20},{8,24},{12,28},{16,0},{20,4},{24,8},{28,12},{1,17},{... | collective-permute-start | bytes 1572872 | tf_op jit(solution)/shard_map/ppermute | solution.py:635
  269.5 11.7 %collective-permute-start.41 = (bf16[16,2176]{1,0:T(8,128)(2,1)S(1)}, bf16[16,2176]{1,0:T(8,128)(2,1)S(1)}, u32[]{:S(2)}, u32[]{:S(2)}) collective-permute-start(bf16[16,2176]{1,0:T(8,128)(2,1)S(1)} %get-tuple-element.339), channel_id=1, source_target_pairs={{0,16},{4,20},{8,24},{12,28},{16,0},{20,4},{24,8},{28,12},{1,17},{... | collective-permute-start | bytes 208904 | tf_op jit(solution)/shard_map/ppermute | solution.py:627
  269.5 11.7 %collective-permute-start.40 = (bf16[16,2176]{1,0:T(8,128)(2,1)S(1)}, bf16[16,2176]{1,0:T(8,128)(2,1)S(1)}, u32[]{:S(2)}, u32[]{:S(2)}) collective-permute-start(bf16[16,2176]{1,0:T(8,128)(2,1)S(1)} %get-tuple-element.340), channel_id=1, source_target_pairs={{0,8},{4,12},{8,16},{12,20},{16,24},{20,28},{24,0},{28,4},{1,9},{5... | collective-permute-start | bytes 208904 | tf_op jit(solution)/shard_map/ppermute | solution.py:627
  (72 other events, 654.9 us)
